TPU v7x, 128 devices: a whole 4x4x4 slice. The times are simulated.
128 devices in a mesh: gx: 8 (over z, core), gy: 16 (over y, x).
Axes of the slice: x: 4, y: 4, z: 4, core: 2. Of those that a mesh axis runs over, the one named last changes fastest.
Arguments:
- populations: float32 [19, 512, 16, 16, 128], P(None, ('gx', 'gy')), may hold values from 0.01 to 0.1
- charge: float32 [512, 16, 16, 128], P(('gx', 'gy')), may hold values from -6 to 6
- fluid_mask: int32 [512, 18, 18, 128], P(('gx', 'gy')), may hold values from 0 to 1, as said below
- tile_ids: int32 [512], P(('gx', 'gy')), may hold values from 0 to 63, as said below
- phase_label: int32 [256, 512, 128], P('gx', 'gy'), may hold values from 0 to 3
- permittivity: float32 [4], replicated, may hold values from 0.5 to 5
Outputs:
- populations_next: float32 [19, 512, 16, 16, 128], P(None, ('gx', 'gy'))
- charge_next: float32 [512, 16, 16, 128], P(('gx', 'gy'))
- potential: float32 [256, 512, 128], P('gx', 'gy')
Inputs may be any that keep to these rules, and one draw needn't show every extreme that they name: Within the slots of the devices of one gx index, tile_ids is a permutation of 0 to 63. Position p belongs to the regular block of gy index (p % 32) // 2; every device holds at most 1 positions of any one such block, and some device holds exactly 1. fluid_mask[s, i, j, z] is the fluid flag of grid cell (x0 + i - 1, y0 + j - 1, z), periodic, where (x0, y0) is the first cell of slot s's tile; the rim repeats flags of the neighbouring tiles.
All inputs are finite; a program needn't handle non-finite values.
Results may differ from a plain program's by a relative error of at most 0.0003.
Values sent between devices are 32-bit elements; how exact they have to be, the bound alone decides.
A program may use at most 192 MiB of HBM per device.

v0:
```python
import jax
import jax.numpy as jnp
from jax import lax
from jax.sharding import PartitionSpec as P

EDGE = 16
DEPTH = 128
TILE_ROWS = 2
TILE_COLS = 2
PHASES = 4
SWEEPS = 4


LATTICE = (
    (0, 0, 0),
    (1, 0, 0),
    (-1, 0, 0),
    (0, 1, 0),
    (0, -1, 0),
    (0, 0, 1),
    (0, 0, -1),
    (1, 1, 0),
    (-1, -1, 0),
    (1, -1, 0),
    (-1, 1, 0),
    (1, 0, 1),
    (-1, 0, -1),
    (1, 0, -1),
    (-1, 0, 1),
    (0, 1, 1),
    (0, -1, -1),
    (0, 1, -1),
    (0, -1, 1),
)
relax_time = 0.8
screening = 0.001
spectrum_low = 0.1
spectrum_high = 2.0


def extended(value, sides, width):
    for axis, dim in sides:
        size, length = (lax.axis_size(axis), value.shape[dim])
        up = [(i, (i + 1) % size) for i in range(size)]
        down = [(j, i) for i, j in up]
        last = lax.slice_in_dim(value, length - width, length, axis=dim)
        first = lax.slice_in_dim(value, 0, width, axis=dim)
        before = lax.ppermute(last, axis, up)
        after = lax.ppermute(first, axis, down)
        value = jnp.concatenate([before, value, after], axis=dim)
    return value


def lattice_weight(direction):
    length = sum((abs(entry) for entry in LATTICE[direction]))
    if length == 0:
        return 1.0 / 3.0
    if length == 1:
        return 1.0 / 18.0
    return 1.0 / 36.0


def opposite(direction):
    return LATTICE.index(tuple((-entry for entry in LATTICE[direction])))


def crossing(axis_index, face_sign):
    return [direction for direction in range(19) if LATTICE[direction][axis_index] == face_sign]


def population_sum(population):
    density = population[0]
    for direction in range(1, 19):
        density = density + population[direction]
    return density


def velocity_sums(population):
    sums_list = []
    for axis_index in range(3):
        total = None
        for direction in range(19):
            component = LATTICE[direction][axis_index]
            if component != 0:
                contrib = population[direction] if component > 0 else -population[direction]
                total = contrib if total is None else total + contrib
        sums_list.append(total)
    return sums_list


def collide(population, density, velocity, body_force):
    speed_sq = velocity[0] * velocity[0] + velocity[1] * velocity[1] + velocity[2] * velocity[2]
    source_scale = 1.0 - 0.5 / relax_time
    result = []
    for direction in range(19):
        lattice_step = LATTICE[direction]
        weight = lattice_weight(direction)
        projected = (
            lattice_step[0] * velocity[0]
            + lattice_step[1] * velocity[1]
            + lattice_step[2] * velocity[2]
        )
        force_dot = (
            lattice_step[0] * body_force[0]
            + lattice_step[1] * body_force[1]
            + lattice_step[2] * body_force[2]
        )
        drift_dot = (
            (lattice_step[0] - velocity[0]) * body_force[0]
            + (lattice_step[1] - velocity[1]) * body_force[1]
            + (lattice_step[2] - velocity[2]) * body_force[2]
        )
        equilibrium = (
            weight
            * density
            * (1.0 + 3.0 * projected + 4.5 * projected * projected - 1.5 * speed_sq)
        )
        source = source_scale * weight * (3.0 * drift_dot + 9.0 * projected * force_dot)
        result.append(
            population[direction] - (population[direction] - equilibrium) / relax_time + source
        )
    return result


def harmonic(left_value, right_value):
    return 2.0 * left_value * right_value / (left_value + right_value)


def tiles_from_block(block_data):
    leading = block_data.shape[0]
    pieces = block_data.reshape(leading, TILE_ROWS, EDGE, TILE_COLS, EDGE, DEPTH)
    pieces = jnp.transpose(pieces, (1, 3, 0, 2, 4, 5))
    return pieces.reshape(TILE_ROWS * TILE_COLS, leading, EDGE, EDGE, DEPTH)


def block_from_tiles(tile_data):
    pieces = tile_data.reshape(TILE_ROWS, TILE_COLS, EDGE, EDGE, DEPTH)
    pieces = jnp.transpose(pieces, (0, 2, 1, 3, 4))
    return pieces.reshape(TILE_ROWS * EDGE, TILE_COLS * EDGE, DEPTH)


def spread_rows(row_data, selector, present):
    picked = row_data[selector]
    full_shape = present.shape + (1,) * (picked.ndim - present.ndim)
    return jnp.where(present.reshape(full_shape), picked, jnp.zeros((), picked.dtype))


def with_margin(field_value):
    return extended(field_value, (("gx", 0), ("gy", 1)), 1)


def face_package(relaxed, charge, velocity):
    faces = []
    for axis_index, face_sign, layer_index in (
        (0, -1, 0),
        (0, 1, EDGE - 1),
        (1, -1, 0),
        (1, 1, EDGE - 1),
    ):
        channels = [relaxed[direction] for direction in crossing(axis_index, face_sign)]
        channels = channels + [charge, velocity[axis_index]]
        if axis_index == 0:
            face_parts = [channel[:, layer_index] for channel in channels]
        else:
            face_parts = [channel[:, :, layer_index] for channel in channels]
        faces.append(jnp.stack(face_parts, axis=1))
    return jnp.stack(faces, axis=1)


def build_cycles(xlo_table, xhi_table, ylo_table, yhi_table, index_of):
    below = jnp.concatenate(
        [
            xhi_table[index_of(-1, -1)][:, :, EDGE - 1 :],
            xhi_table[index_of(-1, 0)],
            xhi_table[index_of(-1, 1)][:, :, :1],
        ],
        axis=2,
    )
    above = jnp.concatenate(
        [
            xlo_table[index_of(1, -1)][:, :, EDGE - 1 :],
            xlo_table[index_of(1, 0)],
            xlo_table[index_of(1, 1)][:, :, :1],
        ],
        axis=2,
    )
    left_side = yhi_table[index_of(0, -1)]
    right_side = ylo_table[index_of(0, 1)]
    return (jnp.stack([below, above], axis=1), jnp.stack([left_side, right_side], axis=1))


def stream_tiles(relaxed, populations, fluid_mask, cycle_x, cycle_y):
    own_fluid = fluid_mask[:, 1 : EDGE + 1, 1 : EDGE + 1] == 1
    x_plus = crossing(0, 1)
    x_minus = crossing(0, -1)
    y_plus = crossing(1, 1)
    y_minus = crossing(1, -1)
    outputs = []
    for direction in range(19):
        step_x, step_y, step_z = LATTICE[direction]
        middle = relaxed[direction]
        if step_y == 1:
            middle = jnp.concatenate(
                [cycle_y[:, 0, y_plus.index(direction)][:, :, None], middle], axis=2
            )
            y_window = slice(0, EDGE + 1)
        elif step_y == -1:
            middle = jnp.concatenate(
                [middle, cycle_y[:, 1, y_minus.index(direction)][:, :, None]], axis=2
            )
            y_window = slice(1, EDGE + 2)
        else:
            y_window = slice(1, EDGE + 1)
        if step_x == 1:
            middle = jnp.concatenate(
                [cycle_x[:, 0, x_plus.index(direction), y_window][:, None], middle], axis=1
            )
        elif step_x == -1:
            middle = jnp.concatenate(
                [middle, cycle_x[:, 1, x_minus.index(direction), y_window][:, None]], axis=1
            )
        start_x = 1 if step_x == -1 else 0
        start_y = 1 if step_y == -1 else 0
        pulled = middle[:, start_x : start_x + EDGE, start_y : start_y + EDGE]
        source_fluid = fluid_mask[:, 1 - step_x : 1 - step_x + EDGE, 1 - step_y : 1 - step_y + EDGE]
        if step_z != 0:
            pulled = jnp.roll(pulled, step_z, axis=3)
            source_fluid = jnp.roll(source_fluid, step_z, axis=3)
        read = jnp.where(source_fluid == 1, pulled, relaxed[opposite(direction)])
        outputs.append(jnp.where(own_fluid, read, populations[direction]))
    return jnp.stack(outputs)


def face_difference(values, speeds, flags, axis_index):
    count = values.shape[axis_index]
    lower_values = lax.slice_in_dim(values, 0, count - 1, axis=axis_index)
    upper_values = lax.slice_in_dim(values, 1, count, axis=axis_index)
    lower_speeds = lax.slice_in_dim(speeds, 0, count - 1, axis=axis_index)
    upper_speeds = lax.slice_in_dim(speeds, 1, count, axis=axis_index)
    lower_flags = lax.slice_in_dim(flags, 0, count - 1, axis=axis_index)
    upper_flags = lax.slice_in_dim(flags, 1, count, axis=axis_index)
    face_vel = 0.5 * (lower_speeds + upper_speeds)
    upwind = jnp.where(face_vel > 0, lower_values, upper_values)
    face_flux = face_vel * upwind * lower_flags * upper_flags
    return lax.slice_in_dim(face_flux, 1, count - 1, axis=axis_index) - lax.slice_in_dim(
        face_flux, 0, count - 2, axis=axis_index
    )


def advect_tiles(charge, velocity, fluid_mask, cycle_x, cycle_y):
    flags_all = fluid_mask.astype(jnp.float32)
    values_x = jnp.concatenate(
        [cycle_x[:, 0, 5, 1 : EDGE + 1][:, None], charge, cycle_x[:, 1, 5, 1 : EDGE + 1][:, None]],
        axis=1,
    )
    speeds_x = jnp.concatenate(
        [
            cycle_x[:, 0, 6, 1 : EDGE + 1][:, None],
            velocity[0],
            cycle_x[:, 1, 6, 1 : EDGE + 1][:, None],
        ],
        axis=1,
    )
    term_x = face_difference(values_x, speeds_x, flags_all[:, :, 1 : EDGE + 1], 1)
    values_y = jnp.concatenate(
        [cycle_y[:, 0, 5][:, :, None], charge, cycle_y[:, 1, 5][:, :, None]], axis=2
    )
    speeds_y = jnp.concatenate(
        [cycle_y[:, 0, 6][:, :, None], velocity[1], cycle_y[:, 1, 6][:, :, None]], axis=2
    )
    term_y = face_difference(values_y, speeds_y, flags_all[:, 1 : EDGE + 1], 2)
    inner_flags = flags_all[:, 1 : EDGE + 1, 1 : EDGE + 1]
    face_vel = 0.5 * (velocity[2] + jnp.roll(velocity[2], -1, 3))
    upwind = jnp.where(face_vel > 0, charge, jnp.roll(charge, -1, 3))
    face_flux = face_vel * upwind * inner_flags * jnp.roll(inner_flags, -1, 3)
    term_z = face_flux - jnp.roll(face_flux, 1, 3)
    return term_x + term_y + term_z


def per_device(populations, charge, fluid_mask, tile_ids, phase_label, permittivity):
    groups = lax.axis_size("gy")
    tiles_dev = charge.shape[0]
    capacity = (tiles_dev + groups - 1) // groups
    band_cols = TILE_COLS * groups
    slot_index = jnp.arange(tiles_dev, dtype=jnp.int32)
    owner_peer = tile_ids % band_cols // TILE_COLS
    earlier = (owner_peer[:, None] == owner_peer[None, :]) & (
        slot_index[None, :] < slot_index[:, None]
    )
    rank_in_peer = jnp.sum(earlier.astype(jnp.int32), axis=1)
    slot_match = (
        owner_peer[None, None, :] == jnp.arange(groups, dtype=jnp.int32)[:, None, None]
    ) & (rank_in_peer[None, None, :] == jnp.arange(capacity, dtype=jnp.int32)[None, :, None])
    send_filled = jnp.any(slot_match, axis=2)
    send_slot = jnp.sum(jnp.where(slot_match, slot_index[None, None, :], 0), axis=2)
    band_ids = lax.all_gather(tile_ids, "gy", axis=0, tiled=True)
    band_table = band_ids.reshape(groups, tiles_dev)
    owner_all = band_table % band_cols // TILE_COLS
    local_all = band_table // band_cols * TILE_COLS + band_table % TILE_COLS
    earlier_all = (owner_all[:, :, None] == owner_all[:, None, :]) & (
        slot_index[None, None, :] < slot_index[None, :, None]
    )
    rank_all = jnp.sum(earlier_all.astype(jnp.int32), axis=2)
    is_mine = owner_all == lax.axis_index("gy")
    found_slot = is_mine[None] & (local_all[None] == slot_index[:, None, None])
    flat_slot = jnp.arange(groups, dtype=jnp.int32)[:, None] * capacity + rank_all
    source_index = jnp.sum(jnp.where(found_slot, flat_slot[None], 0), axis=(1, 2))
    back_match = is_mine[:, None, :] & (
        rank_all[:, None, :] == jnp.arange(capacity, dtype=jnp.int32)[None, :, None]
    )
    back_filled = jnp.any(back_match, axis=2)
    back_tile = jnp.sum(jnp.where(back_match, local_all[:, None, :], 0), axis=2)
    own_fluid = fluid_mask[:, 1 : EDGE + 1, 1 : EDGE + 1] == 1
    masked_charge = charge * own_fluid.astype(jnp.float32)
    arrived_charge = lax.all_to_all(
        spread_rows(masked_charge, send_slot, send_filled),
        "gy",
        split_axis=0,
        concat_axis=0,
        tiled=True,
    )
    source = block_from_tiles(
        arrived_charge.reshape((groups * capacity,) + arrived_charge.shape[2:])[source_index]
    )
    permit = jnp.zeros(phase_label.shape, jnp.float32)
    for phase_index in range(PHASES):
        permit = jnp.where(phase_label == phase_index, permittivity[phase_index], permit)
    permit_rim = extended(permit, (("gx", 0), ("gy", 1)), 1)
    center = permit_rim[1:-1, 1:-1]
    weights_plus = [
        harmonic(center, permit_rim[2:, 1:-1]),
        harmonic(center, permit_rim[1:-1, 2:]),
        harmonic(center, jnp.roll(center, -1, 2)),
    ]
    weights_minus = [
        harmonic(permit_rim[:-2, 1:-1], center),
        harmonic(permit_rim[1:-1, :-2], center),
        harmonic(jnp.roll(center, 1, 2), center),
    ]
    diagonal = (
        weights_plus[0]
        + weights_minus[0]
        + weights_plus[1]
        + weights_minus[1]
        + weights_plus[2]
        + weights_minus[2]
        + screening
    )
    center_value = 0.5 * (spectrum_high + spectrum_low)
    half_width = 0.5 * (spectrum_high - spectrum_low)
    ratio_value = center_value / half_width
    rho_old = 1.0 / ratio_value
    residual = source / diagonal
    update = residual / center_value
    potential = update
    for sweep_index in range(SWEEPS - 1):
        with_rim = with_margin(update)
        result = diagonal * update
        result = (
            result - weights_plus[0] * with_rim[2:, 1:-1] - weights_minus[0] * with_rim[:-2, 1:-1]
        )
        result = (
            result - weights_plus[1] * with_rim[1:-1, 2:] - weights_minus[1] * with_rim[1:-1, :-2]
        )
        result = (
            result
            - weights_plus[2] * jnp.roll(update, -1, 2)
            - weights_minus[2] * jnp.roll(update, 1, 2)
        )
        residual = residual - result / diagonal
        rho_new = 1.0 / (2.0 * ratio_value - rho_old)
        update = rho_new * rho_old * update + 2.0 * rho_new / half_width * residual
        potential = potential + update
        rho_old = rho_new
    potential_rim = with_margin(potential)
    field_block = jnp.stack(
        [
            0.5 * (potential_rim[:-2, 1:-1] - potential_rim[2:, 1:-1]),
            0.5 * (potential_rim[1:-1, :-2] - potential_rim[1:-1, 2:]),
            0.5 * (jnp.roll(potential, 1, 2) - jnp.roll(potential, -1, 2)),
        ]
    )
    field_local = tiles_from_block(field_block)
    returned = lax.all_to_all(
        spread_rows(field_local, back_tile, back_filled),
        "gy",
        split_axis=0,
        concat_axis=0,
        tiled=True,
    )
    field_mine = returned[owner_peer, rank_in_peer]
    field_tiles = [field_mine[:, axis_index] for axis_index in range(3)]
    body_force = [charge * field_tiles[axis_index] for axis_index in range(3)]
    density = population_sum(populations)
    momentum = velocity_sums(populations)
    velocity = [
        (momentum[axis_index] + 0.5 * body_force[axis_index]) / density for axis_index in range(3)
    ]
    relaxed = collide(populations, density, velocity, body_force)
    package = face_package(relaxed, charge, velocity)
    gathered = lax.all_gather(package, "gy", axis=0, tiled=True)
    band_count = groups * tiles_dev
    positions = jnp.arange(band_count, dtype=jnp.int32)
    row_of = jnp.sum(
        jnp.where(band_ids[None, :] == positions[:, None], positions[None, :], 0), axis=1
    )
    low_edge = gathered[row_of[:band_cols], 0]
    high_edge = gathered[row_of[(TILE_ROWS - 1) * band_cols :], 1]
    band_rims = extended(jnp.stack([low_edge, high_edge]), (("gx", 0),), 1)
    xhi_table = jnp.concatenate([band_rims[0], gathered[:, 1]])
    xlo_table = jnp.concatenate([gathered[:, 0], band_rims[3]])
    my_row = tile_ids // band_cols
    my_col = tile_ids % band_cols

    def band_index(row_step, col_step):
        row_value = my_row + row_step
        col_value = (my_col + col_step) % band_cols
        inside = row_of[jnp.clip(row_value, 0, TILE_ROWS - 1) * band_cols + col_value]
        if row_step < 0:
            return jnp.where(row_value < 0, col_value, band_cols + inside)
        if row_step > 0:
            return jnp.where(row_value >= TILE_ROWS, band_count + col_value, inside)
        return inside

    cycle_x, cycle_y = build_cycles(
        xlo_table, xhi_table, gathered[:, 2], gathered[:, 3], band_index
    )
    populations_next = stream_tiles(relaxed, populations, fluid_mask, cycle_x, cycle_y)
    change = advect_tiles(charge, velocity, fluid_mask, cycle_x, cycle_y)
    charge_next = jnp.where(own_fluid, charge - change, charge)
    return (populations_next, charge_next, potential)


def solution(mesh):
    placed = (
        P(None, ("gx", "gy"), None, None, None),
        P(("gx", "gy"), None, None, None),
        P(("gx", "gy"), None, None, None),
        P(("gx", "gy")),
        P("gx", "gy", None),
        P(),
    )
    return jax.shard_map(
        per_device,
        mesh=mesh,
        in_specs=placed,
        out_specs=(
            P(None, ("gx", "gy"), None, None, None),
            P(("gx", "gy"), None, None, None),
            P("gx", "gy", None),
        ),
        check_vma=False,
    )
```

profile of v0, /device:TPU:0, one launch (start us, length us, event | category | flops | bytes accessed | tf_op | source)
XLA Modules:
  0.0 557.8 jit_solution(2015840348691275668)
XLA Ops:
  11.2 16.6 %all-reduce.2 = s32[64]{0:T(128)S(1)} all-reduce(s32[64]{0:T(128)S(1)} %dynamic-update-slice), channel_id=1, replica_groups=mesh['gx'=8,'gy'=16] {'gy'}, use_global_device_ids=true, to_apply=%add.2 | all-reduce | flops 64 | bytes 512
  35.9 3.7 all-to-all-start
  40.3 3.7 select_select_fusion
  49.6 5.3 collective-permute-start.2
  54.9 12.4 %all-to-all-done = f32[16,1,16,16,128]{4,2,3,1,0:T(8,128)S(1)} async-done(((f32[16,1,16,16,128]{4,2,3,1,0:T(8,128)}), f32[16,1,16,16,128]{4,2,3,1,0:T(8,128)S(1)}, u32[]{:S(2)}, u32[]{:S(2)}) %all-to-all-start) | async-done | bytes 2097184 | tf_op jit(solution)/shard_map/all_to_all | solution.py:315
  73.8 4.1 collective-permute-done.5
  119.9 5.3 collective-permute-start.19
  127.6 3.7 gather_fusion.2
  131.2 6.3 %bitcast_select_fusion = f32[16,1,3,16,16,128]{5,4,3,2,1,0:T(8,128)} fusion(f32[16,3,16,16,128]{4,3,2,1,0:T(8,128)} %gather_fusion.2, pred[16]{0:T(512)(128)(4,1)S(1)} %get-tuple-element.42), kind=kLoop, calls=%fused_computation.22 | loop fusion | flops 1572864 | bytes 12582928 | tf_op jit(solution)/shard_map/jit(_where)/select_n | solution.py:145
  137.5 6.8 %all-to-all-start.1 = ((f32[16,1,3,16,16,128]{5,4,3,2,1,0:T(8,128)}), f32[16,1,3,16,16,128]{5,4,3,2,1,0:T(8,128)}, u32[]{:S(2)}, u32[]{:S(2)}) async-start(f32[16,1,3,16,16,128]{5,4,3,2,1,0:T(8,128)} %bitcast_select_fusion), calls=%async_computation.1 | async-start | bytes 12582912 | tf_op jit(solution)/shard_map/all_to_all | solution.py:384
  144.4 4.5 fusion.342
  151.9 4.5 broadcast_multiply_fusion.2
  156.4 73.5 %all-to-all-done.1 = f32[16,1,3,16,16,128]{5,4,3,2,1,0:T(8,128)} async-done(((f32[16,1,3,16,16,128]{5,4,3,2,1,0:T(8,128)}), f32[16,1,3,16,16,128]{5,4,3,2,1,0:T(8,128)}, u32[]{:S(2)}, u32[]{:S(2)}) %all-to-all-start.1) | async-done | bytes 6291488 | tf_op jit(solution)/shard_map/all_to_all | solution.py:384
  229.9 4.6 gather_fusion.3
  238.3 3.9 fusion.247
  242.6 5.1 fusion.111
  248.6 12.8 %copy_multiply_fusion.9 = f32[4,16,16,128]{3,2,1,0:T(8,128)S(1)} fusion(f32[4,16,16,128]{3,1,0,2:T(8,128)S(1)} %multiply_add_fusion.2), kind=kLoop, calls=%fused_computation.499 | loop fusion | flops 131072 | bytes 1048576 | tf_op jit(solution)/shard_map/mul | solution.py:116
  264.0 5.2 add_multiply_fusion
  274.0 4.3 fusion.265
  282.7 8.0 %copy_add_fusion.1 = (f32[4,16,16,128]{3,2,1,0:T(8,128)}, f32[4,16,16,128]{3,2,1,0:T(8,128)S(1)}, f32[4,16,16,128]{3,2,1,0:T(8,128)S(1)}, f32[4,16,16,128]{3,2,1,0:T(8,128)S(1)}) fusion(f32[4,16,16,128]{3,1,0,2:T(8,128)S(1)} %get-tuple-element.125, f32[4,16,16,128]{3,1,0,2:T(8,128)S(1)} %get-tuple-element.5, f32[4,16,16,128]{3,1,0,2:T(8,128)S(1)} %copy-done.72, ...), kind=kLoop, calls=%fused_computation.465 | loop fusion | flops 3014656 | bytes 11534336 | tf_op jit(solution)/shard_map/add | solution.py:120
  341.2 66.9 %all-gather.2.cloned.1.call-done = f32[64,4,7,16,128]{4,3,2,0,1:T(8,128)} async-done(((f32[4,4,7,16,128]{4,3,2,0,1:T(8,128)}), f32[64,4,7,16,128]{4,3,2,0,1:T(8,128)}) %all-gather.2.cloned.1.call-update) | async-done | bytes 14680080 | tf_op jit(solution)/shard_map/all_gather | solution.py:401
  408.1 7.1 %gather_fusion.4 = f32[32,7,16,128]{3,2,1,0:T(8,128)} fusion(f32[64,4,7,16,128]{4,3,2,0,1:T(8,128)} %all-gather.2.cloned.1.call-done, s32[32]{0:T(128)S(1)} %get-tuple-element.258), kind=kCustom, calls=%fused_computation.4 | custom fusion | bytes 3670272 | tf_op jit(solution)/shard_map/gather | solution.py:408
  415.1 7.1 %gather_fusion.11 = f32[32,7,16,128]{3,2,1,0:T(8,128)} fusion(f32[64,4,7,16,128]{4,3,2,0,1:T(8,128)} %all-gather.2.cloned.1.call-done, s32[32]{0:T(128)S(1)} %get-tuple-element.257), kind=kCustom, calls=%fused_computation.11 | custom fusion | bytes 3670272 | tf_op jit(solution)/shard_map/gather | solution.py:407
  425.2 10.6 %slice_bitcast_fusion = (f32[64,7,16,128]{3,2,1,0:T(8,128)}, f32[64,7,16,128]{3,2,1,0:T(8,128)}, f32[64,7,16,128]{3,2,1,0:T(8,128)}, f32[64,7,16,128]{3,2,1,0:T(8,128)}) fusion(f32[64,4,7,16,128]{4,3,2,0,1:T(8,128)} %all-gather.2.cloned.1.call-done), kind=kLoop, calls=%fused_computation.25 | loop fusion | bytes 29360128 | tf_op jit(solution)/shard_map/squeeze | solution.py:426
  461.5 4.3 pad_maximum_fusion
  465.7 3.9 gather_fusion.8
  469.7 3.9 gather_fusion.6
  475.1 3.9 gather_fusion.10
  482.3 5.4 pad_maximum_fusion.1
  487.6 3.8 gather_fusion.15
  491.5 3.8 gather_fusion.13
  496.8 3.8 gather_fusion.17
  (556 shorter events, 221.8 us)
Async XLA Ops:
  7.2 32.5 %copy-start.133 = (f32[4]{0:T(128)S(1)}, f32[4]{0:T(128)}, u32[]{:S(2)}) copy-start(f32[4]{0:T(128)} %param.11) | copy-start | bytes 52
  35.9 31.4 %all-to-all-start = ((f32[16,1,16,16,128]{4,2,3,1,0:T(8,128)}), f32[16,1,16,16,128]{4,2,3,1,0:T(8,128)S(1)}, u32[]{:S(2)}, u32[]{:S(2)}) async-start(f32[16,1,16,16,128]{4,2,3,1,0:T(8,128)} %fusion), calls=%async_computation | async-start | bytes 4194304 | tf_op jit(solution)/shard_map/all_to_all | solution.py:315
  44.0 3.0 collective-permute-start
  44.0 5.6 collective-permute-start.1
  49.6 20.3 %collective-permute-start.2 = (f32[34,1,128]{2,1,0:T(1,128)S(1)}, f32[34,1,128]{2,1,0:T(1,128)S(1)}, u32[]{:S(2)}, u32[]{:S(2)}) collective-permute-start(f32[34,1,128]{2,1,0:T(1,128)S(1)} %get-tuple-element.166), channel_id=1, source_target_pairs={{1,0},{2,1},{3,2},{4,3},{5,4},{6,5},{7,6},{8,7},{9,8},{10,9},{11,1... | collective-permute-start | bytes 52232 | tf_op jit(solution)/shard_map/ppermute | solution.py:49
  54.9 15.0 %collective-permute-start.3 = (f32[34,1,128]{2,1,0:T(1,128)S(1)}, f32[34,1,128]{2,1,0:T(1,128)S(1)}, u32[]{:S(2)}, u32[]{:S(2)}) collective-permute-start(f32[34,1,128]{2,1,0:T(1,128)S(1)} %get-tuple-element.167), channel_id=1, source_target_pairs={{0,1},{1,2},{2,3},{3,4},{4,5},{5,6},{6,7},{7,8},{8,9},{9,10},{10,1... | collective-permute-start | bytes 52232 | tf_op jit(solution)/shard_map/ppermute | solution.py:48
  72.4 1.5 collective-permute-start.4
  72.4 5.6 collective-permute-start.5
  78.0 3.8 collective-permute-start.6
  78.1 7.1 %collective-permute-start.7 = (f32[34,1,128]{2,1,0:T(1,128)S(1)}, f32[34,1,128]{2,1,0:T(1,128)S(1)}, u32[]{:S(2)}, u32[]{:S(2)}) collective-permute-start(f32[34,1,128]{2,1,0:T(1,128)S(1)} %get-tuple-element.165), channel_id=1, source_target_pairs={{0,1},{1,2},{2,3},{3,4},{4,5},{5,6},{6,7},{7,8},{8,9},{9,10},{10,1... | collective-permute-start | bytes 52232 | tf_op jit(solution)/shard_map/ppermute | solution.py:48
  87.3 1.5 collective-permute-start.8
  87.3 4.4 collective-permute-start.9
  91.7 3.8 collective-permute-start.10
  91.8 7.1 %collective-permute-start.11 = (f32[34,1,128]{2,1,0:T(1,128)S(1)}, f32[34,1,128]{2,1,0:T(1,128)S(1)}, u32[]{:S(2)}, u32[]{:S(2)}) collective-permute-start(f32[34,1,128]{2,1,0:T(1,128)S(1)} %get-tuple-element.163), channel_id=1, source_target_pairs={{0,1},{1,2},{2,3},{3,4},{4,5},{5,6},{6,7},{7,8},{8,9},{9,10},{10,1... | collective-permute-start | bytes 52232 | tf_op jit(solution)/shard_map/ppermute | solution.py:48
  101.1 1.5 collective-permute-start.12
  101.1 4.4 collective-permute-start.13
  105.5 3.8 collective-permute-start.14
  105.6 7.1 %collective-permute-start.15 = (f32[34,1,128]{2,1,0:T(1,128)S(1)}, f32[34,1,128]{2,1,0:T(1,128)S(1)}, u32[]{:S(2)}, u32[]{:S(2)}) collective-permute-start(f32[34,1,128]{2,1,0:T(1,128)S(1)} %get-tuple-element.161), channel_id=1, source_target_pairs={{0,1},{1,2},{2,3},{3,4},{4,5},{5,6},{6,7},{7,8},{8,9},{9,10},{10,1... | collective-permute-start | bytes 52232 | tf_op jit(solution)/shard_map/ppermute | solution.py:48
  115.2 4.4 collective-permute-start.16
  115.2 4.4 collective-permute-start.17
  119.6 7.4 %collective-permute-start.18 = (f32[34,1,128]{2,1,0:T(1,128)S(1)}, f32[34,1,128]{2,1,0:T(1,128)S(1)}, u32[]{:S(2)}, u32[]{:S(2)}) collective-permute-start(f32[34,1,128]{2,1,0:T(1,128)S(1)} %get-tuple-element.158), channel_id=1, source_target_pairs={{0,1},{1,2},{2,3},{3,4},{4,5},{5,6},{6,7},{7,8},{8,9},{9,10},{10,1... | collective-permute-start | bytes 52232 | tf_op jit(solution)/shard_map/ppermute | solution.py:48
  119.9 7.1 %collective-permute-start.19 = (f32[34,1,128]{2,1,0:T(1,128)S(1)}, f32[34,1,128]{2,1,0:T(1,128)S(1)}, u32[]{:S(2)}, u32[]{:S(2)}) collective-permute-start(f32[34,1,128]{2,1,0:T(1,128)S(1)} %get-tuple-element.159), channel_id=1, source_target_pairs={{1,0},{2,1},{3,2},{4,3},{5,4},{6,5},{7,6},{8,7},{9,8},{10,9},{11,1... | collective-permute-start | bytes 52232 | tf_op jit(solution)/shard_map/ppermute | solution.py:49
  137.5 92.4 %all-to-all-start.1 = ((f32[16,1,3,16,16,128]{5,4,3,2,1,0:T(8,128)}), f32[16,1,3,16,16,128]{5,4,3,2,1,0:T(8,128)}, u32[]{:S(2)}, u32[]{:S(2)}) async-start(f32[16,1,3,16,16,128]{5,4,3,2,1,0:T(8,128)} %bitcast_select_fusion), calls=%async_computation.1 | async-start | bytes 12582912 | tf_op jit(solution)/shard_map/all_to_all | solution.py:384
  144.3 263.8 %all-gather.2.cloned.1.call-start = ((), (), s32[]{:S(2)}) async-start(), calls=%async_computation.2 | async-start | bytes 15597568 | tf_op jit(solution)/shard_map/all_gather | solution.py:401
  149.0 85.5 %copy-start.12 = (f32[1,4,16,16,128]{4,3,2,1,0:T(8,128)}, f32[1,4,16,16,128]{4,3,2,1,0:T(8,128)S(1)}, u32[]{:S(2)}) copy-start(f32[1,4,16,16,128]{4,3,2,1,0:T(8,128)S(1)} %get-tuple-element.65) | copy-start | bytes 1572868
  149.0 88.9 %copy-start.9 = (f32[1,4,16,16,128]{4,3,2,1,0:T(8,128)}, f32[1,4,16,16,128]{4,3,2,1,0:T(8,128)S(1)}, u32[]{:S(2)}) copy-start(f32[1,4,16,16,128]{4,3,2,1,0:T(8,128)S(1)} %get-tuple-element.64) | copy-start | bytes 1572868
  149.0 89.2 %copy-start.15 = (f32[1,4,16,16,128]{4,3,2,1,0:T(8,128)}, f32[1,4,16,16,128]{4,3,2,1,0:T(8,128)S(1)}, u32[]{:S(2)}) copy-start(f32[1,4,16,16,128]{4,3,2,1,0:T(8,128)S(1)} %get-tuple-element.72) | copy-start | bytes 1572868
  149.0 87.0 %copy-start.2 = (f32[4,16,16,128]{3,2,1,0:T(8,128)S(1)}, f32[4,16,16,128]{3,2,1,0:T(8,128)}, u32[]{:S(2)}) copy-start(f32[4,16,16,128]{3,2,1,0:T(8,128)} %param.7) | copy-start | bytes 1572868
  247.7 31.5 %copy-start.8 = (f32[4,16,16,128]{3,1,0,2:T(8,128)}, f32[4,16,16,128]{3,1,0,2:T(8,128)S(1)}, u32[]{:S(2)}) copy-start(f32[4,16,16,128]{3,1,0,2:T(8,128)S(1)} %get-tuple-element.9) | copy-start | bytes 1572868
  248.6 34.1 %copy-start.55 = (f32[4,16,16,128]{3,1,0,2:T(8,128)}, f32[4,16,16,128]{3,1,0,2:T(8,128)S(1)}, u32[]{:S(2)}) copy-start(f32[4,16,16,128]{3,1,0,2:T(8,128)S(1)} %multiply_add_fusion.2) | copy-start | bytes 1572868
  415.1 46.3 %collective-permute-start.20 = (f32[1,32,7,16,128]{4,3,2,1,0:T(8,128)}, f32[1,32,7,16,128]{4,3,2,1,0:T(8,128)}, u32[]{:S(2)}, u32[]{:S(2)}) collective-permute-start(f32[1,32,7,16,128]{4,3,2,1,0:T(8,128)} %bitcast.526), channel_id=1, source_target_pairs={{0,16},{16,32},{32,48},{48,64},{64,80},{80,96},{96,112},{112,0},{1... | collective-permute-start | bytes 5505032 | tf_op jit(solution)/shard_map/ppermute | solution.py:48
  422.2 60.0 %collective-permute-start.21 = (f32[1,32,7,16,128]{4,3,2,1,0:T(8,128)}, f32[1,32,7,16,128]{4,3,2,1,0:T(8,128)}, u32[]{:S(2)}, u32[]{:S(2)}) collective-permute-start(f32[1,32,7,16,128]{4,3,2,1,0:T(8,128)} %bitcast.525), channel_id=1, source_target_pairs={{16,0},{32,16},{48,32},{64,48},{80,64},{96,80},{112,96},{0,112},{1... | collective-permute-start | bytes 5505032 | tf_op jit(solution)/shard_map/ppermute | solution.py:49
  (130 other events, 1303.1 us)
Sparse Core Ops, SparseCore 0:
  302.5 105.5 all-gather.1
where the time goes:
time: 568 us; the launch traced here: 558 us
  waiting for transfers between devices  185 us (33%)
  local copies, waits for them, and re-layouts  154 us (27%)
  other arithmetic  149 us (26%)
  starting transfers between devices  35.7 us (6%)
  between operations  17.1 us (3%)
  blocking collectives  16.6 us (3%)
    all_to_all x1, waiting for transfers between devices, per_device(): lax.all_to_all(spread_rows(field_local, back_tile, back_filled), 'gy', sp...  73.5 us
    all_gather x1, waiting for transfers between devices, per_device(): gathered = lax.all_gather(package, 'gy', axis=0, tiled=True)  66.9 us
    unnamed x322, local copies, waits for them, and re-layouts  37 us
    ppermute x11, waiting for transfers between devices, extended(): before = lax.ppermute(last, axis, up)  25.4 us
    unnamed x8, other arithmetic  19.2 us
    ppermute x11, starting transfers between devices, extended(): after = lax.ppermute(first, axis, down)  16.8 us
    unnamed x1, blocking collectives  16.6 us
    add x4, other arithmetic, collide(): population[direction] - (population[direction] - equilibrium) / relax_time  16.5 us
  transfers between devices with their start and end apart: 25, of which 18 were waited for; matrix products, arithmetic and copies ran while one was open for 22% of the time, Pallas kernels for 0%

commit v1 on v0

v1 whole, which is shorter than its diff:
```python
import functools

import jax
import jax.numpy as jnp
from jax import lax
from jax.experimental import pallas as pl
from jax.experimental.pallas import tpu as pltpu
from jax.sharding import PartitionSpec as P

EDGE = 16
DEPTH = 128
BLOCK = 32
PHASES = 4
TILES = 4
GROUPS = 16
BANDS = 8
COLS = 32
SIDE = 8
MESH = pl.DeviceIdType.MESH

LATTICE = (
    (0, 0, 0),
    (1, 0, 0),
    (-1, 0, 0),
    (0, 1, 0),
    (0, -1, 0),
    (0, 0, 1),
    (0, 0, -1),
    (1, 1, 0),
    (-1, -1, 0),
    (1, -1, 0),
    (-1, 1, 0),
    (1, 0, 1),
    (-1, 0, -1),
    (1, 0, -1),
    (-1, 0, 1),
    (0, 1, 1),
    (0, -1, -1),
    (0, 1, -1),
    (0, -1, 1),
)
WEIGHTS = (1.0 / 3.0, 1.0 / 18.0, 1.0 / 36.0)
PAIRS = ((1, 2), (3, 4), (5, 6), (7, 8), (9, 10), (11, 12), (13, 14), (15, 16), (17, 18))
relax_time = 0.8
screening = 0.001
spectrum_low = 0.1
spectrum_high = 2.0

AROUND = tuple((dx, dy) for dx in (-1, 0, 1) for dy in (-1, 0, 1) if (dx, dy) != (0, 0))

T_PEER = 0
T_BACK = 4
T_OWNER = 20
T_YLO = 24
T_YHI = 28
T_XIN = 32
T_CLO = 36
T_CHI = 40
T_ROW = 44
T_UP = 48
T_UPLO = 52
T_UPHI = 56
T_DN = 60
T_DNLO = 64
T_DNHI = 68
T_FACE = 72
T_SIZE = 80


def opposite(direction):
    return LATTICE.index(tuple(-entry for entry in LATTICE[direction]))


def crossing(axis_index, face_sign):
    return [d for d in range(19) if LATTICE[d][axis_index] == face_sign]


def shifted_id(dx, dy):
    gx = lax.rem(lax.axis_index("gx") + dx + BANDS, BANDS)
    gy = lax.rem(lax.axis_index("gy") + dy + GROUPS, GROUPS)
    return {"gx": gx, "gy": gy}


def span(step, width, pad):
    if step == 0:
        return pl.ds(0, BLOCK), pl.ds(pad, BLOCK)
    if step > 0:
        return pl.ds(BLOCK - width, width), pl.ds(pad - width, width)
    return pl.ds(0, width), pl.ds(pad + BLOCK, width)


def halo_copies(block_ref, ext_ref, width, send_sem, recv_sem):
    copies = []
    for n, (dx, dy) in enumerate(AROUND):
        src_i, dst_i = span(dx, width, width)
        src_j, dst_j = span(dy, SIDE, SIDE)
        copies.append(
            pltpu.make_async_remote_copy(
                src_ref=block_ref.at[src_i, src_j],
                dst_ref=ext_ref.at[dst_i, dst_j],
                send_sem=send_sem.at[n],
                recv_sem=recv_sem.at[n],
                device_id=shifted_id(dx, dy),
                device_id_type=MESH,
            )
        )
    return copies


def start_kernel(ids_ref, phase_ref, all_ref, ext_ref, send_sem, recv_sem, ids_send, ids_recv, own_sem):
    barrier = pltpu.get_barrier_semaphore()
    targets = [shifted_id(0, k) for k in range(1, GROUPS)]
    targets += [shifted_id(dx, dy) for dx, dy in AROUND if dx != 0]
    for target in targets:
        pl.semaphore_signal(barrier, inc=1, device_id=target, device_id_type=MESH)
    pl.semaphore_wait(barrier, len(targets))
    copies = []
    for k in range(1, GROUPS):
        copies.append((k, shifted_id(0, k)))
    copies.append((GROUPS, shifted_id(-1, 0)))
    copies.append((GROUPS + 1, shifted_id(1, 0)))
    started = []
    for k, target in copies:
        copy = pltpu.make_async_remote_copy(
            src_ref=ids_ref,
            dst_ref=all_ref.at[k],
            send_sem=ids_send.at[k],
            recv_sem=ids_recv.at[k],
            device_id=target,
            device_id_type=MESH,
        )
        copy.start()
        started.append(copy)
    for copy in halo_copies(phase_ref, ext_ref, 5, send_sem, recv_sem):
        copy.start()
        started.append(copy)
    own = [
        pltpu.make_async_copy(ids_ref, all_ref.at[0], own_sem.at[0]),
        pltpu.make_async_copy(
            phase_ref, ext_ref.at[pl.ds(5, BLOCK), pl.ds(SIDE, BLOCK)], own_sem.at[1]
        ),
    ]
    for copy in own:
        copy.start()
    for copy in own:
        copy.wait()
    for copy in started:
        copy.wait()


def exchange_start(ids, phase):
    vmem = pl.BlockSpec(memory_space=pltpu.VMEM)
    return pl.pallas_call(
        start_kernel,
        out_shape=(
            jax.ShapeDtypeStruct((GROUPS + 2, 8, DEPTH), jnp.int32),
            jax.ShapeDtypeStruct((BLOCK + 10, BLOCK + 2 * SIDE, DEPTH), jnp.int32),
        ),
        in_specs=[vmem, vmem],
        out_specs=(vmem, vmem),
        scratch_shapes=[
            pltpu.SemaphoreType.DMA((8,)),
            pltpu.SemaphoreType.DMA((8,)),
            pltpu.SemaphoreType.DMA((GROUPS + 2,)),
            pltpu.SemaphoreType.DMA((GROUPS + 2,)),
            pltpu.SemaphoreType.DMA((2,)),
        ],
        compiler_params=pltpu.CompilerParams(
            collective_id=0, has_side_effects=True, vmem_limit_bytes=8 << 20
        ),
        name="start",
    )(ids, phase)


def halo_kernel(block_ref, ext_ref, send_sem, recv_sem, own_sem):
    barrier = pltpu.get_barrier_semaphore()
    for dx, dy in AROUND:
        pl.semaphore_signal(barrier, inc=1, device_id=shifted_id(dx, dy), device_id_type=MESH)
    pl.semaphore_wait(barrier, len(AROUND))
    copies = halo_copies(block_ref, ext_ref, 4, send_sem, recv_sem)
    for copy in copies:
        copy.start()
    own = pltpu.make_async_copy(
        block_ref, ext_ref.at[pl.ds(4, BLOCK), pl.ds(SIDE, BLOCK)], own_sem
    )
    own.start()
    own.wait()
    for copy in copies:
        copy.wait()


def exchange_halo(block):
    vmem = pl.BlockSpec(memory_space=pltpu.VMEM)
    return pl.pallas_call(
        halo_kernel,
        out_shape=jax.ShapeDtypeStruct((BLOCK + 8, BLOCK + 2 * SIDE, DEPTH), jnp.float32),
        in_specs=[vmem],
        out_specs=vmem,
        scratch_shapes=[
            pltpu.SemaphoreType.DMA((8,)),
            pltpu.SemaphoreType.DMA((8,)),
            pltpu.SemaphoreType.DMA,
        ],
        compiler_params=pltpu.CompilerParams(
            collective_id=1, has_side_effects=True, vmem_limit_bytes=8 << 20
        ),
        name="halo",
    )(block)


def table_kernel(me_ref, ids_ref, out_ref, row_of):
    me = me_ref[0]

    def place(p, carry):
        k = lax.rem(me - p + GROUPS, GROUPS)
        for s in range(TILES):
            row_of[ids_ref[k, s]] = p * TILES + s
        return carry

    lax.fori_loop(0, GROUPS, place, 0)
    for p in range(GROUPS):
        out_ref[T_BACK + p] = 0
    for t in range(TILES):
        slot = row_of[(t // 2) * COLS + me * 2 + t % 2]
        peer = slot // TILES
        out_ref[T_PEER + t] = peer
        out_ref[T_BACK + peer] = t
    for s in range(TILES):
        own = ids_ref[0, s]
        row, col = own // COLS, lax.rem(own, COLS)
        left, right = lax.rem(col + COLS - 1, COLS), lax.rem(col + 1, COLS)
        other = (1 - row) * COLS
        out_ref[T_OWNER + s] = col // 2
        out_ref[T_YLO + s] = row_of[row * COLS + left]
        out_ref[T_YHI + s] = row_of[row * COLS + right]
        out_ref[T_XIN + s] = row_of[other + col]
        out_ref[T_CLO + s] = row_of[other + left]
        out_ref[T_CHI + s] = row_of[other + right]
        out_ref[T_ROW + s] = row
        out_ref[T_FACE + s] = row
        for slot, base, first in ((GROUPS, COLS, T_UP), (GROUPS + 1, 0, T_DN)):
            col = lax.rem(ids_ref[slot, s], COLS)
            left, right = lax.rem(col + COLS - 1, COLS), lax.rem(col + 1, COLS)
            out_ref[first + s] = row_of[base + col]
            out_ref[first + 4 + s] = row_of[base + left]
            out_ref[first + 8 + s] = row_of[base + right]


def make_table(me, ids):
    smem = pl.BlockSpec(memory_space=pltpu.SMEM)
    return pl.pallas_call(
        table_kernel,
        out_shape=jax.ShapeDtypeStruct((T_SIZE,), jnp.int32),
        in_specs=[smem, smem],
        out_specs=smem,
        scratch_shapes=[pltpu.SMEM((2 * COLS,), jnp.int32)],
        name="table",
    )(me, ids)


def spread_kernel(ids_ref, charge_ref, mask_ref, out_ref, masked):
    def fill(s, carry):
        def rows(i, inner):
            flags = mask_ref[s, i + 1, pl.ds(1, EDGE), :].astype(jnp.float32)
            masked[s, i] = charge_ref[s, i] * flags
            return inner

        return lax.fori_loop(0, EDGE, rows, carry)

    lax.fori_loop(0, TILES, fill, 0)

    def send(p, carry):
        slot = 0
        for s in range(1, TILES):
            owner = lax.rem(ids_ref[s], COLS) // 2
            slot = jnp.where(owner == p, s, slot)
        out_ref[p] = masked[slot]
        return carry

    lax.fori_loop(0, GROUPS, send, 0)


def spread(tile_ids, charge, fluid_mask):
    vmem = pl.BlockSpec(memory_space=pltpu.VMEM)
    return pl.pallas_call(
        spread_kernel,
        out_shape=jax.ShapeDtypeStruct((GROUPS, EDGE, EDGE, DEPTH), jnp.float32),
        in_specs=[pl.BlockSpec(memory_space=pltpu.SMEM), vmem, vmem],
        out_specs=vmem,
        scratch_shapes=[pltpu.VMEM((TILES, EDGE, EDGE, DEPTH), jnp.float32)],
        compiler_params=pltpu.CompilerParams(vmem_limit_bytes=16 << 20),
        name="spread",
    )(tile_ids, charge, fluid_mask)


def assemble_kernel(table_ref, arrived_ref, out_ref):
    out_ref[...] = arrived_ref[0]


def assemble(table, arrived):
    return pl.pallas_call(
        assemble_kernel,
        out_shape=jax.ShapeDtypeStruct((BLOCK, BLOCK, DEPTH), jnp.float32),
        grid_spec=pltpu.PrefetchScalarGridSpec(
            num_scalar_prefetch=1,
            grid=(TILES,),
            in_specs=[
                pl.BlockSpec((1, EDGE, EDGE, DEPTH), lambda t, tab: (tab[T_PEER + t], 0, 0, 0))
            ],
            out_specs=pl.BlockSpec((EDGE, EDGE, DEPTH), lambda t, tab: (t // 2, t % 2, 0)),
        ),
        compiler_params=pltpu.CompilerParams(vmem_limit_bytes=8 << 20),
        name="assemble",
    )(table, arrived)


WIDE = BLOCK + 2 * SIDE
TALL = BLOCK + 8
ROOM = WIDE + 16
INNER = pl.ds(8, WIDE)
BEFORE = pl.ds(7, WIDE)
AFTER = pl.ds(9, WIDE)
PACK = 24


def harmonic(left, right):
    return 2.0 * left * right / (left + right)


def solve_kernel(
    table_ref, permit_ref, phase_ref, source_ref, pot_ref, send_ref, permit, coef, resid, upd_a, upd_b, total, pack
):
    center = 0.5 * (spectrum_high + spectrum_low)
    half = 0.5 * (spectrum_high - spectrum_low)
    ratio = center / half

    def look_up(i, carry):
        label = phase_ref[i]
        value = jnp.where(label == 0, permit_ref[0], 0.0)
        for k in range(1, PHASES):
            value = jnp.where(label == k, permit_ref[k], value)
        permit[i] = value
        return carry

    lax.fori_loop(0, TALL + 2, look_up, 0)

    def weigh(i, below):
        here = permit[i + 1]
        above = harmonic(here, permit[i + 2])
        right = harmonic(here, pltpu.roll(here, WIDE - 1, 0))
        left = pltpu.roll(right, 1, 0)
        up = harmonic(here, pltpu.roll(here, DEPTH - 1, 1))
        down = pltpu.roll(up, 1, 1)
        scale = 1.0 / (above + below + right + left + up + down + screening)
        for k, weight in enumerate((above, below, right, left, up, down)):
            coef[k, i] = weight * scale
        first = source_ref[i] * scale
        resid[i] = first
        first = first * (1.0 / center)
        upd_a[i, INNER] = first
        total[i] = first
        return above

    lax.fori_loop(0, TALL, weigh, harmonic(permit[0], permit[1]))

    rho = 1.0 / ratio
    old, new = upd_a, upd_b
    for sweep in range(3):
        rho_new = 1.0 / (2.0 * ratio - rho)
        keep, gain = rho_new * rho, 2.0 * rho_new / half

        def relax(i, carry, old=old, new=new, keep=keep, gain=gain):
            here = old[i, INNER]
            near = coef[0, i] * old[i + 1, INNER] + coef[1, i] * old[i - 1, INNER]
            near += coef[2, i] * old[i, AFTER] + coef[3, i] * old[i, BEFORE]
            near += coef[4, i] * pltpu.roll(here, DEPTH - 1, 1)
            near += coef[5, i] * pltpu.roll(here, 1, 1)
            left = resid[i] - here + near
            resid[i] = left
            here = keep * here + gain * left
            new[i, INNER] = here
            total[i] = total[i] + here
            return carry

        lax.fori_loop(sweep + 1, TALL - 1 - sweep, relax, 0)
        old, new = new, old
        rho = rho_new

    def emit(i, carry):
        pot_ref[i] = total[i + 4, pl.ds(SIDE, BLOCK)]
        return carry

    lax.fori_loop(0, BLOCK, emit, 0)
    for t in range(TILES):
        i0, j0 = 4 + (t // 2) * EDGE, SIDE + (t % 2) * EDGE

        def rows(i, carry, t=t, i0=i0, j0=j0):
            pack[t, i] = total[i0 + i, pl.ds(j0, EDGE)]
            for place, ref in ((EDGE + 2, total), (EDGE + 6, source_ref)):
                pack[t, place, pl.ds(i, 1)] = ref[i0 + i, pl.ds(j0 - 1, 1)]
                pack[t, place + 1, pl.ds(i, 1)] = ref[i0 + i, pl.ds(j0 + EDGE, 1)]
            return carry

        lax.fori_loop(0, EDGE, rows, 0)
        for place, ref in ((EDGE, total), (EDGE + 4, source_ref)):
            pack[t, place] = ref[i0 - 1, pl.ds(j0, EDGE)]
            pack[t, place + 1] = ref[i0 + EDGE, pl.ds(j0, EDGE)]

    def send(p, carry):
        send_ref[p] = pack[table_ref[T_BACK + p]]
        return carry

    lax.fori_loop(0, GROUPS, send, 0)


def solve(table, permittivity, phase, source):
    vmem = pl.BlockSpec(memory_space=pltpu.VMEM)
    smem = pl.BlockSpec(memory_space=pltpu.SMEM)
    f32 = jnp.float32
    return pl.pallas_call(
        solve_kernel,
        out_shape=(
            jax.ShapeDtypeStruct((BLOCK, BLOCK, DEPTH), f32),
            jax.ShapeDtypeStruct((GROUPS, PACK, EDGE, DEPTH), f32),
        ),
        in_specs=[smem, smem, vmem, vmem],
        out_specs=(vmem, vmem),
        scratch_shapes=[
            pltpu.VMEM((TALL + 2, WIDE, DEPTH), f32),
            pltpu.VMEM((6, TALL, WIDE, DEPTH), f32),
            pltpu.VMEM((TALL, WIDE, DEPTH), f32),
            pltpu.VMEM((TALL, ROOM, DEPTH), f32),
            pltpu.VMEM((TALL, ROOM, DEPTH), f32),
            pltpu.VMEM((TALL, WIDE, DEPTH), f32),
            pltpu.VMEM((TILES, PACK, EDGE, DEPTH), f32),
        ],
        compiler_params=pltpu.CompilerParams(vmem_limit_bytes=32 << 20),
        name="solve",
    )(table, permittivity, phase, source)


def collide_rows(pops, charge, field):
    force = [charge * component for component in field]
    sums = {}
    diffs = {}
    for a, b in PAIRS:
        sums[a] = pops[a] + pops[b]
        diffs[a] = pops[a] - pops[b]
    density = pops[0]
    for a, _ in PAIRS:
        density = density + sums[a]
    momentum = [
        diffs[1] + diffs[7] + diffs[9] + diffs[11] + diffs[13],
        diffs[3] + diffs[7] - diffs[9] + diffs[15] + diffs[17],
        diffs[5] + diffs[11] - diffs[13] + diffs[15] - diffs[17],
    ]
    inverse = 1.0 / density
    velocity = [(momentum[d] + 0.5 * force[d]) * inverse for d in range(3)]
    scale = 1.0 - 0.5 / relax_time
    rate = 1.0 / relax_time
    speed = velocity[0] * velocity[0] + velocity[1] * velocity[1] + velocity[2] * velocity[2]
    work = velocity[0] * force[0] + velocity[1] * force[1] + velocity[2] * force[2]
    weighted = rate * density
    base = weighted - (1.5 * weighted) * speed - (3.0 * scale) * work
    odd = [3.0 * weighted * velocity[d] + (3.0 * scale) * force[d] for d in range(3)]
    inner = [4.5 * weighted * velocity[d] + (9.0 * scale) * force[d] for d in range(3)]
    keep = 1.0 - rate
    result = [None] * 19
    result[0] = keep * pops[0] + WEIGHTS[0] * base
    for a, b in PAIRS:
        step = LATTICE[a]
        axes = [d for d in range(3) if step[d] != 0]
        if len(axes) == 1:
            (d,) = axes
            cu, co, ci = velocity[d], odd[d], inner[d]
            weight = WEIGHTS[1]
        else:
            d, e = axes
            weight = WEIGHTS[2]
            if step[d] * step[e] > 0:
                cu, co, ci = velocity[d] + velocity[e], odd[d] + odd[e], inner[d] + inner[e]
            else:
                cu, co, ci = velocity[d] - velocity[e], odd[d] - odd[e], inner[d] - inner[e]
        even = weight * (base + cu * ci)
        lean = weight * co
        result[a] = keep * pops[a] + (even + lean)
        result[b] = keep * pops[b] + (even - lean)
    return result, velocity


def collide_kernel(table_ref, pops_ref, charge_ref, mask_ref, pot_ref, out_ref, vel_ref, face_ref, grown):
    def place(i, carry):
        grown[i + 1, pl.ds(8, EDGE)] = pot_ref[0, i]
        grown[i + 1, pl.ds(7, 1)] = pot_ref[0, EDGE + 2, pl.ds(i, 1)]
        grown[i + 1, pl.ds(8 + EDGE, 1)] = pot_ref[0, EDGE + 3, pl.ds(i, 1)]
        return carry

    lax.fori_loop(0, EDGE, place, 0)
    grown[0, pl.ds(8, EDGE)] = pot_ref[0, EDGE]
    grown[EDGE + 1, pl.ds(8, EDGE)] = pot_ref[0, EDGE + 1]
    y_low, y_high = crossing(1, -1), crossing(1, 1)

    def rows(i, carry):
        here = grown[i + 1, pl.ds(8, EDGE)]
        field = [
            0.5 * (grown[i, pl.ds(8, EDGE)] - grown[i + 2, pl.ds(8, EDGE)]),
            0.5 * (grown[i + 1, pl.ds(7, EDGE)] - grown[i + 1, pl.ds(9, EDGE)]),
            0.5 * (pltpu.roll(here, 1, 1) - pltpu.roll(here, DEPTH - 1, 1)),
        ]
        pops = [pops_ref[q, 0, i] for q in range(19)]
        relaxed, velocity = collide_rows(pops, charge_ref[0, i], field)
        fluid = mask_ref[0, i + 1, pl.ds(1, EDGE), :] == 1
        for q in range(19):
            value = jnp.where(fluid, relaxed[q], pops[q])
            out_ref[q, 0, i] = value
            if q in y_low:
                face_ref[0, 2, y_low.index(q), pl.ds(i, 1)] = value[0:1]
            if q in y_high:
                face_ref[0, 3, y_high.index(q), pl.ds(i, 1)] = value[EDGE - 1 :]
        for d in range(3):
            vel_ref[d, 0, i] = velocity[d]
        face_ref[0, 2, 5, pl.ds(i, 1)] = velocity[1][0:1]
        face_ref[0, 3, 5, pl.ds(i, 1)] = velocity[1][EDGE - 1 :]
        return carry

    lax.fori_loop(0, EDGE, rows, 0)
    for face, sign, layer in ((0, -1, 0), (1, 1, EDGE - 1)):
        for k, q in enumerate(crossing(0, sign)):
            face_ref[0, face, k] = out_ref[q, 0, layer]
        face_ref[0, face, 5] = vel_ref[0, 0, layer]


def collide(table, populations, charge, fluid_mask, returned):
    f32 = jnp.float32
    return pl.pallas_call(
        collide_kernel,
        out_shape=(
            jax.ShapeDtypeStruct((19, TILES, EDGE, EDGE, DEPTH), f32),
            jax.ShapeDtypeStruct((3, TILES, EDGE, EDGE, DEPTH), f32),
            jax.ShapeDtypeStruct((TILES, 4, 6, EDGE, DEPTH), f32),
        ),
        grid_spec=pltpu.PrefetchScalarGridSpec(
            num_scalar_prefetch=1,
            grid=(TILES,),
            in_specs=[
                pl.BlockSpec((19, 1, EDGE, EDGE, DEPTH), lambda s, tab: (0, s, 0, 0, 0)),
                pl.BlockSpec((1, EDGE, EDGE, DEPTH), lambda s, tab: (s, 0, 0, 0)),
                pl.BlockSpec((1, EDGE + 2, EDGE + 2, DEPTH), lambda s, tab: (s, 0, 0, 0)),
                pl.BlockSpec((1, PACK, EDGE, DEPTH), lambda s, tab: (tab[T_OWNER + s], 0, 0, 0)),
            ],
            out_specs=[
                pl.BlockSpec((19, 1, EDGE, EDGE, DEPTH), lambda s, tab: (0, s, 0, 0, 0)),
                pl.BlockSpec((3, 1, EDGE, EDGE, DEPTH), lambda s, tab: (0, s, 0, 0, 0)),
                pl.BlockSpec((1, 4, 6, EDGE, DEPTH), lambda s, tab: (s, 0, 0, 0, 0)),
            ],
            scratch_shapes=[pltpu.VMEM((EDGE + 2, 32, DEPTH), f32)],
        ),
        compiler_params=pltpu.CompilerParams(vmem_limit_bytes=32 << 20),
        name="collide",
    )(table, populations, charge, fluid_mask, returned)


def outer_kernel(table_ref, up_ref, uplo_ref, uphi_ref, dn_ref, dnlo_ref, dnhi_ref, to_up, to_dn):
    plus, minus = crossing(0, 1), crossing(0, -1)
    for out, face, low, high, low_q, high_q in (
        (to_up, up_ref, uplo_ref, uphi_ref, plus.index(7), plus.index(9)),
        (to_dn, dn_ref, dnlo_ref, dnhi_ref, minus.index(10), minus.index(8)),
    ):
        for k in range(6):
            out[0, k] = face[0, 0, k]
        out[0, 6, pl.ds(0, 1)] = low[0, 0, low_q, pl.ds(EDGE - 1, 1)]
        out[0, 6, pl.ds(1, 1)] = high[0, 0, high_q, pl.ds(0, 1)]


def outer(table, gathered):
    def face(place, side):
        return pl.BlockSpec(
            (1, 1, 6, EDGE, DEPTH), lambda s, tab: (tab[place + s], side, 0, 0, 0)
        )

    shape = jax.ShapeDtypeStruct((TILES, 7, EDGE, DEPTH), jnp.float32)
    spec = pl.BlockSpec((1, 7, EDGE, DEPTH), lambda s, tab: (s, 0, 0, 0))
    return pl.pallas_call(
        outer_kernel,
        out_shape=(shape, shape),
        grid_spec=pltpu.PrefetchScalarGridSpec(
            num_scalar_prefetch=1,
            grid=(TILES,),
            in_specs=[
                face(T_UP, 1),
                face(T_UPLO, 1),
                face(T_UPHI, 1),
                face(T_DN, 0),
                face(T_DNLO, 0),
                face(T_DNHI, 0),
            ],
            out_specs=[spec, spec],
        ),
        compiler_params=pltpu.CompilerParams(vmem_limit_bytes=8 << 20),
        name="outer",
    )(table, *([gathered] * 6))


def stream_kernel(
    table_ref,
    relaxed_ref,
    vel_ref,
    charge_ref,
    mask_ref,
    rim_ref,
    ylo_ref,
    yhi_ref,
    xin_ref,
    clo_ref,
    chi_ref,
    below_ref,
    above_ref,
    pops_out,
    charge_out,
    xrim,
    corner,
):
    row = table_ref[T_ROW + pl.program_id(0)]
    plus = [crossing(0, 1), crossing(1, 1)]
    minus = [crossing(0, -1), crossing(1, -1)]

    def inside(side, low_q, high_q):
        for k in range(6):
            xrim[side, k] = xin_ref[0, 0, k]
        corner[side, pl.ds(0, 1)] = clo_ref[0, 0, low_q, pl.ds(EDGE - 1, 1)]
        corner[side, pl.ds(1, 1)] = chi_ref[0, 0, high_q, pl.ds(0, 1)]

    def outside(side, ref):
        for k in range(6):
            xrim[side, k] = ref[0, k]
        corner[side, pl.ds(0, 2)] = ref[0, 6, pl.ds(0, 2)]

    @pl.when(row == 0)
    def _():
        outside(0, below_ref)
        inside(1, minus[0].index(10), minus[0].index(8))

    @pl.when(row == 1)
    def _():
        inside(0, plus[0].index(7), plus[0].index(9))
        outside(1, above_ref)

    place = lax.broadcasted_iota(jnp.int32, (EDGE, DEPTH), 0)
    first, last = place == 0, place == EDGE - 1

    def rows(i, low_edge, high_edge):
        own = mask_ref[0, i + 1, pl.ds(1, EDGE), :]
        own_fluid = own == 1
        for q in range(19):
            step_x, step_y, step_z = LATTICE[q]
            value_here = relaxed_ref[q, 0, i]
            if q == 0:
                pops_out[q, 0, i] = value_here
                continue
            side = None
            if step_x == 1 and low_edge:
                side, channel = 0, plus[0].index(q)
            if step_x == -1 and high_edge:
                side, channel = 1, minus[0].index(q)
            if side is None:
                moved = value_here if step_x == 0 else relaxed_ref[q, 0, i - step_x]
            else:
                moved = xrim[side, channel]
            if step_y == 1:
                if side is None:
                    edge = ylo_ref[0, 0, plus[1].index(q), pl.ds(i - step_x, 1)]
                else:
                    edge = corner[side, pl.ds(0, 1)]
                moved = jnp.where(first, edge, pltpu.roll(moved, 1, 0))
            elif step_y == -1:
                if side is None:
                    edge = yhi_ref[0, 0, minus[1].index(q), pl.ds(i - step_x, 1)]
                else:
                    edge = corner[side, pl.ds(1, 1)]
                moved = jnp.where(last, edge, pltpu.roll(moved, EDGE - 1, 0))
            from_fluid = mask_ref[0, i + 1 - step_x, pl.ds(1 - step_y, EDGE), :]
            if step_z != 0:
                moved = pltpu.roll(moved, step_z % DEPTH, 1)
                from_fluid = pltpu.roll(from_fluid, step_z % DEPTH, 1)
            bounced = relaxed_ref[opposite(q), 0, i]
            read = jnp.where(from_fluid == 1, moved, bounced)
            pops_out[q, 0, i] = jnp.where(own_fluid, read, value_here)

        charge = charge_ref[0, i]
        flag = own.astype(jnp.float32)

        def flux(speed_a, speed_b, value_a, value_b, flags):
            speed = 0.5 * (speed_a + speed_b)
            return speed * jnp.where(speed > 0, value_a, value_b) * flags

        speed = vel_ref[0, 0, i]
        if low_edge:
            other, other_speed = rim_ref[0, 0], xrim[0, 5]
        else:
            other, other_speed = charge_ref[0, i - 1], vel_ref[0, 0, i - 1]
        other_flag = mask_ref[0, i, pl.ds(1, EDGE), :].astype(jnp.float32)
        change = -flux(other_speed, speed, other, charge, other_flag * flag)
        if high_edge:
            other, other_speed = rim_ref[0, 1], xrim[1, 5]
        else:
            other, other_speed = charge_ref[0, i + 1], vel_ref[0, 0, i + 1]
        other_flag = mask_ref[0, i + 2, pl.ds(1, EDGE), :].astype(jnp.float32)
        change += flux(speed, other_speed, charge, other, flag * other_flag)

        speed = vel_ref[1, 0, i]
        other = jnp.where(first, rim_ref[0, 2, pl.ds(i, 1)], pltpu.roll(charge, 1, 0))
        other_speed = jnp.where(first, ylo_ref[0, 0, 5, pl.ds(i, 1)], pltpu.roll(speed, 1, 0))
        other_flag = mask_ref[0, i + 1, pl.ds(0, EDGE), :].astype(jnp.float32)
        change -= flux(other_speed, speed, other, charge, other_flag * flag)
        other = jnp.where(last, rim_ref[0, 3, pl.ds(i, 1)], pltpu.roll(charge, EDGE - 1, 0))
        other_speed = jnp.where(
            last, yhi_ref[0, 0, 5, pl.ds(i, 1)], pltpu.roll(speed, EDGE - 1, 0)
        )
        other_flag = mask_ref[0, i + 1, pl.ds(2, EDGE), :].astype(jnp.float32)
        change += flux(speed, other_speed, charge, other, flag * other_flag)

        speed = vel_ref[2, 0, i]
        over = flux(
            speed,
            pltpu.roll(speed, DEPTH - 1, 1),
            charge,
            pltpu.roll(charge, DEPTH - 1, 1),
            flag * pltpu.roll(flag, DEPTH - 1, 1),
        )
        change += over - pltpu.roll(over, 1, 1)
        charge_out[0, i] = jnp.where(own_fluid, charge - change, charge)

    rows(0, True, False)

    def middle(i, carry):
        rows(i, False, False)
        return carry

    lax.fori_loop(1, EDGE - 1, middle, 0)
    rows(EDGE - 1, False, True)


def stream(table, relaxed, velocity, charge, fluid_mask, returned, gathered, below, above):
    f32 = jnp.float32

    def face(place, side):
        return pl.BlockSpec(
            (1, 1, 6, EDGE, DEPTH), lambda s, tab: (tab[place + s], side, 0, 0, 0)
        )

    def inner_face(place):
        return pl.BlockSpec(
            (1, 1, 6, EDGE, DEPTH),
            lambda s, tab: (tab[place + s], tab[T_FACE + s], 0, 0, 0),
        )

    outer_spec = pl.BlockSpec((1, 7, EDGE, DEPTH), lambda s, tab: (s, 0, 0, 0))
    return pl.pallas_call(
        stream_kernel,
        out_shape=(
            jax.ShapeDtypeStruct((19, TILES, EDGE, EDGE, DEPTH), f32),
            jax.ShapeDtypeStruct((TILES, EDGE, EDGE, DEPTH), f32),
        ),
        grid_spec=pltpu.PrefetchScalarGridSpec(
            num_scalar_prefetch=1,
            grid=(TILES,),
            in_specs=[
                pl.BlockSpec((19, 1, EDGE, EDGE, DEPTH), lambda s, tab: (0, s, 0, 0, 0)),
                pl.BlockSpec((3, 1, EDGE, EDGE, DEPTH), lambda s, tab: (0, s, 0, 0, 0)),
                pl.BlockSpec((1, EDGE, EDGE, DEPTH), lambda s, tab: (s, 0, 0, 0)),
                pl.BlockSpec((1, EDGE + 2, EDGE + 2, DEPTH), lambda s, tab: (s, 0, 0, 0)),
                pl.BlockSpec((1, 4, EDGE, DEPTH), lambda s, tab: (tab[T_OWNER + s], 5, 0, 0)),
                face(T_YLO, 3),
                face(T_YHI, 2),
                inner_face(T_XIN),
                inner_face(T_CLO),
                inner_face(T_CHI),
                outer_spec,
                outer_spec,
            ],
            out_specs=[
                pl.BlockSpec((19, 1, EDGE, EDGE, DEPTH), lambda s, tab: (0, s, 0, 0, 0)),
                pl.BlockSpec((1, EDGE, EDGE, DEPTH), lambda s, tab: (s, 0, 0, 0)),
            ],
            scratch_shapes=[
                pltpu.VMEM((2, 6, EDGE, DEPTH), f32),
                pltpu.VMEM((2, 8, DEPTH), f32),
            ],
        ),
        compiler_params=pltpu.CompilerParams(vmem_limit_bytes=32 << 20),
        name="stream",
    )(
        table,
        relaxed,
        velocity,
        charge,
        fluid_mask,
        returned,
        gathered,
        gathered,
        gathered,
        gathered,
        gathered,
        below,
        above,
    )


def per_device(populations, charge, fluid_mask, tile_ids, phase_label, permittivity):
    outgoing = spread(tile_ids, charge, fluid_mask)
    arrived = lax.all_to_all(outgoing, "gy", split_axis=0, concat_axis=0, tiled=True)
    ids_row = jnp.pad(tile_ids[None], ((0, 7), (0, DEPTH - TILES)))
    ids_all, phase_ext = exchange_start(ids_row, phase_label)
    me = lax.axis_index("gy").astype(jnp.int32).reshape(1)
    table = make_table(me, ids_all[:, 0, :TILES])
    source_ext = exchange_halo(assemble(table, arrived))
    potential, packed = solve(table, permittivity, phase_ext, source_ext)
    returned = lax.all_to_all(packed, "gy", split_axis=0, concat_axis=0, tiled=True)
    relaxed, velocity, faces = collide(table, populations, charge, fluid_mask, returned)
    gathered = lax.all_gather(faces, "gy", axis=0, tiled=True)
    to_up, to_dn = outer(table, gathered)
    up = [(k, (k + 1) % BANDS) for k in range(BANDS)]
    below = lax.ppermute(to_up, "gx", up)
    above = lax.ppermute(to_dn, "gx", [(b, a) for a, b in up])
    populations_next, charge_next = stream(
        table, relaxed, velocity, charge, fluid_mask, returned, gathered, below, above
    )
    return (populations_next, charge_next, potential)


def solution(mesh):
    placed = (
        P(None, ("gx", "gy"), None, None, None),
        P(("gx", "gy"), None, None, None),
        P(("gx", "gy"), None, None, None),
        P(("gx", "gy")),
        P("gx", "gy", None),
        P(),
    )
    return jax.shard_map(
        per_device,
        mesh=mesh,
        in_specs=placed,
        out_specs=(
            P(None, ("gx", "gy"), None, None, None),
            P(("gx", "gy"), None, None, None),
            P("gx", "gy", None),
        ),
        check_vma=False,
    )
```

time: 568 us -> 274 us (0.48); the launches traced: 558 us -> 272 us
  other arithmetic: 149 us -> 0 us
  local copies, waits for them, and re-layouts: 154 us -> 18.1 us
  Pallas kernels: 0 us -> 97.5 us
  waiting for transfers between devices: 185 us -> 89.4 us
  blocking collectives: 16.6 us -> 42.4 us
  starting transfers between devices: 35.7 us -> 10.1 us
    pallas_call x0 -> x9, Pallas kernels: none -> 97.5 us  [the longest x1 36.9 us: exchange_start(): pl.pallas_call(start_kernel, out_shape=(jax.ShapeDtypeStruct((GROUPS + 2,...]
    all_to_all x2 -> x1, waiting for transfers between devices: 85.9 us -> 0.01 us  [per_device(): lax.all_to_all(outgoing, 'gy', split_axis=0, concat_axis=0, tiled=True)]
    gather x24 -> x0, local copies, waits for them, and re-layouts: 62.2 us -> none  [the longest x1 7.09 us: per_device(): low_edge = gathered[row_of[:band_cols], 0]]
    all_to_all x0 -> x1, blocking collectives: none -> 42.4 us  [per_device(): lax.all_to_all(packed, 'gy', split_axis=0, concat_axis=0, tiled=True)]
    mul x15 -> x0, other arithmetic: 32.4 us -> none  [the longest x1 12.8 us: collide(): 1.5 * speed_sq]
    slice x51 -> x2, local copies, waits for them, and re-layouts: 29.9 us -> 0.1 us  [per_device(): table = make_table(me, ids_all[:, 0, :TILES])]
    ppermute x22 -> x2, waiting for transfers between devices: 32.2 us -> 3.7 us  [the longest x1 3.7 us: per_device(): below = lax.ppermute(to_up, 'gx', up)]
    add x11 -> x0, other arithmetic: 28.4 us -> none  [the longest x4 16.5 us: collide(): population[direction] - (population[direction] - equilibrium) / relax_time]
  transfers between devices with their start and end apart: 25 -> 4, of which waited for: 18 -> 2; matrix products, arithmetic and copies ran while one was open for 22% -> 0% of each run, Pallas kernels for 0% -> 14%
where the time goes in v1:
time: 274 us; the launch traced here: 272 us
  Pallas kernels  97.5 us (36%)
  waiting for transfers between devices  89.4 us (33%)
  blocking collectives  42.4 us (15%)
  local copies, waits for them, and re-layouts  18.1 us (7%)
  between operations  14.2 us (5%)
  starting transfers between devices  10.1 us (4%)
    all_gather x1, waiting for transfers between devices, per_device(): gathered = lax.all_gather(faces, 'gy', axis=0, tiled=True)  85.7 us
    all_to_all x1, blocking collectives, per_device(): lax.all_to_all(packed, 'gy', split_axis=0, concat_axis=0, tiled=True)  42.4 us
    pallas_call x1, Pallas kernels, exchange_start(): pl.pallas_call(start_kernel, out_shape=(jax.ShapeDtypeStruct((GROUPS + 2,...  36.9 us
    pallas_call x1, Pallas kernels, solve(): pl.pallas_call(solve_kernel, out_shape=(jax.ShapeDtypeStruct((BLOCK, BLOC...  19 us
    unnamed x39, local copies, waits for them, and re-layouts  17.3 us
    pallas_call x1, Pallas kernels, stream(): pl.pallas_call(stream_kernel, out_shape=(jax.ShapeDtypeStruct((19, TILES,...  13.7 us
    pallas_call x1, Pallas kernels, exchange_halo(): pl.pallas_call(halo_kernel, out_shape=jax.ShapeDtypeStruct((BLOCK + 8, BL...  11.9 us
    pallas_call x1, Pallas kernels, collide(): pl.pallas_call(collide_kernel, out_shape=(jax.ShapeDtypeStruct((19, TILES...  11.2 us
  transfers between devices with their start and end apart: 4, of which 2 were waited for; matrix products, arithmetic and copies ran while one was open for 0% of the time, Pallas kernels for 14%

profile of v1, /device:TPU:0, one launch (start us, length us, event | category | flops | bytes accessed | tf_op | source)
XLA Modules:
  0.0 271.8 jit_solution(18224671914283764892)
XLA Ops:
  7.2 1.2 copy.17.mask_ref
  8.3 0.0 copy-start.7
  8.3 1.0 copy-done.7
  9.4 0.7 copy-done.16
  10.0 1.6 spread.1
  11.7 0.9 copy-done.1
  12.6 1.3 copy-done.6
  13.9 7.1 %all-to-all-start = ((f32[16,16,16,128]{3,2,1,0:T(8,128)}), f32[16,16,16,128]{3,2,1,0:T(8,128)S(1)}, u32[]{:S(2)}, u32[]{:S(2)}) async-start(f32[16,16,16,128]{3,2,1,0:T(8,128)} %copy-done.6), calls=%async_computation | async-start | bytes 4194304 | tf_op jit(solution)/shard_map/all_to_all | solution.py:811
  21.1 0.0 copy-start.18
  21.1 0.0 all-gather.2.cloned.1.call-start
  21.2 1.0 copy-done.13
  22.2 36.9 %start.1 = (s32[18,8,128]{2,1,0:T(8,128)S(1)}, s32[42,48,128]{2,1,0:T(8,128)S(1)}) custom-call(s32[8,128]{1,0:T(8,128)S(1)} %pad.4.ids_ref, s32[32,32,128]{2,1,0:T(8,128)S(1)} %copy-done.13), custom_call_target="tpu_custom_call" | custom-call | tf_op jit(solution)/shard_map/start/pallas_call | solution.py:153
  59.2 0.1 copy.14
  59.2 0.7 copy.15.ids_ref
  59.9 1.7 table.1.table_ref
  61.7 0.6 copy-done.14
  62.3 0.8 assemble.1.block_ref
  63.1 11.9 %halo.1.source_ref = f32[40,48,128]{2,1,0:T(8,128)S(1)} custom-call(f32[32,32,128]{2,1,0:T(8,128)S(1)} %assemble.1.block_ref), custom_call_target="tpu_custom_call" | custom-call | tf_op jit(solution)/shard_map/halo/pallas_call | solution.py:194
  75.0 19.0 %solve.1 = (f32[32,32,128]{2,1,0:T(8,128)}, f32[16,24,16,128]{3,2,1,0:T(8,128)S(1)}) custom-call(s32[80]{0:T(128)S(1)} %copy-done.14, f32[4]{0:T(128)S(1)} %copy-done.18, s32[42,48,128]{2,1,0:T(8,128)S(1)} %get-tuple-element.15.phase_ref, f32[40,48,128]{2,1,0:T(8,128)S(1)} %halo.1.source_ref), custom_call_target="tpu_custom_call" | custom-call | tf_op jit(solution)/shard_map/solve/pallas_call | solution.py:420
  94.1 42.4 %all_to_all.10.pot_ref.rim_ref = f32[16,24,16,128]{3,2,1,0:T(8,128)S(1)} all-to-all(f32[16,24,16,128]{3,2,1,0:T(8,128)S(1)} %get-tuple-element.16), channel_id=1, replica_groups=mesh['gx'=8,'gy'=16] {'gy'}, dimensions={0} | all-to-all | bytes 6291456 | tf_op jit(solution)/shard_map/all_to_all | solution.py:818
  136.5 11.2 %collide.1 = (f32[19,4,16,16,128]{4,3,2,1,0:T(8,128)S(1)}, f32[3,4,16,16,128]{4,3,2,1,0:T(8,128)S(1)}, f32[4,4,6,16,128]{4,3,2,1,0:T(8,128)S(1)}) custom-call(s32[80]{0:T(128)S(1)} %copy-done.15, f32[19,4,16,16,128]{4,3,2,1,0:T(8,128)} %pops_ref.1, f32[4,16,16,128]{3,2,1,0:T(8,128)S(1)} %copy-done.8, s32[4,18,18,128]{3,2,1,0:T(8,128)S(1)} %copy-done.2, ...), custom_call_target="tpu_custom_call" | custom-call | tf_op jit(solution)/shard_map/collide/pallas_call | solution.py:535
  147.7 3.9 %copy-done.4 = f32[19,4,16,16,128]{4,3,2,1,0:T(8,128)} copy-done((f32[19,4,16,16,128]{4,3,2,1,0:T(8,128)}, f32[19,4,16,16,128]{4,3,2,1,0:T(8,128)S(1)}, u32[]{:S(2)}) %copy-start.4) | copy-done | bytes 9961496
  151.6 1.2 copy-done.10
  152.7 0.9 copy-done.12
  153.6 0.0 all-gather.2.cloned.1.call-update
  153.6 85.7 %all-gather.2.cloned.1.call-done.up_ref.uplo_ref.uphi_ref.dn_ref.dnlo_ref.dnhi_ref.ylo_ref.yhi_ref.xin_ref.clo_ref.chi_ref = f32[64,4,6,16,128]{4,3,2,1,0:T(8,128)} async-done(((f32[4,4,6,16,128]{4,3,2,1,0:T(8,128)}), f32[64,4,6,16,128]{4,3,2,1,0:T(8,128)}) %all-gather.2.cloned.1.call-update) | async-done | bytes 12582928 | tf_op jit(solution)/shard_map/all_gather | solution.py:820
  239.3 4.6 %copy-done = f32[64,4,6,16,128]{4,3,2,1,0:T(8,128)S(1)} copy-done((f32[64,4,6,16,128]{4,3,2,1,0:T(8,128)S(1)}, f32[64,4,6,16,128]{4,3,2,1,0:T(8,128)}, u32[]{:S(2)}) %copy-start) | copy-done | bytes 12582936
  243.9 0.7 outer.1
  244.6 0.0 collective-permute-start
  244.6 2.9 %collective-permute-start.1 = (f32[4,7,16,128]{3,2,1,0:T(8,128)S(1)}, f32[4,7,16,128]{3,2,1,0:T(8,128)S(1)}, u32[]{:S(2)}, u32[]{:S(2)}) collective-permute-start(f32[4,7,16,128]{3,2,1,0:T(8,128)S(1)} %get-tuple-element.21), channel_id=1, source_target_pairs={{16,0},{32,16},{48,32},{64,48},{80,64},{96,80},{112,96},{0,112},{1... | collective-permute-start | bytes 688136 | tf_op jit(solution)/shard_map/ppermute | solution.py:824
  247.5 3.7 %collective-permute-done.below_ref = f32[4,7,16,128]{3,2,1,0:T(8,128)S(1)} collective-permute-done((f32[4,7,16,128]{3,2,1,0:T(8,128)S(1)}, f32[4,7,16,128]{3,2,1,0:T(8,128)S(1)}, u32[]{:S(2)}, u32[]{:S(2)}) %collective-permute-start) | collective-permute-done | bytes 229408 | tf_op jit(solution)/shard_map/ppermute | solution.py:823
  251.3 13.7 %stream.1 = (f32[19,4,16,16,128]{4,3,2,1,0:T(8,128)}, f32[4,16,16,128]{3,2,1,0:T(8,128)}) custom-call(s32[80]{0:T(128)S(1)} %copy-done.15, f32[19,4,16,16,128]{4,3,2,1,0:T(8,128)S(1)} %copy-done.5, f32[3,4,16,16,128]{4,3,2,1,0:T(8,128)S(1)} %copy-done.11, f32[4,16,16,128]{3,2,1,0:T(8,128)S(1)} %copy-done.9, s32[4,18,18,128]{3,2,1,0:T(8,128)S(1)} %copy-done.3, ...), custom_call_target="tpu_custom_call" | custom-call | tf_op jit(solution)/shard_map/stream/pallas_call | solution.py:758
  (30 shorter events, 0.1 us)
Async XLA Ops:
  8.3 1.0 copy-start.7
  9.4 0.7 copy-start.16
  10.0 11.1 %copy-start.17 = (s32[4]{0:T(128)S(1)}, s32[4]{0:T(128)}, u32[]{:S(2)}) copy-start(s32[4]{0:T(128)} %ids_ref.1) | copy-start | bytes 52
  11.7 0.9 copy-start.1
  12.6 1.3 copy-start.6
  13.9 47.7 %all-to-all-start = ((f32[16,16,16,128]{3,2,1,0:T(8,128)}), f32[16,16,16,128]{3,2,1,0:T(8,128)S(1)}, u32[]{:S(2)}, u32[]{:S(2)}) async-start(f32[16,16,16,128]{3,2,1,0:T(8,128)} %copy-done.6), calls=%async_computation | async-start | bytes 4194304 | tf_op jit(solution)/shard_map/all_to_all | solution.py:811
  21.1 54.0 %copy-start.18 = (f32[4]{0:T(128)S(1)}, f32[4]{0:T(128)}, u32[]{:S(2)}) copy-start(f32[4]{0:T(128)} %permit_ref.1) | copy-start | bytes 52
  21.1 218.2 %all-gather.2.cloned.1.call-start = ((), (), s32[]{:S(2)}) async-start(), calls=%async_computation.2 | async-start | bytes 13369344 | tf_op jit(solution)/shard_map/all_gather | solution.py:820
  21.2 1.0 copy-start.13
  61.7 0.6 copy-start.14
  94.1 42.4 %copy-start.2 = (s32[4,18,18,128]{3,2,1,0:T(8,128)S(1)}, s32[4,18,18,128]{3,2,1,0:T(8,128)}, u32[]{:S(2)}) copy-start(s32[4,18,18,128]{3,2,1,0:T(8,128)} %copy-done.1) | copy-start | bytes 1990660
  94.1 42.4 %copy-start.8 = (f32[4,16,16,128]{3,2,1,0:T(8,128)S(1)}, f32[4,16,16,128]{3,2,1,0:T(8,128)}, u32[]{:S(2)}) copy-start(f32[4,16,16,128]{3,2,1,0:T(8,128)} %charge_ref.5) | copy-start | bytes 1572868
  94.1 42.4 %copy-start.15 = (s32[80]{0:T(128)S(1)}, s32[80]{0:T(128)}, u32[]{:S(2)}) copy-start(s32[80]{0:T(128)} %table.1.table_ref) | copy-start | bytes 964
  147.6 3.9 %copy-start.4 = (f32[19,4,16,16,128]{4,3,2,1,0:T(8,128)}, f32[19,4,16,16,128]{4,3,2,1,0:T(8,128)S(1)}, u32[]{:S(2)}) copy-start(f32[19,4,16,16,128]{4,3,2,1,0:T(8,128)S(1)} %get-tuple-element.17.relaxed_ref) | copy-start | bytes 29884420
  151.6 1.2 copy-start.10
  152.7 0.9 copy-start.12
  239.3 4.6 %copy-start = (f32[64,4,6,16,128]{4,3,2,1,0:T(8,128)S(1)}, f32[64,4,6,16,128]{4,3,2,1,0:T(8,128)}, u32[]{:S(2)}) copy-start(f32[64,4,6,16,128]{4,3,2,1,0:T(8,128)} %all-gather.2.cloned.1.call-done.up_ref.uplo_ref.uphi_ref.dn_ref.dnlo_ref.dnhi_ref.ylo_ref.yhi_ref.xin_ref.clo_ref.chi_ref) | copy-start | bytes 37748740
  243.9 7.4 %copy-start.3 = (s32[4,18,18,128]{3,2,1,0:T(8,128)S(1)}, s32[4,18,18,128]{3,2,1,0:T(8,128)}, u32[]{:S(2)}) copy-start(s32[4,18,18,128]{3,2,1,0:T(8,128)} %copy-done.1) | copy-start | bytes 1990660
  243.9 7.4 %copy-start.5 = (f32[19,4,16,16,128]{4,3,2,1,0:T(8,128)S(1)}, f32[19,4,16,16,128]{4,3,2,1,0:T(8,128)}, u32[]{:S(2)}) copy-start(f32[19,4,16,16,128]{4,3,2,1,0:T(8,128)} %copy-done.4) | copy-start | bytes 29884420
  243.9 7.4 %copy-start.9 = (f32[4,16,16,128]{3,2,1,0:T(8,128)S(1)}, f32[4,16,16,128]{3,2,1,0:T(8,128)}, u32[]{:S(2)}) copy-start(f32[4,16,16,128]{3,2,1,0:T(8,128)} %charge_ref.5) | copy-start | bytes 1572868
  243.9 7.4 %copy-start.11 = (f32[3,4,16,16,128]{4,3,2,1,0:T(8,128)S(1)}, f32[3,4,16,16,128]{4,3,2,1,0:T(8,128)}, u32[]{:S(2)}) copy-start(f32[3,4,16,16,128]{4,3,2,1,0:T(8,128)} %copy-done.10) | copy-start | bytes 4718596
  244.6 6.7 %collective-permute-start = (f32[4,7,16,128]{3,2,1,0:T(8,128)S(1)}, f32[4,7,16,128]{3,2,1,0:T(8,128)S(1)}, u32[]{:S(2)}, u32[]{:S(2)}) collective-permute-start(f32[4,7,16,128]{3,2,1,0:T(8,128)S(1)} %get-tuple-element.20), channel_id=1, source_target_pairs={{0,16},{16,32},{32,48},{48,64},{64,80},{80,96},{96,112},{112,0},{1... | collective-permute-start | bytes 688136 | tf_op jit(solution)/shard_map/ppermute | solution.py:823
  244.6 6.6 %collective-permute-start.1 = (f32[4,7,16,128]{3,2,1,0:T(8,128)S(1)}, f32[4,7,16,128]{3,2,1,0:T(8,128)S(1)}, u32[]{:S(2)}, u32[]{:S(2)}) collective-permute-start(f32[4,7,16,128]{3,2,1,0:T(8,128)S(1)} %get-tuple-element.21), channel_id=1, source_target_pairs={{16,0},{32,16},{48,32},{64,48},{80,64},{96,80},{112,96},{0,112},{1... | collective-permute-start | bytes 688136 | tf_op jit(solution)/shard_map/ppermute | solution.py:824
Sparse Core Ops, SparseCore 0:
  153.7 85.5 all-gather.1

commit v2 on v1

--- a/solution.py
+++ b/solution.py
@@ -49,22 +49,9 @@
 AROUND = tuple((dx, dy) for dx in (-1, 0, 1) for dy in (-1, 0, 1) if (dx, dy) != (0, 0))
 
 T_PEER = 0
-T_BACK = 4
-T_OWNER = 20
-T_YLO = 24
-T_YHI = 28
-T_XIN = 32
-T_CLO = 36
-T_CHI = 40
-T_ROW = 44
-T_UP = 48
-T_UPLO = 52
-T_UPHI = 56
-T_DN = 60
-T_DNLO = 64
-T_DNHI = 68
-T_FACE = 72
-T_SIZE = 80
+T_ROW = 4
+T_CORNER = 8
+T_SIZE = 24
 
 
 def opposite(direction):
@@ -107,69 +94,109 @@
     return copies
 
 
-def start_kernel(ids_ref, phase_ref, all_ref, ext_ref, send_sem, recv_sem, ids_send, ids_recv, own_sem):
+def start_kernel(
+    ids_ref,
+    phase_ref,
+    tiles_ref,
+    all_ref,
+    ext_ref,
+    arrived_ref,
+    send_sem,
+    recv_sem,
+    ids_send,
+    ids_recv,
+    tile_send,
+    tile_recv,
+    own_sem,
+):
+    me = lax.axis_index("gy")
     barrier = pltpu.get_barrier_semaphore()
-    targets = [shifted_id(0, k) for k in range(1, GROUPS)]
-    targets += [shifted_id(dx, dy) for dx, dy in AROUND if dx != 0]
+    peers = [shifted_id(0, k) for k in range(1, GROUPS)]
+    targets = peers + [shifted_id(dx, dy) for dx, dy in AROUND if dx != 0]
     for target in targets:
         pl.semaphore_signal(barrier, inc=1, device_id=target, device_id_type=MESH)
     pl.semaphore_wait(barrier, len(targets))
-    copies = []
-    for k in range(1, GROUPS):
-        copies.append((k, shifted_id(0, k)))
-    copies.append((GROUPS, shifted_id(-1, 0)))
-    copies.append((GROUPS + 1, shifted_id(1, 0)))
-    started = []
-    for k, target in copies:
+    early, late = [], []
+    for k, target in enumerate(peers):
         copy = pltpu.make_async_remote_copy(
             src_ref=ids_ref,
-            dst_ref=all_ref.at[k],
+            dst_ref=all_ref.at[0, me],
             send_sem=ids_send.at[k],
             recv_sem=ids_recv.at[k],
             device_id=target,
             device_id_type=MESH,
         )
         copy.start()
-        started.append(copy)
+        early.append(copy)
+    for k, target in enumerate(peers):
+        copy = pltpu.make_async_remote_copy(
+            src_ref=tiles_ref.at[target["gy"]],
+            dst_ref=arrived_ref.at[me],
+            send_sem=tile_send.at[k],
+            recv_sem=tile_recv.at[k],
+            device_id=target,
+            device_id_type=MESH,
+        )
+        copy.start()
+        late.append(copy)
     for copy in halo_copies(phase_ref, ext_ref, 5, send_sem, recv_sem):
         copy.start()
-        started.append(copy)
+        late.append(copy)
     own = [
-        pltpu.make_async_copy(ids_ref, all_ref.at[0], own_sem.at[0]),
+        pltpu.make_async_copy(ids_ref, all_ref.at[0, me], own_sem.at[0]),
         pltpu.make_async_copy(
             phase_ref, ext_ref.at[pl.ds(5, BLOCK), pl.ds(SIDE, BLOCK)], own_sem.at[1]
         ),
+        pltpu.make_async_copy(tiles_ref.at[me], arrived_ref.at[me], own_sem.at[2]),
     ]
     for copy in own:
         copy.start()
-    for copy in own:
+    own[0].wait()
+    for copy in early:
         copy.wait()
-    for copy in started:
+    for n, step in enumerate((1, -1)):
+        copy = pltpu.make_async_remote_copy(
+            src_ref=all_ref.at[0],
+            dst_ref=all_ref.at[1 + n],
+            send_sem=ids_send.at[GROUPS - 1 + n],
+            recv_sem=ids_recv.at[GROUPS - 1 + n],
+            device_id=shifted_id(step, 0),
+            device_id_type=MESH,
+        )
+        copy.start()
+        late.append(copy)
+    own[1].wait()
+    own[2].wait()
+    for copy in late:
         copy.wait()
 
 
-def exchange_start(ids, phase):
+def exchange_start(ids, phase, tiles):
     vmem = pl.BlockSpec(memory_space=pltpu.VMEM)
+    dma = pltpu.SemaphoreType.DMA
     return pl.pallas_call(
         start_kernel,
         out_shape=(
-            jax.ShapeDtypeStruct((GROUPS + 2, 8, DEPTH), jnp.int32),
+            jax.ShapeDtypeStruct((3, GROUPS, 8, DEPTH), jnp.int32),
             jax.ShapeDtypeStruct((BLOCK + 10, BLOCK + 2 * SIDE, DEPTH), jnp.int32),
+            jax.ShapeDtypeStruct((GROUPS, EDGE, EDGE, DEPTH), jnp.float32),
         ),
-        in_specs=[vmem, vmem],
-        out_specs=(vmem, vmem),
+        in_specs=[vmem, vmem, vmem],
+        out_specs=(vmem, vmem, vmem),
         scratch_shapes=[
-            pltpu.SemaphoreType.DMA((8,)),
-            pltpu.SemaphoreType.DMA((8,)),
-            pltpu.SemaphoreType.DMA((GROUPS + 2,)),
-            pltpu.SemaphoreType.DMA((GROUPS + 2,)),
-            pltpu.SemaphoreType.DMA((2,)),
+            dma((8,)),
+            dma((8,)),
+            dma((GROUPS + 1,)),
+            dma((GROUPS + 1,)),
+            dma((GROUPS - 1,)),
+            dma((GROUPS - 1,)),
+            dma((3,)),
         ],
         compiler_params=pltpu.CompilerParams(
-            collective_id=0, has_side_effects=True, vmem_limit_bytes=8 << 20
+            collective_id=0, has_side_effects=True, vmem_limit_bytes=16 << 20
         ),
         name="start",
-    )(ids, phase)
+    )(ids, phase, tiles)
 
 
 def halo_kernel(block_ref, ext_ref, send_sem, recv_sem, own_sem):
@@ -211,39 +238,23 @@
 def table_kernel(me_ref, ids_ref, out_ref, row_of):
     me = me_ref[0]
 
-    def place(p, carry):
-        k = lax.rem(me - p + GROUPS, GROUPS)
-        for s in range(TILES):
-            row_of[ids_ref[k, s]] = p * TILES + s
+    def place(e, carry):
+        for band in range(3):
+            row_of[band * 2 * COLS + ids_ref[band, e]] = band * 2 * COLS + e
         return carry
 
-    lax.fori_loop(0, GROUPS, place, 0)
-    for p in range(GROUPS):
-        out_ref[T_BACK + p] = 0
+    lax.fori_loop(0, 2 * COLS, place, 0)
     for t in range(TILES):
-        slot = row_of[(t // 2) * COLS + me * 2 + t % 2]
-        peer = slot // TILES
-        out_ref[T_PEER + t] = peer
-        out_ref[T_BACK + peer] = t
+        out_ref[T_PEER + t] = row_of[(t // 2) * COLS + me * 2 + t % 2] // TILES
     for s in range(TILES):
-        own = ids_ref[0, s]
+        own = ids_ref[0, me * TILES + s]
         row, col = own // COLS, lax.rem(own, COLS)
         left, right = lax.rem(col + COLS - 1, COLS), lax.rem(col + 1, COLS)
-        other = (1 - row) * COLS
-        out_ref[T_OWNER + s] = col // 2
-        out_ref[T_YLO + s] = row_of[row * COLS + left]
-        out_ref[T_YHI + s] = row_of[row * COLS + right]
-        out_ref[T_XIN + s] = row_of[other + col]
-        out_ref[T_CLO + s] = row_of[other + left]
-        out_ref[T_CHI + s] = row_of[other + right]
+        low = jnp.where(row == 1, 0, 2 * COLS) + (1 - row) * COLS
+        high = jnp.where(row == 0, 0, 4 * COLS) + (1 - row) * COLS
         out_ref[T_ROW + s] = row
-        out_ref[T_FACE + s] = row
-        for slot, base, first in ((GROUPS, COLS, T_UP), (GROUPS + 1, 0, T_DN)):
-            col = lax.rem(ids_ref[slot, s], COLS)
-            left, right = lax.rem(col + COLS - 1, COLS), lax.rem(col + 1, COLS)
-            out_ref[first + s] = row_of[base + col]
-            out_ref[first + 4 + s] = row_of[base + left]
-            out_ref[first + 8 + s] = row_of[base + right]
+        for n, place_of in enumerate((low + left, low + right, high + left, high + right)):
+            out_ref[T_CORNER + n * TILES + s] = row_of[place_of]
 
 
 def make_table(me, ids):
@@ -253,9 +264,399 @@
         out_shape=jax.ShapeDtypeStruct((T_SIZE,), jnp.int32),
         in_specs=[smem, smem],
         out_specs=smem,
-        scratch_shapes=[pltpu.SMEM((2 * COLS,), jnp.int32)],
+        scratch_shapes=[pltpu.SMEM((6 * COLS,), jnp.int32)],
         name="table",
     )(me, ids)
+
+
+K_FIRST, K_X2, K_X3, K_X4, K_Y2, K_Y3, K_Y4, K_LAST = range(8)
+PERMS = 6
+PORTS = 64
+
+
+def to_column(row, eye):
+    return jnp.sum(jnp.where(eye, row, 0), axis=1, keepdims=True)
+
+
+def split_edges(left, right, sub, lane):
+    def partners(ends):
+        same = ends[0] == ends[1]
+        before = jnp.where(same & (lane < sub), 1, 0)
+        after = jnp.where(same & (sub < lane), 1, 0)
+        rank_c = jnp.sum(before, axis=1, keepdims=True)
+        rank_r = jnp.sum(after, axis=0, keepdims=True)
+        pair = same & ((rank_c >> 1) == (rank_r >> 1)) & (sub != lane)
+        return jnp.where(pair, 1.0, 0.0).astype(jnp.bfloat16)
+
+    def times(a, b):
+        return jnp.dot(a, b, preferred_element_type=jnp.float32)
+
+    by_left, by_right = partners(left), partners(right)
+    reach = jnp.where(sub == lane, 1.0, times(by_left, by_right)).astype(jnp.bfloat16)
+    for _ in range(5):
+        reach = jnp.where(times(reach, reach) > 0.0, 1.0, 0.0).astype(jnp.bfloat16)
+    mate = times(by_left, reach)
+    own = reach.astype(jnp.float32) > 0.0
+    mate = mate > 0.0
+    size = sub.shape[0]
+    col = jnp.where(
+        jnp.min(jnp.where(own, lane, size), axis=1, keepdims=True)
+        > jnp.min(jnp.where(mate, lane, size), axis=1, keepdims=True),
+        1,
+        0,
+    )
+    row = jnp.where(
+        jnp.min(jnp.where(own, sub, size), axis=0, keepdims=True)
+        > jnp.min(jnp.where(mate, sub, size), axis=0, keepdims=True),
+        1,
+        0,
+    )
+    return col, row
+
+
+def join(first, second, base):
+    return tuple(a * base + b for a, b in zip(first, second))
+
+
+def colour(left, right, sub, lane):
+    high = split_edges(left, right, sub, lane)
+    low = split_edges(join(left, high, 2), join(right, high, 2), sub, lane)
+    return join(high, low, 2)
+
+
+def routing_tables(me, ids, store):
+    size = 2 * PORTS
+    sub = lax.broadcasted_iota(jnp.int32, (size, size), 0)
+    lane = lax.broadcasted_iota(jnp.int32, (size, size), 1)
+    eye = sub == lane
+    edge = (
+        lax.broadcasted_iota(jnp.int32, (size, 1), 0),
+        lax.broadcasted_iota(jnp.int32, (1, size), 1),
+    )
+    port = tuple(e & (PORTS - 1) for e in edge)
+    half = tuple(e >> 6 for e in edge)
+    device = tuple(e >> 2 for e in port)
+    owner = (port[1] & 3) // 2 * COLS + device[1] * 2 + (port[1] & 1)
+    own, below, above = (ids[n : n + 1] for n in range(3))
+
+    def turn(pos, step):
+        return (pos & COLS) + ((pos + step) & (COLS - 1))
+
+    def both(first, second):
+        return jnp.where(half[1] == 0, first, pltpu.roll(second, PORTS, 1))
+
+    twice = both(own, own)
+    at = to_column(twice, eye) + half[0] * PORTS
+    my_row, my_col = me >> 2, me & 3
+    entry = lax.broadcasted_iota(jnp.int32, (size, size), 1)
+    for pair, target in enumerate(
+        (
+            both(owner, turn(own, 1)),
+            both(turn(own, COLS - 1), own ^ COLS),
+            both(below ^ COLS, above ^ COLS),
+        )
+    ):
+        target = target + half[1] * PORTS
+        drop = jnp.sum(jnp.where(at == target, sub & (PORTS - 1), 0), axis=0, keepdims=True)
+        drop = (to_column(drop, eye), drop)
+        goal = tuple(d >> 2 for d in drop)
+        begin = tuple(h * GROUPS + d for h, d in zip(half, device))
+        end = tuple(h * GROUPS + d for h, d in zip(half, goal))
+        j = colour(begin, end, sub, lane)
+        group = tuple(h * 4 + c for h, c in zip(half, j))
+        src_row, src_col = (tuple(d >> 2 for d in device), tuple(d & 3 for d in device))
+        dst_row, dst_col = (tuple(d >> 2 for d in goal), tuple(d & 3 for d in goal))
+        b = colour(join(group, src_row, 4), join(group, dst_row, 4), sub, lane)
+        g = colour(join(group, src_col, 4), join(group, dst_col, 4), sub, lane)
+        for h in range(2):
+            mine = half[0] == h
+            for kind, given, key, value in (
+                (K_FIRST, device[0] == me, j, port[0] & 3),
+                (K_X2, (src_row[0] == my_row) & (j[0] == my_col), b, src_col[0]),
+                (K_X3, (j[0] == my_col) & (b[0] == my_row), dst_row, src_row[0]),
+                (K_X4, (j[0] == my_col) & (dst_row[0] == my_row), dst_col, b[0]),
+                (K_Y2, (src_col[0] == my_col) & (j[0] == my_row), g, src_row[0]),
+                (K_Y3, (j[0] == my_row) & (g[0] == my_col), dst_col, src_col[0]),
+                (K_Y4, (j[0] == my_row) & (dst_col[0] == my_col), dst_row, g[0]),
+                (K_LAST, goal[0] == me, (drop[0] & 3,), j[0]),
+            ):
+                kept = jnp.where(mine & given, value, 0)
+                found = jnp.where(key[0] == entry, kept, 0)
+                store((2 * pair + h) * 8 + kind, jnp.sum(found, axis=0, keepdims=True))
+
+
+def routing_kernel(me_ref, ids_ref, out_ref):
+    def store(place, row):
+        out_ref[pl.ds(place, 1)] = row
+
+    routing_tables(me_ref[0], ids_ref[...], store)
+
+
+def make_routes(me, ids):
+    vmem = pl.BlockSpec(memory_space=pltpu.VMEM)
+    return pl.pallas_call(
+        routing_kernel,
+        out_shape=jax.ShapeDtypeStruct((8 * PERMS, DEPTH), jnp.int32),
+        in_specs=[pl.BlockSpec(memory_space=pltpu.SMEM), vmem],
+        out_specs=vmem,
+        compiler_params=pltpu.CompilerParams(vmem_limit_bytes=8 << 20),
+        name="routes",
+    )(me, ids)
+
+
+def ring(axis, step):
+    gy = lax.axis_index("gy")
+    row, col = gy // 4, lax.rem(gy, 4)
+    if axis == 0:
+        place = lax.rem(col + step, 4)
+        return col, place, {"gx": lax.axis_index("gx"), "gy": row * 4 + place}
+    place = lax.rem(row + step, 4)
+    return row, place, {"gx": lax.axis_index("gx"), "gy": place * 4 + col}
+
+
+RING_AXES = ((0, 1, 1, 0), (1, 0, 0, 1))
+RING_KINDS = ((K_FIRST, K_X2, K_X3, K_X4), (K_FIRST, K_Y2, K_Y3, K_Y4))
+
+
+def exchange(order, stage, perms, first, table_ref, before, bufs, sems, sent):
+    send, recv = bufs
+    send_sem, recv_sem = sems
+    started = []
+    for step in (2, 1, 3, 0):
+        here, place, target = ring(RING_AXES[order][stage], step)
+        for n, perm in enumerate(perms):
+            slot = table_ref[perm * 8 + RING_KINDS[order][stage], place]
+            value = before(order, first + n, slot)
+            if step:
+                send[step - 1, first + n] = value
+            else:
+                recv[here, first + n] = value
+        if step:
+            items = pl.ds(first, len(perms))
+            copy = pltpu.make_async_remote_copy(
+                src_ref=send.at[step - 1, items],
+                dst_ref=recv.at[here, items],
+                send_sem=send_sem.at[order, step - 1],
+                recv_sem=recv_sem.at[order, step - 1],
+                device_id=target,
+                device_id_type=MESH,
+            )
+            copy.start()
+            started.append(copy)
+            sent.append(copy)
+    return started
+
+
+def greet(targets):
+    barrier = pltpu.get_barrier_semaphore()
+    for target in targets:
+        pl.semaphore_signal(barrier, inc=1, device_id=target, device_id_type=MESH)
+    pl.semaphore_wait(barrier, len(targets))
+
+
+def back_kernel(table_ref, items_ref, outx_ref, outy_ref, *scratch):
+    greet([ring(axis, step)[2] for axis in range(2) for step in (1, 2, 3)])
+    buffers, semaphores = scratch[:16], scratch[16:]
+    half = PACK // 2
+    sent = []
+
+    def first(order, n, slot):
+        return items_ref[slot, order * half : (order + 1) * half]
+
+    waiting = [None, None]
+    for stage in range(4):
+        sems = semaphores[2 * stage : 2 * stage + 2]
+        for order in range(2):
+            bufs = ring_buffers(buffers, stage, order)
+            if stage:
+                for copy in waiting[order]:
+                    copy.wait_recv()
+                before = reader(buffers, stage - 1)
+            else:
+                before = first
+            waiting[order] = exchange(order, stage, (0,), 0, table_ref, before, bufs, sems, sent)
+    for order, out in ((0, outx_ref), (1, outy_ref)):
+        for copy in waiting[order]:
+            copy.wait_recv()
+        final = ring_buffers(buffers, 3, order)[1]
+        for slot in range(4):
+            out[slot] = final[slot, 0]
+    for copy in sent:
+        copy.wait_send()
+
+
+def ring_scratch(items, shape):
+    scratch = []
+    for _ in range(8):
+        scratch.append(pltpu.VMEM((3, items) + shape, jnp.float32))
+        scratch.append(pltpu.VMEM((4, items) + shape, jnp.float32))
+    return scratch
+
+
+def ring_buffers(buffers, stage, order):
+    place = 4 * stage + 2 * order
+    return buffers[place : place + 2]
+
+
+def reader(buffers, stage):
+    def before(order, n, slot):
+        return ring_buffers(buffers, stage, order)[1][slot, n]
+
+    return before
+
+
+def send_back(routes, packed):
+    vmem = pl.BlockSpec(memory_space=pltpu.VMEM)
+    half = (PACK // 2, EDGE, DEPTH)
+    shape = jax.ShapeDtypeStruct((TILES,) + half, jnp.float32)
+    return pl.pallas_call(
+        back_kernel,
+        out_shape=(shape, shape),
+        in_specs=[pl.BlockSpec(memory_space=pltpu.SMEM), vmem],
+        out_specs=(vmem, vmem),
+        scratch_shapes=ring_scratch(1, half) + [pltpu.SemaphoreType.DMA((2, 3))] * 8,
+        compiler_params=pltpu.CompilerParams(
+            collective_id=2, has_side_effects=True, vmem_limit_bytes=32 << 20
+        ),
+        name="back",
+    )(routes, packed)
+
+
+FACES = 5
+
+
+def faces_kernel(
+    table_ref,
+    faces_ref,
+    corners_ref,
+    outx_ref,
+    outy_ref,
+    all_ref,
+    shifted,
+    corner_send,
+    corner_recv,
+    shift_send,
+    shift_recv,
+    late_send,
+    late_recv,
+    own_sem,
+    *scratch,
+):
+    me = lax.axis_index("gy")
+    peers = [shifted_id(0, k) for k in range(1, GROUPS)]
+    bands = [shifted_id(1, 0), shifted_id(-1, 0)]
+    greet(peers + bands)
+    buffers, semaphores = scratch[:16], scratch[16:]
+    sent = []
+    shifts = []
+    for n, target in enumerate(bands):
+        copy = pltpu.make_async_remote_copy(
+            src_ref=faces_ref.at[:, 3 + n],
+            dst_ref=shifted.at[n],
+            send_sem=shift_send.at[n],
+            recv_sem=shift_recv.at[n],
+            device_id=target,
+            device_id_type=MESH,
+        )
+        copy.start()
+        shifts.append(copy)
+
+    def first(order, n, slot):
+        if n < 3:
+            return faces_ref[slot, n, order * 3 : order * 3 + 3]
+        return shifted[n - 3, slot, order * 3 : order * 3 + 3]
+
+    waiting = [[], []]
+    for order in range(2):
+        waiting[order] += exchange(
+            order, 0, (1, 2, 3), 0, table_ref, first, ring_buffers(buffers, 0, order), semaphores[:2], sent
+        )
+    spread_out = []
+    for k, target in enumerate(peers):
+        copy = pltpu.make_async_remote_copy(
+            src_ref=corners_ref,
+            dst_ref=all_ref.at[0, me],
+            send_sem=corner_send.at[k],
+            recv_sem=corner_recv.at[k],
+            device_id=target,
+            device_id_type=MESH,
+        )
+        copy.start()
+        spread_out.append(copy)
+    own = pltpu.make_async_copy(corners_ref, all_ref.at[0, me], own_sem)
+    own.start()
+    for copy in shifts:
+        copy.wait_recv()
+    late = (late_send, late_recv)
+    for order in range(2):
+        waiting[order] += exchange(
+            order, 0, (4, 5), 3, table_ref, first, ring_buffers(buffers, 0, order), late, sent
+        )
+    forward = []
+    for stage in range(1, 4):
+        sems = semaphores[2 * stage : 2 * stage + 2]
+        before = reader(buffers, stage - 1)
+        for order in range(2):
+            bufs = ring_buffers(buffers, stage, order)
+            for copy in waiting[order]:
+                copy.wait_recv()
+            waiting[order] = exchange(
+                order, stage, (1, 2, 3, 4, 5), 0, table_ref, before, bufs, sems, sent
+            )
+        if stage == 1:
+            own.wait()
+            for copy in spread_out:
+                copy.wait_recv()
+            for n, target in enumerate(bands):
+                copy = pltpu.make_async_remote_copy(
+                    src_ref=all_ref.at[0],
+                    dst_ref=all_ref.at[1 + n],
+                    send_sem=corner_send.at[GROUPS - 1 + n],
+                    recv_sem=corner_recv.at[GROUPS - 1 + n],
+                    device_id=target,
+                    device_id_type=MESH,
+                )
+                copy.start()
+                forward.append(copy)
+    for order, out in ((0, outx_ref), (1, outy_ref)):
+        for copy in waiting[order]:
+            copy.wait_recv()
+        final = ring_buffers(buffers, 3, order)[1]
+        for slot in range(4):
+            out[slot] = final[slot]
+    for copy in forward:
+        copy.wait_recv()
+    for copy in shifts + spread_out + forward + sent:
+        copy.wait_send()
+
+
+def send_faces(routes, faces, corners):
+    vmem = pl.BlockSpec(memory_space=pltpu.VMEM)
+    f32 = jnp.float32
+    dma = pltpu.SemaphoreType.DMA
+    shape = jax.ShapeDtypeStruct((TILES, FACES, 3, EDGE, DEPTH), f32)
+    return pl.pallas_call(
+        faces_kernel,
+        out_shape=(shape, shape, jax.ShapeDtypeStruct((3, GROUPS, 2, 8, DEPTH), f32)),
+        in_specs=[pl.BlockSpec(memory_space=pltpu.SMEM), vmem, vmem],
+        out_specs=(vmem, vmem, vmem),
+        scratch_shapes=[
+            pltpu.VMEM((2, TILES, 6, EDGE, DEPTH), f32),
+            dma((GROUPS + 1,)),
+            dma((GROUPS + 1,)),
+            dma((2,)),
+            dma((2,)),
+            dma((2, 3)),
+            dma((2, 3)),
+            dma,
+        ]
+        + ring_scratch(FACES, (3, EDGE, DEPTH))
+        + [dma((2, 3))] * 8,
+        compiler_params=pltpu.CompilerParams(
+            collective_id=3, has_side_effects=True, vmem_limit_bytes=24 << 20
+        ),
+        name="faces",
+    )(routes, faces, corners)
 
 
 def spread_kernel(ids_ref, charge_ref, mask_ref, out_ref, masked):
@@ -328,7 +729,7 @@
 
 
 def solve_kernel(
-    table_ref, permit_ref, phase_ref, source_ref, pot_ref, send_ref, permit, coef, resid, upd_a, upd_b, total, pack
+    permit_ref, phase_ref, source_ref, pot_ref, pack, permit, coef, resid, upd_a, upd_b, total
 ):
     center = 0.5 * (spectrum_high + spectrum_low)
     half = 0.5 * (spectrum_high - spectrum_low)
@@ -406,14 +807,8 @@
             pack[t, place] = ref[i0 - 1, pl.ds(j0, EDGE)]
             pack[t, place + 1] = ref[i0 + EDGE, pl.ds(j0, EDGE)]
 
-    def send(p, carry):
-        send_ref[p] = pack[table_ref[T_BACK + p]]
-        return carry
-
-    lax.fori_loop(0, GROUPS, send, 0)
-
-
-def solve(table, permittivity, phase, source):
+
+def solve(permittivity, phase, source):
     vmem = pl.BlockSpec(memory_space=pltpu.VMEM)
     smem = pl.BlockSpec(memory_space=pltpu.SMEM)
     f32 = jnp.float32
@@ -421,9 +816,9 @@
         solve_kernel,
         out_shape=(
             jax.ShapeDtypeStruct((BLOCK, BLOCK, DEPTH), f32),
-            jax.ShapeDtypeStruct((GROUPS, PACK, EDGE, DEPTH), f32),
+            jax.ShapeDtypeStruct((TILES, PACK, EDGE, DEPTH), f32),
         ),
-        in_specs=[smem, smem, vmem, vmem],
+        in_specs=[smem, vmem, vmem],
         out_specs=(vmem, vmem),
         scratch_shapes=[
             pltpu.VMEM((TALL + 2, WIDE, DEPTH), f32),
@@ -432,11 +827,10 @@
             pltpu.VMEM((TALL, ROOM, DEPTH), f32),
             pltpu.VMEM((TALL, ROOM, DEPTH), f32),
             pltpu.VMEM((TALL, WIDE, DEPTH), f32),
-            pltpu.VMEM((TILES, PACK, EDGE, DEPTH), f32),
         ],
         compiler_params=pltpu.CompilerParams(vmem_limit_bytes=32 << 20),
         name="solve",
-    )(table, permittivity, phase, source)
+    )(permittivity, phase, source)
 
 
 def collide_rows(pops, charge, field):
@@ -488,16 +882,28 @@
     return result, velocity
 
 
-def collide_kernel(table_ref, pops_ref, charge_ref, mask_ref, pot_ref, out_ref, vel_ref, face_ref, grown):
-    def place(i, carry):
-        grown[i + 1, pl.ds(8, EDGE)] = pot_ref[0, i]
-        grown[i + 1, pl.ds(7, 1)] = pot_ref[0, EDGE + 2, pl.ds(i, 1)]
-        grown[i + 1, pl.ds(8 + EDGE, 1)] = pot_ref[0, EDGE + 3, pl.ds(i, 1)]
+def collide_kernel(
+    table_ref, routes_ref, pops_ref, charge_ref, mask_ref, potx_ref, poty_ref, out_ref, vel_ref, face_ref, corner_ref, grown
+):
+    half = PACK // 2
+    tile = pl.program_id(0)
+
+    for ref, first, count in ((potx_ref, 0, half), (poty_ref, half, EDGE - half)):
+
+        def place(i, carry, ref=ref, first=first):
+            grown[first + i + 1, pl.ds(8, EDGE)] = ref[0, i]
+            return carry
+
+        lax.fori_loop(0, count, place, 0)
+
+    def sides(i, carry):
+        grown[i + 1, pl.ds(7, 1)] = poty_ref[0, EDGE + 2 - half, pl.ds(i, 1)]
+        grown[i + 1, pl.ds(8 + EDGE, 1)] = poty_ref[0, EDGE + 3 - half, pl.ds(i, 1)]
         return carry
 
-    lax.fori_loop(0, EDGE, place, 0)
-    grown[0, pl.ds(8, EDGE)] = pot_ref[0, EDGE]
-    grown[EDGE + 1, pl.ds(8, EDGE)] = pot_ref[0, EDGE + 1]
+    lax.fori_loop(0, EDGE, sides, 0)
+    grown[0, pl.ds(8, EDGE)] = poty_ref[0, EDGE - half]
+    grown[EDGE + 1, pl.ds(8, EDGE)] = poty_ref[0, EDGE + 1 - half]
     y_low, y_high = crossing(1, -1), crossing(1, 1)
 
     def rows(i, carry):
@@ -514,136 +920,113 @@
             value = jnp.where(fluid, relaxed[q], pops[q])
             out_ref[q, 0, i] = value
             if q in y_low:
-                face_ref[0, 2, y_low.index(q), pl.ds(i, 1)] = value[0:1]
+                face_ref[0, 1, y_low.index(q), pl.ds(i, 1)] = value[0:1]
             if q in y_high:
-                face_ref[0, 3, y_high.index(q), pl.ds(i, 1)] = value[EDGE - 1 :]
+                face_ref[0, 0, y_high.index(q), pl.ds(i, 1)] = value[EDGE - 1 :]
         for d in range(3):
             vel_ref[d, 0, i] = velocity[d]
-        face_ref[0, 2, 5, pl.ds(i, 1)] = velocity[1][0:1]
-        face_ref[0, 3, 5, pl.ds(i, 1)] = velocity[1][EDGE - 1 :]
+        face_ref[0, 1, 5, pl.ds(i, 1)] = velocity[1][0:1]
+        face_ref[0, 0, 5, pl.ds(i, 1)] = velocity[1][EDGE - 1 :]
         return carry
 
     lax.fori_loop(0, EDGE, rows, 0)
-    for face, sign, layer in ((0, -1, 0), (1, 1, EDGE - 1)):
+
+    def x_face(face, sign, layer):
         for k, q in enumerate(crossing(0, sign)):
             face_ref[0, face, k] = out_ref[q, 0, layer]
         face_ref[0, face, 5] = vel_ref[0, 0, layer]
 
-
-def collide(table, populations, charge, fluid_mask, returned):
+    x_face(3, 1, EDGE - 1)
+    x_face(4, -1, 0)
+
+    @pl.when(table_ref[T_ROW + tile] == 0)
+    def _():
+        x_face(2, 1, EDGE - 1)
+
+    @pl.when(table_ref[T_ROW + tile] == 1)
+    def _():
+        x_face(2, -1, 0)
+
+    for n, (q, i, j) in enumerate(
+        ((7, EDGE - 1, EDGE - 1), (9, EDGE - 1, 0), (10, 0, EDGE - 1), (8, 0, 0))
+    ):
+        corner_ref[tile // 2, pl.ds(lax.rem(tile, 2) * 4 + n, 1)] = out_ref[q, 0, i, pl.ds(j, 1)]
+
+
+def collide(table, routes, populations, charge, fluid_mask, potx, poty):
     f32 = jnp.float32
+    pot_spec = pl.BlockSpec(
+        (1, PACK // 2, EDGE, DEPTH), lambda s, tab, rts: (rts[K_LAST, s], 0, 0, 0)
+    )
     return pl.pallas_call(
         collide_kernel,
         out_shape=(
             jax.ShapeDtypeStruct((19, TILES, EDGE, EDGE, DEPTH), f32),
             jax.ShapeDtypeStruct((3, TILES, EDGE, EDGE, DEPTH), f32),
-            jax.ShapeDtypeStruct((TILES, 4, 6, EDGE, DEPTH), f32),
+            jax.ShapeDtypeStruct((TILES, FACES, 6, EDGE, DEPTH), f32),
+            jax.ShapeDtypeStruct((2, 8, DEPTH), f32),
         ),
         grid_spec=pltpu.PrefetchScalarGridSpec(
-            num_scalar_prefetch=1,
+            num_scalar_prefetch=2,
             grid=(TILES,),
             in_specs=[
-                pl.BlockSpec((19, 1, EDGE, EDGE, DEPTH), lambda s, tab: (0, s, 0, 0, 0)),
-                pl.BlockSpec((1, EDGE, EDGE, DEPTH), lambda s, tab: (s, 0, 0, 0)),
-                pl.BlockSpec((1, EDGE + 2, EDGE + 2, DEPTH), lambda s, tab: (s, 0, 0, 0)),
-                pl.BlockSpec((1, PACK, EDGE, DEPTH), lambda s, tab: (tab[T_OWNER + s], 0, 0, 0)),
+                pl.BlockSpec((19, 1, EDGE, EDGE, DEPTH), lambda s, tab, rts: (0, s, 0, 0, 0)),
+                pl.BlockSpec((1, EDGE, EDGE, DEPTH), lambda s, tab, rts: (s, 0, 0, 0)),
+                pl.BlockSpec((1, EDGE + 2, EDGE + 2, DEPTH), lambda s, tab, rts: (s, 0, 0, 0)),
+                pot_spec,
+                pot_spec,
             ],
             out_specs=[
-                pl.BlockSpec((19, 1, EDGE, EDGE, DEPTH), lambda s, tab: (0, s, 0, 0, 0)),
-                pl.BlockSpec((3, 1, EDGE, EDGE, DEPTH), lambda s, tab: (0, s, 0, 0, 0)),
-                pl.BlockSpec((1, 4, 6, EDGE, DEPTH), lambda s, tab: (s, 0, 0, 0, 0)),
+                pl.BlockSpec((19, 1, EDGE, EDGE, DEPTH), lambda s, tab, rts: (0, s, 0, 0, 0)),
+                pl.BlockSpec((3, 1, EDGE, EDGE, DEPTH), lambda s, tab, rts: (0, s, 0, 0, 0)),
+                pl.BlockSpec((1, FACES, 6, EDGE, DEPTH), lambda s, tab, rts: (s, 0, 0, 0, 0)),
+                pl.BlockSpec((2, 8, DEPTH), lambda s, tab, rts: (0, 0, 0)),
             ],
             scratch_shapes=[pltpu.VMEM((EDGE + 2, 32, DEPTH), f32)],
         ),
         compiler_params=pltpu.CompilerParams(vmem_limit_bytes=32 << 20),
         name="collide",
-    )(table, populations, charge, fluid_mask, returned)
-
-
-def outer_kernel(table_ref, up_ref, uplo_ref, uphi_ref, dn_ref, dnlo_ref, dnhi_ref, to_up, to_dn):
-    plus, minus = crossing(0, 1), crossing(0, -1)
-    for out, face, low, high, low_q, high_q in (
-        (to_up, up_ref, uplo_ref, uphi_ref, plus.index(7), plus.index(9)),
-        (to_dn, dn_ref, dnlo_ref, dnhi_ref, minus.index(10), minus.index(8)),
-    ):
-        for k in range(6):
-            out[0, k] = face[0, 0, k]
-        out[0, 6, pl.ds(0, 1)] = low[0, 0, low_q, pl.ds(EDGE - 1, 1)]
-        out[0, 6, pl.ds(1, 1)] = high[0, 0, high_q, pl.ds(0, 1)]
-
-
-def outer(table, gathered):
-    def face(place, side):
-        return pl.BlockSpec(
-            (1, 1, 6, EDGE, DEPTH), lambda s, tab: (tab[place + s], side, 0, 0, 0)
-        )
-
-    shape = jax.ShapeDtypeStruct((TILES, 7, EDGE, DEPTH), jnp.float32)
-    spec = pl.BlockSpec((1, 7, EDGE, DEPTH), lambda s, tab: (s, 0, 0, 0))
-    return pl.pallas_call(
-        outer_kernel,
-        out_shape=(shape, shape),
-        grid_spec=pltpu.PrefetchScalarGridSpec(
-            num_scalar_prefetch=1,
-            grid=(TILES,),
-            in_specs=[
-                face(T_UP, 1),
-                face(T_UPLO, 1),
-                face(T_UPHI, 1),
-                face(T_DN, 0),
-                face(T_DNLO, 0),
-                face(T_DNHI, 0),
-            ],
-            out_specs=[spec, spec],
-        ),
-        compiler_params=pltpu.CompilerParams(vmem_limit_bytes=8 << 20),
-        name="outer",
-    )(table, *([gathered] * 6))
+    )(table, routes, populations, charge, fluid_mask, potx, poty)
 
 
 def stream_kernel(
     table_ref,
+    routes_ref,
     relaxed_ref,
     vel_ref,
     charge_ref,
     mask_ref,
     rim_ref,
-    ylo_ref,
-    yhi_ref,
-    xin_ref,
-    clo_ref,
-    chi_ref,
-    below_ref,
-    above_ref,
-    pops_out,
-    charge_out,
-    xrim,
-    corner,
+    *rest,
 ):
-    row = table_ref[T_ROW + pl.program_id(0)]
+    halves, (corner_ref, pops_out, charge_out, xrim, yrim, corner) = rest[:10], rest[10:]
+    tile = pl.program_id(0)
+    row = table_ref[T_ROW + tile]
     plus = [crossing(0, 1), crossing(1, 1)]
     minus = [crossing(0, -1), crossing(1, -1)]
 
-    def inside(side, low_q, high_q):
+    def fill(out, face):
         for k in range(6):
-            xrim[side, k] = xin_ref[0, 0, k]
-        corner[side, pl.ds(0, 1)] = clo_ref[0, 0, low_q, pl.ds(EDGE - 1, 1)]
-        corner[side, pl.ds(1, 1)] = chi_ref[0, 0, high_q, pl.ds(0, 1)]
-
-    def outside(side, ref):
-        for k in range(6):
-            xrim[side, k] = ref[0, k]
-        corner[side, pl.ds(0, 2)] = ref[0, 6, pl.ds(0, 2)]
+            out[k] = halves[2 * face + k // 3][0, 0, k % 3]
+
+    fill(yrim.at[0], 0)
+    fill(yrim.at[1], 1)
+    for n, (side, end, which) in enumerate(((0, 0, 0), (0, 1, 1), (1, 0, 2), (1, 1, 3))):
+        found = table_ref[T_CORNER + n * TILES + tile]
+        tile_in = lax.rem(found, TILES)
+        corner[side, pl.ds(end, 1)] = corner_ref[
+            found // TILES, tile_in // 2, pl.ds(lax.rem(tile_in, 2) * 4 + which, 1)
+        ]
 
     @pl.when(row == 0)
     def _():
-        outside(0, below_ref)
-        inside(1, minus[0].index(10), minus[0].index(8))
+        fill(xrim.at[0], 3)
+        fill(xrim.at[1], 2)
 
     @pl.when(row == 1)
     def _():
-        inside(0, plus[0].index(7), plus[0].index(9))
-        outside(1, above_ref)
+        fill(xrim.at[0], 2)
+        fill(xrim.at[1], 4)
 
     place = lax.broadcasted_iota(jnp.int32, (EDGE, DEPTH), 0)
     first, last = place == 0, place == EDGE - 1
@@ -668,13 +1051,13 @@
                 moved = xrim[side, channel]
             if step_y == 1:
                 if side is None:
-                    edge = ylo_ref[0, 0, plus[1].index(q), pl.ds(i - step_x, 1)]
+                    edge = yrim[0, plus[1].index(q), pl.ds(i - step_x, 1)]
                 else:
                     edge = corner[side, pl.ds(0, 1)]
                 moved = jnp.where(first, edge, pltpu.roll(moved, 1, 0))
             elif step_y == -1:
                 if side is None:
-                    edge = yhi_ref[0, 0, minus[1].index(q), pl.ds(i - step_x, 1)]
+                    edge = yrim[1, minus[1].index(q), pl.ds(i - step_x, 1)]
                 else:
                     edge = corner[side, pl.ds(1, 1)]
                 moved = jnp.where(last, edge, pltpu.roll(moved, EDGE - 1, 0))
@@ -709,12 +1092,12 @@
 
         speed = vel_ref[1, 0, i]
         other = jnp.where(first, rim_ref[0, 2, pl.ds(i, 1)], pltpu.roll(charge, 1, 0))
-        other_speed = jnp.where(first, ylo_ref[0, 0, 5, pl.ds(i, 1)], pltpu.roll(speed, 1, 0))
+        other_speed = jnp.where(first, yrim[0, 5, pl.ds(i, 1)], pltpu.roll(speed, 1, 0))
         other_flag = mask_ref[0, i + 1, pl.ds(0, EDGE), :].astype(jnp.float32)
         change -= flux(other_speed, speed, other, charge, other_flag * flag)
         other = jnp.where(last, rim_ref[0, 3, pl.ds(i, 1)], pltpu.roll(charge, EDGE - 1, 0))
         other_speed = jnp.where(
-            last, yhi_ref[0, 0, 5, pl.ds(i, 1)], pltpu.roll(speed, EDGE - 1, 0)
+            last, yrim[1, 5, pl.ds(i, 1)], pltpu.roll(speed, EDGE - 1, 0)
         )
         other_flag = mask_ref[0, i + 1, pl.ds(2, EDGE), :].astype(jnp.float32)
         change += flux(speed, other_speed, charge, other, flag * other_flag)
@@ -740,21 +1123,16 @@
     rows(EDGE - 1, False, True)
 
 
-def stream(table, relaxed, velocity, charge, fluid_mask, returned, gathered, below, above):
+def stream(table, routes, relaxed, velocity, charge, fluid_mask, poty, facex, facey, corners):
     f32 = jnp.float32
-
-    def face(place, side):
-        return pl.BlockSpec(
-            (1, 1, 6, EDGE, DEPTH), lambda s, tab: (tab[place + s], side, 0, 0, 0)
+    face_specs = [
+        pl.BlockSpec(
+            (1, 1, 3, EDGE, DEPTH),
+            lambda s, tab, rts, face=face: (rts[(1 + face) * 8 + K_LAST, s], face, 0, 0, 0),
         )
-
-    def inner_face(place):
-        return pl.BlockSpec(
-            (1, 1, 6, EDGE, DEPTH),
-            lambda s, tab: (tab[place + s], tab[T_FACE + s], 0, 0, 0),
-        )
-
-    outer_spec = pl.BlockSpec((1, 7, EDGE, DEPTH), lambda s, tab: (s, 0, 0, 0))
+        for face in range(FACES)
+        for _ in range(2)
+    ]
     return pl.pallas_call(
         stream_kernel,
         out_shape=(
@@ -762,27 +1140,23 @@
             jax.ShapeDtypeStruct((TILES, EDGE, EDGE, DEPTH), f32),
         ),
         grid_spec=pltpu.PrefetchScalarGridSpec(
-            num_scalar_prefetch=1,
+            num_scalar_prefetch=2,
             grid=(TILES,),
             in_specs=[
-                pl.BlockSpec((19, 1, EDGE, EDGE, DEPTH), lambda s, tab: (0, s, 0, 0, 0)),
-                pl.BlockSpec((3, 1, EDGE, EDGE, DEPTH), lambda s, tab: (0, s, 0, 0, 0)),
-                pl.BlockSpec((1, EDGE, EDGE, DEPTH), lambda s, tab: (s, 0, 0, 0)),
-                pl.BlockSpec((1, EDGE + 2, EDGE + 2, DEPTH), lambda s, tab: (s, 0, 0, 0)),
-                pl.BlockSpec((1, 4, EDGE, DEPTH), lambda s, tab: (tab[T_OWNER + s], 5, 0, 0)),
-                face(T_YLO, 3),
-                face(T_YHI, 2),
-                inner_face(T_XIN),
-                inner_face(T_CLO),
-                inner_face(T_CHI),
-                outer_spec,
-                outer_spec,
-            ],
+                pl.BlockSpec((19, 1, EDGE, EDGE, DEPTH), lambda s, tab, rts: (0, s, 0, 0, 0)),
+                pl.BlockSpec((3, 1, EDGE, EDGE, DEPTH), lambda s, tab, rts: (0, s, 0, 0, 0)),
+                pl.BlockSpec((1, EDGE, EDGE, DEPTH), lambda s, tab, rts: (s, 0, 0, 0)),
+                pl.BlockSpec((1, EDGE + 2, EDGE + 2, DEPTH), lambda s, tab, rts: (s, 0, 0, 0)),
+                pl.BlockSpec((1, 4, EDGE, DEPTH), lambda s, tab, rts: (rts[K_LAST, s], 2, 0, 0)),
+            ]
+            + face_specs
+            + [pl.BlockSpec((3 * GROUPS, 2, 8, DEPTH), lambda s, tab, rts: (0, 0, 0, 0))],
             out_specs=[
-                pl.BlockSpec((19, 1, EDGE, EDGE, DEPTH), lambda s, tab: (0, s, 0, 0, 0)),
-                pl.BlockSpec((1, EDGE, EDGE, DEPTH), lambda s, tab: (s, 0, 0, 0)),
+                pl.BlockSpec((19, 1, EDGE, EDGE, DEPTH), lambda s, tab, rts: (0, s, 0, 0, 0)),
+                pl.BlockSpec((1, EDGE, EDGE, DEPTH), lambda s, tab, rts: (s, 0, 0, 0)),
             ],
             scratch_shapes=[
+                pltpu.VMEM((2, 6, EDGE, DEPTH), f32),
                 pltpu.VMEM((2, 6, EDGE, DEPTH), f32),
                 pltpu.VMEM((2, 8, DEPTH), f32),
             ],
@@ -791,39 +1165,35 @@
         name="stream",
     )(
         table,
+        routes,
         relaxed,
         velocity,
         charge,
         fluid_mask,
-        returned,
-        gathered,
-        gathered,
-        gathered,
-        gathered,
-        gathered,
-        below,
-        above,
+        poty,
+        *([facex, facey] * FACES),
+        corners.reshape(3 * GROUPS, 2, 8, DEPTH),
     )
 
 
 def per_device(populations, charge, fluid_mask, tile_ids, phase_label, permittivity):
     outgoing = spread(tile_ids, charge, fluid_mask)
-    arrived = lax.all_to_all(outgoing, "gy", split_axis=0, concat_axis=0, tiled=True)
-    ids_row = jnp.pad(tile_ids[None], ((0, 7), (0, DEPTH - TILES)))
-    ids_all, phase_ext = exchange_start(ids_row, phase_label)
     me = lax.axis_index("gy").astype(jnp.int32).reshape(1)
-    table = make_table(me, ids_all[:, 0, :TILES])
+    place = jnp.arange(8 * DEPTH, dtype=jnp.int32).reshape(8, DEPTH)
+    ids_row = jnp.where(place // TILES == me, jnp.tile(tile_ids, 2 * DEPTH).reshape(8, DEPTH), 0)
+    ids_all, phase_ext, arrived = exchange_start(ids_row, phase_label, outgoing)
+    ids = jnp.sum(ids_all[:, :, 0, :], axis=1)
+    table = make_table(me, ids)
+    routes = make_routes(me, ids)
     source_ext = exchange_halo(assemble(table, arrived))
-    potential, packed = solve(table, permittivity, phase_ext, source_ext)
-    returned = lax.all_to_all(packed, "gy", split_axis=0, concat_axis=0, tiled=True)
-    relaxed, velocity, faces = collide(table, populations, charge, fluid_mask, returned)
-    gathered = lax.all_gather(faces, "gy", axis=0, tiled=True)
-    to_up, to_dn = outer(table, gathered)
-    up = [(k, (k + 1) % BANDS) for k in range(BANDS)]
-    below = lax.ppermute(to_up, "gx", up)
-    above = lax.ppermute(to_dn, "gx", [(b, a) for a, b in up])
+    potential, packed = solve(permittivity, phase_ext, source_ext)
+    potx, poty = send_back(routes, packed)
+    relaxed, velocity, faces, corners = collide(
+        table, routes, populations, charge, fluid_mask, potx, poty
+    )
+    facex, facey, all_corners = send_faces(routes, faces, corners)
     populations_next, charge_next = stream(
-        table, relaxed, velocity, charge, fluid_mask, returned, gathered, below, above
+        table, routes, relaxed, velocity, charge, fluid_mask, poty, facex, facey, all_corners
     )
     return (populations_next, charge_next, potential)
 

time: 274 us -> 198 us (0.72)
  Pallas kernels: 97.5 us -> 187 us
  waiting for transfers between devices: 89.4 us -> 0 us
  blocking collectives: 42.4 us -> 0 us
  between operations: 14.2 us -> 0.81 us
  starting transfers between devices: 10.1 us -> 0 us
  local copies, waits for them, and re-layouts: 18.1 us -> 8.77 us
    pallas_call x2 -> x4, Pallas kernels: 37.6 us -> 126 us  [the longest x1 42.3 us: exchange_start(): pl.pallas_call(start_kernel, out_shape=(jax.ShapeDtypeStruct((3, GROUPS,...]
    all_gather x1 -> x0, waiting for transfers between devices: 85.7 us -> none  [per_device(): gathered = lax.all_gather(faces, 'gy', axis=0, tiled=True)]
    all_to_all x1 -> x0, blocking collectives: 42.4 us -> none  [per_device(): lax.all_to_all(packed, 'gy', split_axis=0, concat_axis=0, tiled=True)]
    unnamed x39 -> x21, local copies, waits for them, and re-layouts: 17.3 us -> 7.95 us
    all_to_all x1 -> x0, starting transfers between devices: 7.15 us -> none  [per_device(): lax.all_to_all(outgoing, 'gy', split_axis=0, concat_axis=0, tiled=True)]
    ppermute x2 -> x0, waiting for transfers between devices: 3.7 us -> none  [the longest x1 3.7 us: per_device(): below = lax.ppermute(to_up, 'gx', up)]
    ppermute x2 -> x0, starting transfers between devices: 2.96 us -> none  [the longest x1 2.94 us: per_device(): above = lax.ppermute(to_dn, 'gx', [(b, a) for a, b in up])]
  transfers between devices with their start and end apart: 4 -> 0, of which waited for: 2 -> 0; matrix products, arithmetic and copies ran while one was open for 0% -> 0% of each run, Pallas kernels for 14% -> 0%
where the time goes in v2:
time: 198 us; the launch traced here: 197 us
  Pallas kernels  187 us (94%)
  local copies, waits for them, and re-layouts  8.77 us (4%)
    pallas_call x1, Pallas kernels, exchange_start(): pl.pallas_call(start_kernel, out_shape=(jax.ShapeDtypeStruct((3, GROUPS,...  42.3 us
    pallas_call x1, Pallas kernels, send_faces(): pl.pallas_call(faces_kernel, out_shape=(shape, shape, jax.ShapeDtypeStruc...  36.2 us
    pallas_call x1, Pallas kernels, send_back(): pl.pallas_call(back_kernel, out_shape=(shape, shape), in_specs=[pl.BlockS...  27.9 us
    pallas_call x1, Pallas kernels, make_routes(): pl.pallas_call(routing_kernel, out_shape=jax.ShapeDtypeStruct((8 * PERMS,...  20 us
    pallas_call x1, Pallas kernels, solve(): pl.pallas_call(solve_kernel, out_shape=(jax.ShapeDtypeStruct((BLOCK, BLOC...  18.8 us
    pallas_call x1, Pallas kernels, stream(): pl.pallas_call(stream_kernel, out_shape=(jax.ShapeDtypeStruct((19, TILES,...  13.4 us
    pallas_call x1, Pallas kernels, exchange_halo(): pl.pallas_call(halo_kernel, out_shape=jax.ShapeDtypeStruct((BLOCK + 8, BL...  12.3 us
    pallas_call x1, Pallas kernels, collide(): pl.pallas_call(collide_kernel, out_shape=(jax.ShapeDtypeStruct((19, TILES...  12 us

profile of v2, /device:TPU:0, one launch (start us, length us, event | category | flops | bytes accessed | tf_op | source)
XLA Modules:
  0.0 197.3 jit_solution(5229511995506101443)
XLA Ops:
  0.6 0.0 copy-start.1
  0.6 0.0 copy-start.9
  0.7 0.7 tile.10
  1.4 0.1 tile.11
  1.5 1.2 copy.12.mask_ref
  2.7 0.0 copy-start
  2.7 1.0 copy-done
  3.7 0.7 copy-done.8
  4.4 1.6 spread.1.tiles_ref
  6.0 0.0 copy-start.4
  6.0 1.0 copy-done.4
  7.0 42.3 %start.1 = (s32[3,16,8,128]{3,2,1,0:T(8,128)S(1)}, s32[42,48,128]{2,1,0:T(8,128)S(1)}, f32[16,16,16,128]{3,2,1,0:T(8,128)S(1)}) custom-call(s32[8,128]{1,0:T(8,128)S(1)} %fusion.3.ids_ref, s32[32,32,128]{2,1,0:T(8,128)S(1)} %copy-done.4, f32[16,16,16,128]{3,2,1,0:T(8,128)S(1)} %spread.1.tiles_ref), custom_call_target="tpu_custom_call" | custom-call | tf_op jit(solution)/shard_map/start/pallas_call | solution.py:177
  49.3 0.0 copy-start.2
  49.3 1.0 copy-done.2
  50.3 0.6 slice_reduce_fusion.ids_ref
  50.9 1.9 table.1.table_ref
  52.8 0.0 copy-start.6
  52.8 0.6 copy-done.6
  53.4 0.8 assemble.1.block_ref
  54.2 0.0 copy-start.5
  54.2 0.7 copy-done.5
  54.8 20.0 %routes.1.table_ref.routes_ref = s32[48,128]{1,0:T(8,128)S(1)} custom-call(s32[1]{0:T(128)} %bitcast.me_ref, s32[3,128]{1,0:T(4,128)S(1)} %copy-done.5), custom_call_target="tpu_custom_call" | custom-call | tf_op jit(solution)/shard_map/routes/pallas_call | solution.py:397
  74.9 12.3 %halo.1.source_ref = f32[40,48,128]{2,1,0:T(8,128)S(1)} custom-call(f32[32,32,128]{2,1,0:T(8,128)S(1)} %assemble.1.block_ref), custom_call_target="tpu_custom_call" | custom-call | tf_op jit(solution)/shard_map/halo/pallas_call | solution.py:221
  87.2 0.0 copy-done.9
  87.2 0.0 copy-start.3
  87.2 1.2 copy-done.3
  88.4 18.8 %solve.1 = (f32[32,32,128]{2,1,0:T(8,128)}, f32[4,24,16,128]{3,2,1,0:T(8,128)S(1)}) custom-call(f32[4]{0:T(128)S(1)} %copy-done.9, s32[42,48,128]{2,1,0:T(8,128)S(1)} %copy-done.3, f32[40,48,128]{2,1,0:T(8,128)S(1)} %halo.1.source_ref), custom_call_target="tpu_custom_call" | custom-call | tf_op jit(solution)/shard_map/solve/pallas_call | solution.py:815
  107.2 27.9 %back.1 = (f32[4,12,16,128]{3,2,1,0:T(8,128)S(1)}, f32[4,12,16,128]{3,2,1,0:T(8,128)S(1)}) custom-call(s32[48,128]{1,0:T(8,128)S(1)} %routes.1.table_ref.routes_ref, f32[4,24,16,128]{3,2,1,0:T(8,128)S(1)} %get-tuple-element.22.items_ref), custom_call_target="tpu_custom_call" | custom-call | tf_op jit(solution)/shard_map/back/pallas_call | solution.py:512
  135.0 0.6 copy-done.7
  135.6 12.0 %collide.1 = (f32[19,4,16,16,128]{4,3,2,1,0:T(8,128)S(1)}, f32[3,4,16,16,128]{4,3,2,1,0:T(8,128)S(1)}, f32[4,5,6,16,128]{4,3,2,1,0:T(8,128)S(1)}, f32[2,8,128]{2,1,0:T(8,128)S(1)}) custom-call(s32[24]{0:T(128)S(1)} %copy-done.7, s32[48,128]{1,0:T(8,128)S(1)} %routes.1.table_ref.routes_ref, f32[19,4,16,16,128]{4,3,2,1,0:T(8,128)} %pops_ref.1, ...), custom_call_target="tpu_custom_call" | custom-call | tf_op jit(solution)/shard_map/collide/pallas_call | solution.py:961
  147.7 36.2 %faces.1 = (f32[4,5,3,16,128]{4,3,2,1,0:T(8,128)S(1)}, f32[4,5,3,16,128]{4,3,2,1,0:T(8,128)S(1)}, f32[3,16,2,8,128]{4,3,2,1,0:T(8,128)S(1)}) custom-call(s32[48,128]{1,0:T(8,128)S(1)} %routes.1.table_ref.routes_ref, f32[4,5,6,16,128]{4,3,2,1,0:T(8,128)S(1)} %get-tuple-element.27.faces_ref, f32[2,8,128]{2,1,0:T(8,128)S(1)} %get-tuple-element.28.corners_ref), custom_call_target="tpu_custom_call" | custom-call | tf_op jit(solution)/shard_map/faces/pallas_call | solution.py:638
  183.9 13.4 %stream.1 = (f32[19,4,16,16,128]{4,3,2,1,0:T(8,128)}, f32[4,16,16,128]{3,2,1,0:T(8,128)}) custom-call(s32[24]{0:T(128)S(1)} %copy-done.7, s32[48,128]{1,0:T(8,128)S(1)} %routes.1.table_ref.routes_ref, f32[19,4,16,16,128]{4,3,2,1,0:T(8,128)S(1)} %get-tuple-element.25.relaxed_ref, f32[3,4,16,16,128]{4,3,2,1,0:T(8,128)S(1)} %get-tuple-element.26.vel_ref, ...), custom_call_target="tpu_custom_call" | custom-call | tf_op jit(solution)/shard_map/stream/pallas_call | solution.py:1136
  (4 shorter events, 0.0 us)
Async XLA Ops:
  0.6 134.4 %copy-start.1 = (f32[4,16,16,128]{3,2,1,0:T(8,128)S(1)}, f32[4,16,16,128]{3,2,1,0:T(8,128)}, u32[]{:S(2)}) copy-start(f32[4,16,16,128]{3,2,1,0:T(8,128)} %charge_ref.5) | copy-start | bytes 1572868
  0.6 86.5 %copy-start.9 = (f32[4]{0:T(128)S(1)}, f32[4]{0:T(128)}, u32[]{:S(2)}) copy-start(f32[4]{0:T(128)} %permit_ref.1) | copy-start | bytes 52
  2.7 1.0 copy-start
  3.7 0.7 copy-start.8
  6.0 1.0 copy-start.4
  49.3 1.0 copy-start.2
  52.8 0.6 copy-start.6
  54.2 0.7 copy-start.5
  87.2 1.2 copy-start.3
  135.0 0.6 copy-start.7

commit v3 on v2

v3 whole, which is shorter than its diff:
```python
import functools

import jax
import jax.numpy as jnp
from jax import lax
from jax.experimental import pallas as pl
from jax.experimental.pallas import tpu as pltpu
from jax.sharding import PartitionSpec as P

EDGE = 16
DEPTH = 128
BLOCK = 32
PHASES = 4
TILES = 4
GROUPS = 16
BANDS = 8
COLS = 32
SIDE = 8
MESH = pl.DeviceIdType.MESH

LATTICE = (
    (0, 0, 0),
    (1, 0, 0),
    (-1, 0, 0),
    (0, 1, 0),
    (0, -1, 0),
    (0, 0, 1),
    (0, 0, -1),
    (1, 1, 0),
    (-1, -1, 0),
    (1, -1, 0),
    (-1, 1, 0),
    (1, 0, 1),
    (-1, 0, -1),
    (1, 0, -1),
    (-1, 0, 1),
    (0, 1, 1),
    (0, -1, -1),
    (0, 1, -1),
    (0, -1, 1),
)
WEIGHTS = (1.0 / 3.0, 1.0 / 18.0, 1.0 / 36.0)
PAIRS = ((1, 2), (3, 4), (5, 6), (7, 8), (9, 10), (11, 12), (13, 14), (15, 16), (17, 18))
relax_time = 0.8
screening = 0.001
spectrum_low = 0.1
spectrum_high = 2.0

AROUND = tuple((dx, dy) for dx in (-1, 0, 1) for dy in (-1, 0, 1) if (dx, dy) != (0, 0))

TO_OWNER, TO_HOLDER = 0, 1
UP_Y, DOWN_Y, SAME_X, BELOW_X, ABOVE_X = range(5)
R_ROW, R_CORNER = 40, 41


def opposite(direction):
    return LATTICE.index(tuple(-entry for entry in LATTICE[direction]))


def crossing(axis_index, face_sign):
    return [d for d in range(19) if LATTICE[d][axis_index] == face_sign]


def shifted_id(dx, dy):
    gx = lax.rem(lax.axis_index("gx") + dx + BANDS, BANDS)
    gy = lax.rem(lax.axis_index("gy") + dy + GROUPS, GROUPS)
    return {"gx": gx, "gy": gy}


def span(step, width, pad):
    if step == 0:
        return pl.ds(0, BLOCK), pl.ds(pad, BLOCK)
    if step > 0:
        return pl.ds(BLOCK - width, width), pl.ds(pad - width, width)
    return pl.ds(0, width), pl.ds(pad + BLOCK, width)


def halo_copies(block_ref, ext_ref, width, send_sem, recv_sem):
    copies = []
    for n, (dx, dy) in enumerate(AROUND):
        src_i, dst_i = span(dx, width, width)
        src_j, dst_j = span(dy, SIDE, SIDE)
        copies.append(
            pltpu.make_async_remote_copy(
                src_ref=block_ref.at[src_i, src_j],
                dst_ref=ext_ref.at[dst_i, dst_j],
                send_sem=send_sem.at[n],
                recv_sem=recv_sem.at[n],
                device_id=shifted_id(dx, dy),
                device_id_type=MESH,
            )
        )
    return copies


def greet(targets):
    barrier = pltpu.get_barrier_semaphore()
    for target in targets:
        pl.semaphore_signal(barrier, inc=1, device_id=target, device_id_type=MESH)
    pl.semaphore_wait(barrier, len(targets))


def start_kernel(
    ids_ref, phase_ref, all_ref, ext_ref, send_sem, recv_sem, ids_send, ids_recv, own_sem
):
    me = lax.axis_index("gy")
    peers = [shifted_id(0, k) for k in range(1, GROUPS)]
    greet(peers + [shifted_id(dx, dy) for dx, dy in AROUND if dx != 0])
    started = []
    for k, target in enumerate(peers):
        copy = pltpu.make_async_remote_copy(
            src_ref=ids_ref,
            dst_ref=all_ref.at[me],
            send_sem=ids_send.at[k],
            recv_sem=ids_recv.at[k],
            device_id=target,
            device_id_type=MESH,
        )
        copy.start()
        started.append(copy)
    for copy in halo_copies(phase_ref, ext_ref, 5, send_sem, recv_sem):
        copy.start()
        started.append(copy)
    own = [
        pltpu.make_async_copy(ids_ref, all_ref.at[me], own_sem.at[0]),
        pltpu.make_async_copy(
            phase_ref, ext_ref.at[pl.ds(5, BLOCK), pl.ds(SIDE, BLOCK)], own_sem.at[1]
        ),
    ]
    for copy in own:
        copy.start()
    for copy in own + started:
        copy.wait()


def exchange_start(ids, phase):
    vmem = pl.BlockSpec(memory_space=pltpu.VMEM)
    dma = pltpu.SemaphoreType.DMA
    return pl.pallas_call(
        start_kernel,
        out_shape=(
            jax.ShapeDtypeStruct((GROUPS, 8, DEPTH), jnp.int32),
            jax.ShapeDtypeStruct((BLOCK + 10, BLOCK + 2 * SIDE, DEPTH), jnp.int32),
        ),
        in_specs=[vmem, vmem],
        out_specs=(vmem, vmem),
        scratch_shapes=[
            dma((8,)),
            dma((8,)),
            dma((GROUPS - 1,)),
            dma((GROUPS - 1,)),
            dma((2,)),
        ],
        compiler_params=pltpu.CompilerParams(
            collective_id=0, has_side_effects=True, vmem_limit_bytes=8 << 20
        ),
        name="start",
    )(ids, phase)


WIDE = BLOCK + 2 * SIDE
TALL = BLOCK + 8
ROOM = WIDE + 16
INNER = pl.ds(8, WIDE)
BEFORE = pl.ds(7, WIDE)
AFTER = pl.ds(9, WIDE)
PACK = 24


def harmonic(left, right):
    return 2.0 * left * right / (left + right)


def look_up_rows(permit_ref, phase_ref, permit):
    def look_up(i, carry):
        label = phase_ref[i]
        value = jnp.where(label == 0, permit_ref[0], 0.0)
        for k in range(1, PHASES):
            value = jnp.where(label == k, permit_ref[k], value)
        permit[i] = value
        return carry

    lax.fori_loop(0, TALL + 2, look_up, 0)


def weigh_rows(begin, end, permit, coef, scale_ref):
    def weigh(i, below):
        here = permit[i + 1]
        above = harmonic(here, permit[i + 2])
        right = harmonic(here, pltpu.roll(here, WIDE - 1, 0))
        left = pltpu.roll(right, 1, 0)
        up = harmonic(here, pltpu.roll(here, DEPTH - 1, 1))
        down = pltpu.roll(up, 1, 1)
        scale = 1.0 / (above + below + right + left + up + down + screening)
        for k, weight in enumerate((above, below, right, left, up, down)):
            coef[k, i] = weight * scale
        scale_ref[i] = scale
        return above

    lax.fori_loop(begin, end, weigh, harmonic(permit[begin], permit[begin + 1]))


K_FIRST, K_X2, K_X3, K_X4, K_Y2, K_Y3, K_Y4, K_LAST = range(8)
PORTS = 64


def to_column(row, eye):
    return jnp.sum(jnp.where(eye, row, 0), axis=1, keepdims=True)


def split_edges(left, right, sub, lane, doublings):
    def partners(ends):
        same = ends[0] == ends[1]
        before = jnp.where(same & (lane < sub), 1, 0)
        after = jnp.where(same & (sub < lane), 1, 0)
        rank_c = jnp.sum(before, axis=1, keepdims=True)
        rank_r = jnp.sum(after, axis=0, keepdims=True)
        pair = same & ((rank_c >> 1) == (rank_r >> 1)) & (sub != lane)
        return jnp.where(pair, 1.0, 0.0).astype(jnp.bfloat16)

    def times(a, b):
        return jnp.dot(a, b, preferred_element_type=jnp.float32)

    by_left, by_right = partners(left), partners(right)
    reach = times(by_left, by_right) + times(by_right, by_left)
    reach = jnp.where((sub == lane) | (reach > 0.0), 1.0, 0.0).astype(jnp.bfloat16)
    for _ in range(doublings):
        reach = jnp.where(times(reach, reach) > 0.0, 1.0, 0.0).astype(jnp.bfloat16)
    mate = times(by_left, reach) > 0.0
    own = reach.astype(jnp.float32) > 0.0
    size = sub.shape[0]
    col = jnp.where(
        jnp.min(jnp.where(own, lane, size), axis=1, keepdims=True)
        > jnp.min(jnp.where(mate, lane, size), axis=1, keepdims=True),
        1,
        0,
    )
    row = jnp.where(
        jnp.min(jnp.where(own, sub, size), axis=0, keepdims=True)
        > jnp.min(jnp.where(mate, sub, size), axis=0, keepdims=True),
        1,
        0,
    )
    return col, row


def join(first, second, base):
    return tuple(a * base + b for a, b in zip(first, second))


def colour(left, right, sub, lane, doublings):
    high = split_edges(left, right, sub, lane, doublings)
    low = split_edges(join(left, high, 2), join(right, high, 2), sub, lane, doublings - 1)
    return join(high, low, 2)


class Ports:
    def __init__(self, size):
        self.size = size
        self.sub = lax.broadcasted_iota(jnp.int32, (size, size), 0)
        self.lane = lax.broadcasted_iota(jnp.int32, (size, size), 1)
        self.eye = self.sub == self.lane
        edge = (
            lax.broadcasted_iota(jnp.int32, (size, 1), 0),
            lax.broadcasted_iota(jnp.int32, (1, size), 1),
        )
        self.port = tuple(e & (PORTS - 1) for e in edge)
        self.half = tuple(e >> 6 for e in edge)
        self.device = tuple(e >> 2 for e in self.port)
        self.entry = lax.broadcasted_iota(jnp.int32, (size, DEPTH), 1)


def store_routes(me, ports, places, goal_ids, target, store):
    half, port, device = ports.half, ports.port, ports.device
    sub, lane = ports.sub, ports.lane
    my_row, my_col = me >> 2, me & 3
    at = to_column(goal_ids, ports.eye) + half[0] * PORTS
    target = target + half[1] * PORTS
    drop = jnp.sum(jnp.where(at == target, sub & (PORTS - 1), 0), axis=0, keepdims=True)
    drop = (to_column(drop, ports.eye), drop)
    goal = tuple(d >> 2 for d in drop)
    begin = tuple(h * GROUPS + d for h, d in zip(half, device))
    end = tuple(h * GROUPS + d for h, d in zip(half, goal))
    j = colour(begin, end, sub, lane, 4)
    group = tuple(h * 4 + c for h, c in zip(half, j))
    rows = (tuple(d >> 2 for d in device), tuple(d >> 2 for d in goal))
    cols = (tuple(d & 3 for d in device), tuple(d & 3 for d in goal))
    b = colour(join(group, rows[0], 4), join(group, rows[1], 4), sub, lane, 2)[0]
    g = colour(join(group, cols[0], 4), join(group, cols[1], 4), sub, lane, 2)[0]
    j = j[0]
    slots = (port[0] & 3, drop[0] & 3)
    ends = (device[0], goal[0])
    rows, cols = tuple(r[0] for r in rows), tuple(c[0] for c in cols)
    for perm, h, back in places:
        mine = half[0] == h
        src, dst = (1, 0) if back else (0, 1)
        for kind, given, key, value in (
            (K_FIRST, ends[src] == me, j, slots[src]),
            (K_X2, (rows[src] == my_row) & (j == my_col), b, cols[src]),
            (K_X3, (j == my_col) & (b == my_row), rows[dst], rows[src]),
            (K_X4, (j == my_col) & (rows[dst] == my_row), cols[dst], b),
            (K_Y2, (cols[src] == my_col) & (j == my_row), g, rows[src]),
            (K_Y3, (j == my_row) & (g == my_col), cols[dst], cols[src]),
            (K_Y4, (j == my_row) & (cols[dst] == my_col), rows[dst], g),
            (K_LAST, ends[dst] == me, slots[dst], j),
        ):
            kept = jnp.where(mine & given, value, 0)
            found = jnp.where(key == ports.entry, kept, 0)
            store(perm * 8 + kind, jnp.sum(found, axis=0, keepdims=True))


def owner_tables(me, own, store):
    ports = Ports(PORTS)
    owner = (ports.port[1] & 3) // 2 * COLS + ports.device[1] * 2 + (ports.port[1] & 1)
    places = ((TO_OWNER, 0, True), (TO_HOLDER, 0, False))
    store_routes(me, ports, places, own[:, :PORTS], owner, store)


def face_tables(me, own, below, above, store):
    ports = Ports(2 * PORTS)
    half = ports.half

    def turn(pos, step):
        return (pos & COLS) + ((pos + step) & (COLS - 1))

    def both(first, second):
        return jnp.where(half[1] == 0, first, pltpu.roll(second, PORTS, 1))

    twice = both(own, own)
    places = ((UP_Y, 0, False), (DOWN_Y, 0, True), (SAME_X, 1, False))
    store_routes(me, ports, places, twice, both(turn(own, 1), own ^ COLS), store)
    yield
    places = ((BELOW_X, 0, False), (ABOVE_X, 1, False))
    store_routes(me, ports, places, twice, both(below ^ COLS, above ^ COLS), store)
    yield
    mine = jnp.sum(
        jnp.where((ports.sub == me * TILES + ports.lane) & (ports.lane < TILES), to_column(own, ports.eye), 0),
        axis=0,
        keepdims=True,
    )
    store(R_ROW, mine >> 5)
    found = []
    for band in (own, below, above):
        at = to_column(band, ports.eye)
        for step in (-1, 1):
            there = (at == turn(mine ^ COLS, step)) & (ports.sub < PORTS)
            found.append(jnp.sum(jnp.where(there, ports.sub, 0), axis=0, keepdims=True))
    upper = (mine >> 5) == 1
    for n in range(2):
        store(R_CORNER + n, jnp.where(upper, found[n], found[2 + n] + PORTS))
        store(R_CORNER + 2 + n, jnp.where(upper, found[4 + n] + 2 * PORTS, found[n]))


def gathered_ids(ids):
    return jnp.sum(ids, axis=0)[0:1]


def owner_routes_kernel(me_ref, ids_ref, out_ref):
    def store(place, row):
        out_ref[pl.ds(place, 1)] = row

    owner_tables(me_ref[0], gathered_ids(ids_ref[...]), store)


def make_routes(kernel, rows, me, *ids):
    vmem = pl.BlockSpec(memory_space=pltpu.VMEM)
    return pl.pallas_call(
        kernel,
        out_shape=jax.ShapeDtypeStruct((rows, DEPTH), jnp.int32),
        in_specs=[pl.BlockSpec(memory_space=pltpu.SMEM)] + [vmem] * len(ids),
        out_specs=vmem,
        compiler_params=pltpu.CompilerParams(vmem_limit_bytes=8 << 20),
        name=kernel.__name__,
    )(me, *ids)


def ring(axis, step):
    gy = lax.axis_index("gy")
    row, col = gy // 4, lax.rem(gy, 4)
    if axis == 0:
        place = lax.rem(col + step, 4)
        return col, place, {"gx": lax.axis_index("gx"), "gy": row * 4 + place}
    place = lax.rem(row + step, 4)
    return row, place, {"gx": lax.axis_index("gx"), "gy": place * 4 + col}


RING_AXES = ((0, 1, 1, 0), (1, 0, 0, 1))
RING_KINDS = ((K_FIRST, K_X2, K_X3, K_X4), (K_FIRST, K_Y2, K_Y3, K_Y4))


class Lane:
    def __init__(self, order, perms, table_ref, first, scratch, final=None):
        self.order, self.perms, self.table_ref = order, perms, table_ref
        self.first, self.final = first, final
        self.stages = [scratch[4 * n : 4 * n + 4] for n in range(4)]
        self.waiting, self.sent = [], []

    def arrived(self):
        for copy in self.waiting:
            copy.wait_recv()
        self.waiting = []

    def target(self, stage, here):
        if stage == 3 and self.final is not None:
            return self.final(here)
        return self.stages[stage][1].at[here]

    def advance(self, stage):
        self.arrived()
        send, _, send_sem, recv_sem = self.stages[stage]
        for step in (2, 1, 3, 0):
            here, place, target = ring(RING_AXES[self.order][stage], step)
            landing = self.target(stage, here)
            for n, perm in enumerate(self.perms):
                slot = self.table_ref[perm * 8 + RING_KINDS[self.order][stage], place]
                if stage:
                    value = self.stages[stage - 1][1][slot, n]
                else:
                    value = self.first(n, slot)
                if step:
                    send[step - 1, n] = value
                else:
                    landing[n] = value
            if step:
                copy = pltpu.make_async_remote_copy(
                    src_ref=send.at[step - 1],
                    dst_ref=landing,
                    send_sem=send_sem.at[step - 1],
                    recv_sem=recv_sem.at[step - 1],
                    device_id=target,
                    device_id_type=MESH,
                )
                copy.start()
                self.waiting.append(copy)
                self.sent.append(copy)

    def close(self):
        for copy in self.sent:
            copy.wait_send()


def lane_scratch(items, shape):
    scratch = []
    for stage in range(4):
        scratch += [
            pltpu.VMEM((3, items) + shape, jnp.float32),
            pltpu.VMEM((4, items) + shape, jnp.float32),
            pltpu.SemaphoreType.DMA((3,)),
            pltpu.SemaphoreType.DMA((3,)),
        ]
    return scratch


RING_PEERS = tuple((axis, step) for axis in range(2) for step in (1, 2, 3))
LANES = 4


def source_kernel(
    permit_ref,
    me_ref,
    table_ref,
    charge_ref,
    mask_ref,
    ids_ref,
    phase_ref,
    ext_ref,
    face_ref,
    coef_ref,
    scale_ref,
    others,
    permit,
    send_sem,
    recv_sem,
    ids_send,
    ids_recv,
    *scratch,
):
    bands = [shifted_id(1, 0), shifted_id(-1, 0)]
    greet([ring(*peer)[2] for peer in RING_PEERS] + [shifted_id(dx, dy) for dx, dy in AROUND])
    passed = []
    for n, target in enumerate(bands):
        copy = pltpu.make_async_remote_copy(
            src_ref=ids_ref,
            dst_ref=others.at[n],
            send_sem=ids_send.at[n],
            recv_sem=ids_recv.at[n],
            device_id=target,
            device_id_type=MESH,
        )
        copy.start()
        passed.append(copy)
    part = EDGE // LANES
    lanes = []
    for n in range(LANES):

        def first(_, slot, n=n):
            flags = mask_ref[slot, 1 + n * part : 1 + (n + 1) * part, 1 : EDGE + 1]
            return charge_ref[slot, n * part : (n + 1) * part] * flags.astype(jnp.float32)

        lanes.append(
            Lane(n % 2, (TO_OWNER,), table_ref, first, scratch[16 * n : 16 * n + 16])
        )

    def store(place, row):
        face_ref[pl.ds(place, 1)] = row

    def weights(begin, end):
        weigh_rows(begin, end, permit, coef_ref, scale_ref)

    for stage in range(4):
        for lane in lanes:
            lane.advance(stage)
        if stage == 0:
            look_up_rows(permit_ref, phase_ref, permit)
            weights(0, 8)
            for copy in passed:
                copy.wait_recv()
            tables = face_tables(
                me_ref[0],
                gathered_ids(ids_ref[...]),
                gathered_ids(others[0]),
                gathered_ids(others[1]),
                store,
            )
            next(tables)
        elif stage < 3:
            next(tables, None)
        else:
            weights(8, 24)
    for n, lane in enumerate(lanes):
        lane.arrived()
        final = lane.stages[3][1]
        for t in range(TILES):
            i0, j0 = 4 + (t // 2) * EDGE + n * part, SIDE + (t % 2) * EDGE
            ext_ref[i0 : i0 + part, j0 : j0 + EDGE] = final[
                table_ref[TO_OWNER * 8 + K_LAST, t], 0
            ]
    block = ext_ref.at[pl.ds(4, BLOCK), pl.ds(SIDE, BLOCK)]
    copies = halo_copies(block, ext_ref, 4, send_sem, recv_sem)
    for copy in copies:
        copy.start()
    weights(24, TALL)
    for copy in copies:
        copy.wait()
    for copy in passed:
        copy.wait_send()
    for lane in lanes:
        lane.close()


def gather_source(permittivity, me, routes, charge, fluid_mask, ids, phase):
    vmem = pl.BlockSpec(memory_space=pltpu.VMEM)
    smem = pl.BlockSpec(memory_space=pltpu.SMEM)
    dma = pltpu.SemaphoreType.DMA
    f32 = jnp.float32
    return pl.pallas_call(
        source_kernel,
        out_shape=(
            jax.ShapeDtypeStruct((TALL, WIDE, DEPTH), f32),
            jax.ShapeDtypeStruct((48, DEPTH), jnp.int32),
            jax.ShapeDtypeStruct((6, TALL, WIDE, DEPTH), f32),
            jax.ShapeDtypeStruct((TALL, WIDE, DEPTH), f32),
        ),
        in_specs=[smem] * 3 + [vmem] * 4,
        out_specs=(vmem,) * 4,
        scratch_shapes=[
            pltpu.VMEM((2, GROUPS, 8, DEPTH), jnp.int32),
            pltpu.VMEM((TALL + 2, WIDE, DEPTH), f32),
            dma((8,)),
            dma((8,)),
            dma((2,)),
            dma((2,)),
        ]
        + lane_scratch(1, (EDGE // LANES, EDGE, DEPTH)) * LANES,
        compiler_params=pltpu.CompilerParams(
            collective_id=1, has_side_effects=True, vmem_limit_bytes=24 << 20
        ),
        name="source",
    )(permittivity, me, routes, charge, fluid_mask, ids, phase)


def back_kernel(table_ref, items_ref, out_ref, *scratch):
    greet([ring(*peer)[2] for peer in RING_PEERS])
    part = PACK // LANES
    lanes = []
    for n in range(LANES):
        rows = slice(n * part, (n + 1) * part)

        def first(_, slot, rows=rows):
            return items_ref[slot, rows]

        def final(here, n=n):
            return out_ref.at[here, :, pl.ds(n * part, part)]

        lanes.append(
            Lane(n % 2, (TO_HOLDER,), table_ref, first, scratch[16 * n : 16 * n + 16], final)
        )
    for stage in range(4):
        for lane in lanes:
            lane.advance(stage)
    for lane in lanes:
        lane.arrived()
    for lane in lanes:
        lane.close()


def send_back(routes, packed):
    vmem = pl.BlockSpec(memory_space=pltpu.VMEM)
    return pl.pallas_call(
        back_kernel,
        out_shape=jax.ShapeDtypeStruct((TILES, 1, PACK, EDGE, DEPTH), jnp.float32),
        in_specs=[pl.BlockSpec(memory_space=pltpu.SMEM), vmem],
        out_specs=vmem,
        scratch_shapes=lane_scratch(1, (PACK // LANES, EDGE, DEPTH)) * LANES,
        compiler_params=pltpu.CompilerParams(
            collective_id=2, has_side_effects=True, vmem_limit_bytes=24 << 20
        ),
        name="back",
    )(routes, packed)


FACES = 5


FACE_LANES = (
    (0, (UP_Y, DOWN_Y, SAME_X)),
    (1, (UP_Y, DOWN_Y, SAME_X)),
    (0, (BELOW_X, ABOVE_X)),
    (1, (BELOW_X, ABOVE_X)),
)


def faces_kernel(
    table_ref,
    faces_ref,
    corners_ref,
    out_ref,
    all_ref,
    shifted,
    corner_send,
    corner_recv,
    shift_send,
    shift_recv,
    own_sem,
    *scratch,
):
    me = lax.axis_index("gy")
    peers = [shifted_id(0, k) for k in range(1, GROUPS)]
    bands = [shifted_id(1, 0), shifted_id(-1, 0)]
    greet(peers + bands)
    shifts = []
    for n, target in enumerate(bands):
        copy = pltpu.make_async_remote_copy(
            src_ref=faces_ref.at[:, 3 + n],
            dst_ref=shifted.at[n],
            send_sem=shift_send.at[n],
            recv_sem=shift_recv.at[n],
            device_id=target,
            device_id_type=MESH,
        )
        copy.start()
        shifts.append(copy)
    lanes = []
    for n, (order, perms) in enumerate(FACE_LANES):
        rows = slice(order * 3, order * 3 + 3)

        def first(k, slot, perms=perms, rows=rows):
            if perms[k] < BELOW_X:
                return faces_ref[slot, perms[k], rows]
            return shifted[perms[k] - BELOW_X, slot, rows]

        def final(here, perms=perms, order=order):
            return out_ref.at[here, pl.ds(perms[0], len(perms)), pl.ds(order * 3, 3)]

        lanes.append(Lane(order, perms, table_ref, first, scratch[16 * n : 16 * n + 16], final))
    spread_out, forward = [], []
    own = pltpu.make_async_copy(corners_ref, all_ref.at[0, me], own_sem)
    for stage in range(4):
        for n, lane in enumerate(lanes):
            if stage == 0 and n == 2:
                for k, target in enumerate(peers):
                    copy = pltpu.make_async_remote_copy(
                        src_ref=corners_ref,
                        dst_ref=all_ref.at[0, me],
                        send_sem=corner_send.at[k],
                        recv_sem=corner_recv.at[k],
                        device_id=target,
                        device_id_type=MESH,
                    )
                    copy.start()
                    spread_out.append(copy)
                own.start()
                for copy in shifts:
                    copy.wait_recv()
            lane.advance(stage)
        if stage == 1:
            own.wait()
            for copy in spread_out:
                copy.wait_recv()
            for n, target in enumerate(bands):
                copy = pltpu.make_async_remote_copy(
                    src_ref=all_ref.at[0],
                    dst_ref=all_ref.at[1 + n],
                    send_sem=corner_send.at[GROUPS - 1 + n],
                    recv_sem=corner_recv.at[GROUPS - 1 + n],
                    device_id=target,
                    device_id_type=MESH,
                )
                copy.start()
                forward.append(copy)
    for lane in lanes:
        lane.arrived()
    for copy in forward:
        copy.wait_recv()
    for copy in shifts + spread_out + forward:
        copy.wait_send()
    for lane in lanes:
        lane.close()


def send_faces(routes, faces, corners):
    vmem = pl.BlockSpec(memory_space=pltpu.VMEM)
    f32 = jnp.float32
    dma = pltpu.SemaphoreType.DMA
    scratch = []
    for _, perms in FACE_LANES:
        scratch += lane_scratch(len(perms), (3, EDGE, DEPTH))
    return pl.pallas_call(
        faces_kernel,
        out_shape=(
            jax.ShapeDtypeStruct((TILES, FACES, 6, EDGE, DEPTH), f32),
            jax.ShapeDtypeStruct((3, GROUPS, 2, 8, DEPTH), f32),
        ),
        in_specs=[pl.BlockSpec(memory_space=pltpu.SMEM), vmem, vmem],
        out_specs=(vmem, vmem),
        scratch_shapes=[
            pltpu.VMEM((2, TILES, 6, EDGE, DEPTH), f32),
            dma((GROUPS + 1,)),
            dma((GROUPS + 1,)),
            dma((2,)),
            dma((2,)),
            dma,
        ]
        + scratch,
        compiler_params=pltpu.CompilerParams(
            collective_id=3, has_side_effects=True, vmem_limit_bytes=24 << 20
        ),
        name="faces",
    )(routes, faces, corners)


def solve_kernel(
    coef, scale_ref, source_ref, pot_ref, pack, resid, upd_a, upd_b, total
):
    center = 0.5 * (spectrum_high + spectrum_low)
    half = 0.5 * (spectrum_high - spectrum_low)
    ratio = center / half

    def begin(i, carry):
        value = source_ref[i] * scale_ref[i]
        resid[i] = value
        value = value * (1.0 / center)
        upd_a[i, INNER] = value
        total[i] = value
        return carry

    lax.fori_loop(0, TALL, begin, 0)

    rho = 1.0 / ratio
    old, new = upd_a, upd_b
    for sweep in range(3):
        rho_new = 1.0 / (2.0 * ratio - rho)
        keep, gain = rho_new * rho, 2.0 * rho_new / half

        def relax(i, carry, old=old, new=new, keep=keep, gain=gain):
            here = old[i, INNER]
            near = coef[0, i] * old[i + 1, INNER] + coef[1, i] * old[i - 1, INNER]
            near += coef[2, i] * old[i, AFTER] + coef[3, i] * old[i, BEFORE]
            near += coef[4, i] * pltpu.roll(here, DEPTH - 1, 1)
            near += coef[5, i] * pltpu.roll(here, 1, 1)
            left = resid[i] - here + near
            resid[i] = left
            here = keep * here + gain * left
            new[i, INNER] = here
            total[i] = total[i] + here
            return carry

        lax.fori_loop(sweep + 1, TALL - 1 - sweep, relax, 0)
        old, new = new, old
        rho = rho_new

    def emit(i, carry):
        pot_ref[i] = total[i + 4, pl.ds(SIDE, BLOCK)]
        return carry

    lax.fori_loop(0, BLOCK, emit, 0)
    for t in range(TILES):
        i0, j0 = 4 + (t // 2) * EDGE, SIDE + (t % 2) * EDGE

        def rows(i, carry, t=t, i0=i0, j0=j0):
            pack[t, i] = total[i0 + i, pl.ds(j0, EDGE)]
            for place, ref in ((EDGE + 2, total), (EDGE + 6, source_ref)):
                pack[t, place, pl.ds(i, 1)] = ref[i0 + i, pl.ds(j0 - 1, 1)]
                pack[t, place + 1, pl.ds(i, 1)] = ref[i0 + i, pl.ds(j0 + EDGE, 1)]
            return carry

        lax.fori_loop(0, EDGE, rows, 0)
        for place, ref in ((EDGE, total), (EDGE + 4, source_ref)):
            pack[t, place] = ref[i0 - 1, pl.ds(j0, EDGE)]
            pack[t, place + 1] = ref[i0 + EDGE, pl.ds(j0, EDGE)]


def solve(coef, scale, source):
    vmem = pl.BlockSpec(memory_space=pltpu.VMEM)
    f32 = jnp.float32
    return pl.pallas_call(
        solve_kernel,
        out_shape=(
            jax.ShapeDtypeStruct((BLOCK, BLOCK, DEPTH), f32),
            jax.ShapeDtypeStruct((TILES, PACK, EDGE, DEPTH), f32),
        ),
        in_specs=[vmem, vmem, vmem],
        out_specs=(vmem, vmem),
        scratch_shapes=[
            pltpu.VMEM((TALL, WIDE, DEPTH), f32),
            pltpu.VMEM((TALL, ROOM, DEPTH), f32),
            pltpu.VMEM((TALL, ROOM, DEPTH), f32),
            pltpu.VMEM((TALL, WIDE, DEPTH), f32),
        ],
        compiler_params=pltpu.CompilerParams(vmem_limit_bytes=32 << 20),
        name="solve",
    )(coef, scale, source)


def collide_rows(pops, charge, field):
    force = [charge * component for component in field]
    sums = {}
    diffs = {}
    for a, b in PAIRS:
        sums[a] = pops[a] + pops[b]
        diffs[a] = pops[a] - pops[b]
    density = pops[0]
    for a, _ in PAIRS:
        density = density + sums[a]
    momentum = [
        diffs[1] + diffs[7] + diffs[9] + diffs[11] + diffs[13],
        diffs[3] + diffs[7] - diffs[9] + diffs[15] + diffs[17],
        diffs[5] + diffs[11] - diffs[13] + diffs[15] - diffs[17],
    ]
    inverse = 1.0 / density
    velocity = [(momentum[d] + 0.5 * force[d]) * inverse for d in range(3)]
    scale = 1.0 - 0.5 / relax_time
    rate = 1.0 / relax_time
    speed = velocity[0] * velocity[0] + velocity[1] * velocity[1] + velocity[2] * velocity[2]
    work = velocity[0] * force[0] + velocity[1] * force[1] + velocity[2] * force[2]
    weighted = rate * density
    base = weighted - (1.5 * weighted) * speed - (3.0 * scale) * work
    odd = [3.0 * weighted * velocity[d] + (3.0 * scale) * force[d] for d in range(3)]
    inner = [4.5 * weighted * velocity[d] + (9.0 * scale) * force[d] for d in range(3)]
    keep = 1.0 - rate
    result = [None] * 19
    result[0] = keep * pops[0] + WEIGHTS[0] * base
    for a, b in PAIRS:
        step = LATTICE[a]
        axes = [d for d in range(3) if step[d] != 0]
        if len(axes) == 1:
            (d,) = axes
            cu, co, ci = velocity[d], odd[d], inner[d]
            weight = WEIGHTS[1]
        else:
            d, e = axes
            weight = WEIGHTS[2]
            if step[d] * step[e] > 0:
                cu, co, ci = velocity[d] + velocity[e], odd[d] + odd[e], inner[d] + inner[e]
            else:
                cu, co, ci = velocity[d] - velocity[e], odd[d] - odd[e], inner[d] - inner[e]
        even = weight * (base + cu * ci)
        lean = weight * co
        result[a] = keep * pops[a] + (even + lean)
        result[b] = keep * pops[b] + (even - lean)
    return result, velocity


def collide_kernel(
    table_ref, routes_ref, pops_ref, charge_ref, mask_ref, pot_ref, out_ref, vel_ref, face_ref, corner_ref, grown
):
    tile = pl.program_id(0)

    def place(i, carry):
        grown[i + 1, pl.ds(8, EDGE)] = pot_ref[0, 0, i]
        grown[i + 1, pl.ds(7, 1)] = pot_ref[0, 0, EDGE + 2, pl.ds(i, 1)]
        grown[i + 1, pl.ds(8 + EDGE, 1)] = pot_ref[0, 0, EDGE + 3, pl.ds(i, 1)]
        return carry

    lax.fori_loop(0, EDGE, place, 0)
    grown[0, pl.ds(8, EDGE)] = pot_ref[0, 0, EDGE]
    grown[EDGE + 1, pl.ds(8, EDGE)] = pot_ref[0, 0, EDGE + 1]
    y_low, y_high = crossing(1, -1), crossing(1, 1)

    def rows(i, carry):
        here = grown[i + 1, pl.ds(8, EDGE)]
        field = [
            0.5 * (grown[i, pl.ds(8, EDGE)] - grown[i + 2, pl.ds(8, EDGE)]),
            0.5 * (grown[i + 1, pl.ds(7, EDGE)] - grown[i + 1, pl.ds(9, EDGE)]),
            0.5 * (pltpu.roll(here, 1, 1) - pltpu.roll(here, DEPTH - 1, 1)),
        ]
        pops = [pops_ref[q, 0, i] for q in range(19)]
        relaxed, velocity = collide_rows(pops, charge_ref[0, i], field)
        fluid = mask_ref[0, i + 1, pl.ds(1, EDGE), :] == 1
        for q in range(19):
            value = jnp.where(fluid, relaxed[q], pops[q])
            out_ref[q, 0, i] = value
            if q in y_low:
                face_ref[0, 1, y_low.index(q), pl.ds(i, 1)] = value[0:1]
            if q in y_high:
                face_ref[0, 0, y_high.index(q), pl.ds(i, 1)] = value[EDGE - 1 :]
        for d in range(3):
            vel_ref[d, 0, i] = velocity[d]
        face_ref[0, 1, 5, pl.ds(i, 1)] = velocity[1][0:1]
        face_ref[0, 0, 5, pl.ds(i, 1)] = velocity[1][EDGE - 1 :]
        return carry

    lax.fori_loop(0, EDGE, rows, 0)

    def x_face(face, sign, layer):
        for k, q in enumerate(crossing(0, sign)):
            face_ref[0, face, k] = out_ref[q, 0, layer]
        face_ref[0, face, 5] = vel_ref[0, 0, layer]

    x_face(3, 1, EDGE - 1)
    x_face(4, -1, 0)

    @pl.when(table_ref[R_ROW, tile] == 0)
    def _():
        x_face(2, 1, EDGE - 1)

    @pl.when(table_ref[R_ROW, tile] == 1)
    def _():
        x_face(2, -1, 0)

    for n, (q, i, j) in enumerate(
        ((7, EDGE - 1, EDGE - 1), (9, EDGE - 1, 0), (10, 0, EDGE - 1), (8, 0, 0))
    ):
        corner_ref[tile // 2, pl.ds(lax.rem(tile, 2) * 4 + n, 1)] = out_ref[q, 0, i, pl.ds(j, 1)]


def collide(table, routes, populations, charge, fluid_mask, returned):
    f32 = jnp.float32
    pot_spec = pl.BlockSpec(
        (1, 1, PACK, EDGE, DEPTH), lambda s, tab, rts: (rts[TO_HOLDER * 8 + K_LAST, s], 0, 0, 0, 0)
    )
    return pl.pallas_call(
        collide_kernel,
        out_shape=(
            jax.ShapeDtypeStruct((19, TILES, EDGE, EDGE, DEPTH), f32),
            jax.ShapeDtypeStruct((3, TILES, EDGE, EDGE, DEPTH), f32),
            jax.ShapeDtypeStruct((TILES, FACES, 6, EDGE, DEPTH), f32),
            jax.ShapeDtypeStruct((2, 8, DEPTH), f32),
        ),
        grid_spec=pltpu.PrefetchScalarGridSpec(
            num_scalar_prefetch=2,
            grid=(TILES,),
            in_specs=[
                pl.BlockSpec((19, 1, EDGE, EDGE, DEPTH), lambda s, tab, rts: (0, s, 0, 0, 0)),
                pl.BlockSpec((1, EDGE, EDGE, DEPTH), lambda s, tab, rts: (s, 0, 0, 0)),
                pl.BlockSpec((1, EDGE + 2, EDGE + 2, DEPTH), lambda s, tab, rts: (s, 0, 0, 0)),
                pot_spec,
            ],
            out_specs=[
                pl.BlockSpec((19, 1, EDGE, EDGE, DEPTH), lambda s, tab, rts: (0, s, 0, 0, 0)),
                pl.BlockSpec((3, 1, EDGE, EDGE, DEPTH), lambda s, tab, rts: (0, s, 0, 0, 0)),
                pl.BlockSpec((1, FACES, 6, EDGE, DEPTH), lambda s, tab, rts: (s, 0, 0, 0, 0)),
                pl.BlockSpec((2, 8, DEPTH), lambda s, tab, rts: (0, 0, 0)),
            ],
            scratch_shapes=[pltpu.VMEM((EDGE + 2, 32, DEPTH), f32)],
        ),
        compiler_params=pltpu.CompilerParams(vmem_limit_bytes=32 << 20),
        name="collide",
    )(table, routes, populations, charge, fluid_mask, returned)


def stream_kernel(
    table_ref,
    routes_ref,
    relaxed_ref,
    vel_ref,
    charge_ref,
    mask_ref,
    rim_ref,
    *rest,
):
    faces, (corner_ref, pops_out, charge_out, xrim, yrim, corner) = rest[:FACES], rest[FACES:]
    tile = pl.program_id(0)
    row = table_ref[R_ROW, tile]
    plus = [crossing(0, 1), crossing(1, 1)]
    minus = [crossing(0, -1), crossing(1, -1)]

    def fill(out, face):
        for k in range(6):
            out[k] = faces[face][0, 0, k]

    fill(yrim.at[0], 0)
    fill(yrim.at[1], 1)
    for n, (side, end, which) in enumerate(((0, 0, 0), (0, 1, 1), (1, 0, 2), (1, 1, 3))):
        found = table_ref[R_CORNER + n, tile]
        tile_in = lax.rem(found, TILES)
        corner[side, pl.ds(end, 1)] = corner_ref[
            found // TILES, tile_in // 2, pl.ds(lax.rem(tile_in, 2) * 4 + which, 1)
        ]

    @pl.when(row == 0)
    def _():
        fill(xrim.at[0], 3)
        fill(xrim.at[1], 2)

    @pl.when(row == 1)
    def _():
        fill(xrim.at[0], 2)
        fill(xrim.at[1], 4)

    place = lax.broadcasted_iota(jnp.int32, (EDGE, DEPTH), 0)
    first, last = place == 0, place == EDGE - 1

    def rows(i, low_edge, high_edge):
        own = mask_ref[0, i + 1, pl.ds(1, EDGE), :]
        own_fluid = own == 1
        for q in range(19):
            step_x, step_y, step_z = LATTICE[q]
            value_here = relaxed_ref[q, 0, i]
            if q == 0:
                pops_out[q, 0, i] = value_here
                continue
            side = None
            if step_x == 1 and low_edge:
                side, channel = 0, plus[0].index(q)
            if step_x == -1 and high_edge:
                side, channel = 1, minus[0].index(q)
            if side is None:
                moved = value_here if step_x == 0 else relaxed_ref[q, 0, i - step_x]
            else:
                moved = xrim[side, channel]
            if step_y == 1:
                if side is None:
                    edge = yrim[0, plus[1].index(q), pl.ds(i - step_x, 1)]
                else:
                    edge = corner[side, pl.ds(0, 1)]
                moved = jnp.where(first, edge, pltpu.roll(moved, 1, 0))
            elif step_y == -1:
                if side is None:
                    edge = yrim[1, minus[1].index(q), pl.ds(i - step_x, 1)]
                else:
                    edge = corner[side, pl.ds(1, 1)]
                moved = jnp.where(last, edge, pltpu.roll(moved, EDGE - 1, 0))
            from_fluid = mask_ref[0, i + 1 - step_x, pl.ds(1 - step_y, EDGE), :]
            if step_z != 0:
                moved = pltpu.roll(moved, step_z % DEPTH, 1)
                from_fluid = pltpu.roll(from_fluid, step_z % DEPTH, 1)
            bounced = relaxed_ref[opposite(q), 0, i]
            read = jnp.where(from_fluid == 1, moved, bounced)
            pops_out[q, 0, i] = jnp.where(own_fluid, read, value_here)

        charge = charge_ref[0, i]
        flag = own.astype(jnp.float32)

        def flux(speed_a, speed_b, value_a, value_b, flags):
            speed = 0.5 * (speed_a + speed_b)
            return speed * jnp.where(speed > 0, value_a, value_b) * flags

        speed = vel_ref[0, 0, i]
        if low_edge:
            other, other_speed = rim_ref[0, 0, 0], xrim[0, 5]
        else:
            other, other_speed = charge_ref[0, i - 1], vel_ref[0, 0, i - 1]
        other_flag = mask_ref[0, i, pl.ds(1, EDGE), :].astype(jnp.float32)
        change = -flux(other_speed, speed, other, charge, other_flag * flag)
        if high_edge:
            other, other_speed = rim_ref[0, 0, 1], xrim[1, 5]
        else:
            other, other_speed = charge_ref[0, i + 1], vel_ref[0, 0, i + 1]
        other_flag = mask_ref[0, i + 2, pl.ds(1, EDGE), :].astype(jnp.float32)
        change += flux(speed, other_speed, charge, other, flag * other_flag)

        speed = vel_ref[1, 0, i]
        other = jnp.where(first, rim_ref[0, 0, 2, pl.ds(i, 1)], pltpu.roll(charge, 1, 0))
        other_speed = jnp.where(first, yrim[0, 5, pl.ds(i, 1)], pltpu.roll(speed, 1, 0))
        other_flag = mask_ref[0, i + 1, pl.ds(0, EDGE), :].astype(jnp.float32)
        change -= flux(other_speed, speed, other, charge, other_flag * flag)
        other = jnp.where(last, rim_ref[0, 0, 3, pl.ds(i, 1)], pltpu.roll(charge, EDGE - 1, 0))
        other_speed = jnp.where(
            last, yrim[1, 5, pl.ds(i, 1)], pltpu.roll(speed, EDGE - 1, 0)
        )
        other_flag = mask_ref[0, i + 1, pl.ds(2, EDGE), :].astype(jnp.float32)
        change += flux(speed, other_speed, charge, other, flag * other_flag)

        speed = vel_ref[2, 0, i]
        over = flux(
            speed,
            pltpu.roll(speed, DEPTH - 1, 1),
            charge,
            pltpu.roll(charge, DEPTH - 1, 1),
            flag * pltpu.roll(flag, DEPTH - 1, 1),
        )
        change += over - pltpu.roll(over, 1, 1)
        charge_out[0, i] = jnp.where(own_fluid, charge - change, charge)

    rows(0, True, False)

    def middle(i, carry):
        rows(i, False, False)
        return carry

    lax.fori_loop(1, EDGE - 1, middle, 0)
    rows(EDGE - 1, False, True)


def stream(table, routes, relaxed, velocity, charge, fluid_mask, returned, faces, corners):
    f32 = jnp.float32
    face_specs = [
        pl.BlockSpec(
            (1, 1, 6, EDGE, DEPTH),
            lambda s, tab, rts, face=face: (tab[face * 8 + K_LAST, s], face, 0, 0, 0),
        )
        for face in range(FACES)
    ]
    return pl.pallas_call(
        stream_kernel,
        out_shape=(
            jax.ShapeDtypeStruct((19, TILES, EDGE, EDGE, DEPTH), f32),
            jax.ShapeDtypeStruct((TILES, EDGE, EDGE, DEPTH), f32),
        ),
        grid_spec=pltpu.PrefetchScalarGridSpec(
            num_scalar_prefetch=2,
            grid=(TILES,),
            in_specs=[
                pl.BlockSpec((19, 1, EDGE, EDGE, DEPTH), lambda s, tab, rts: (0, s, 0, 0, 0)),
                pl.BlockSpec((3, 1, EDGE, EDGE, DEPTH), lambda s, tab, rts: (0, s, 0, 0, 0)),
                pl.BlockSpec((1, EDGE, EDGE, DEPTH), lambda s, tab, rts: (s, 0, 0, 0)),
                pl.BlockSpec((1, EDGE + 2, EDGE + 2, DEPTH), lambda s, tab, rts: (s, 0, 0, 0)),
                pl.BlockSpec(
                    (1, 1, 4, EDGE, DEPTH), lambda s, tab, rts: (rts[TO_HOLDER * 8 + K_LAST, s], 0, 5, 0, 0)
                ),
            ]
            + face_specs
            + [pl.BlockSpec((3 * GROUPS, 2, 8, DEPTH), lambda s, tab, rts: (0, 0, 0, 0))],
            out_specs=[
                pl.BlockSpec((19, 1, EDGE, EDGE, DEPTH), lambda s, tab, rts: (0, s, 0, 0, 0)),
                pl.BlockSpec((1, EDGE, EDGE, DEPTH), lambda s, tab, rts: (s, 0, 0, 0)),
            ],
            scratch_shapes=[
                pltpu.VMEM((2, 6, EDGE, DEPTH), f32),
                pltpu.VMEM((2, 6, EDGE, DEPTH), f32),
                pltpu.VMEM((2, 8, DEPTH), f32),
            ],
        ),
        compiler_params=pltpu.CompilerParams(vmem_limit_bytes=32 << 20),
        name="stream",
    )(
        table,
        routes,
        relaxed,
        velocity,
        charge,
        fluid_mask,
        returned,
        *([faces] * FACES),
        corners.reshape(3 * GROUPS, 2, 8, DEPTH),
    )


def per_device(populations, charge, fluid_mask, tile_ids, phase_label, permittivity):
    me = lax.axis_index("gy").astype(jnp.int32).reshape(1)
    place = jnp.arange(8 * DEPTH, dtype=jnp.int32).reshape(8, DEPTH)
    ids_row = jnp.where(place // TILES == me, jnp.tile(tile_ids, 2 * DEPTH).reshape(8, DEPTH), 0)
    ids, phase_ext = exchange_start(ids_row, phase_label)
    routes = make_routes(owner_routes_kernel, 16, me, ids)
    source_ext, table, coef, scale = gather_source(
        permittivity, me, routes, charge, fluid_mask, ids, phase_ext
    )
    potential, packed = solve(coef, scale, source_ext)
    returned = send_back(routes, packed)
    relaxed, velocity, faces, corners = collide(
        table, routes, populations, charge, fluid_mask, returned
    )
    rims, all_corners = send_faces(table, faces, corners)
    populations_next, charge_next = stream(
        table, routes, relaxed, velocity, charge, fluid_mask, returned, rims, all_corners
    )
    return (populations_next, charge_next, potential)


def solution(mesh):
    placed = (
        P(None, ("gx", "gy"), None, None, None),
        P(("gx", "gy"), None, None, None),
        P(("gx", "gy"), None, None, None),
        P(("gx", "gy")),
        P("gx", "gy", None),
        P(),
    )
    return jax.shard_map(
        per_device,
        mesh=mesh,
        in_specs=placed,
        out_specs=(
            P(None, ("gx", "gy"), None, None, None),
            P(("gx", "gy"), None, None, None),
            P("gx", "gy", None),
        ),
        check_vma=False,
    )
```

time: 198 us -> 154 us (0.78)
  Pallas kernels: 187 us -> 148 us
  local copies, waits for them, and re-layouts: 8.77 us -> 4.72 us
    pallas_call x8 -> x5, Pallas kernels: 143 us -> 111 us  [the longest x1 35.3 us: gather_source(): pl.pallas_call(source_kernel, out_shape=(jax.ShapeDtypeStruct((TALL, WIDE...]
    pallas_call x1, Pallas kernels: 18.8 us -> 11.4 us  [solve(): pl.pallas_call(solve_kernel, out_shape=(jax.ShapeDtypeStruct((BLOCK, BLOC...]
    unnamed x21 -> x9, local copies, waits for them, and re-layouts: 7.95 us -> 3.91 us
where the time goes in v3:
time: 154 us; the launch traced here: 153 us
  Pallas kernels  148 us (96%)
  local copies, waits for them, and re-layouts  4.72 us (3%)
    pallas_call x1, Pallas kernels, gather_source(): pl.pallas_call(source_kernel, out_shape=(jax.ShapeDtypeStruct((TALL, WIDE...  35.3 us
    pallas_call x1, Pallas kernels, send_faces(): pl.pallas_call(faces_kernel, out_shape=(jax.ShapeDtypeStruct((TILES, FACE...  29.9 us
    pallas_call x1, Pallas kernels, send_back(): pl.pallas_call(back_kernel, out_shape=jax.ShapeDtypeStruct((TILES, 1, PAC...  26.2 us
    pallas_call x1, Pallas kernels, exchange_start(): pl.pallas_call(start_kernel, out_shape=(jax.ShapeDtypeStruct((GROUPS, 8,...  15.2 us
    pallas_call x1, Pallas kernels, stream(): pl.pallas_call(stream_kernel, out_shape=(jax.ShapeDtypeStruct((19, TILES,...  13.5 us
    pallas_call x1, Pallas kernels, collide(): pl.pallas_call(collide_kernel, out_shape=(jax.ShapeDtypeStruct((19, TILES...  11.8 us
    pallas_call x1, Pallas kernels, solve(): pl.pallas_call(solve_kernel, out_shape=(jax.ShapeDtypeStruct((BLOCK, BLOC...  11.4 us
    pallas_call x1, Pallas kernels, make_routes(): pl.pallas_call(kernel, out_shape=jax.ShapeDtypeStruct((rows, DEPTH), jnp....  4.49 us

profile of v3, /device:TPU:0, one launch (start us, length us, event | category | flops | bytes accessed | tf_op | source)
XLA Modules:
  0.0 153.2 jit_solution(11747525575917469043)
XLA Ops:
  0.6 0.0 copy-start.1
  0.6 0.7 tile.10
  1.4 0.1 tile.11
  1.5 1.2 copy.12.mask_ref
  2.7 0.0 copy-start.2
  2.7 1.0 copy-done.2
  3.7 15.2 %start.1 = (s32[16,8,128]{2,1,0:T(8,128)S(1)}, s32[42,48,128]{2,1,0:T(8,128)S(1)}) custom-call(s32[8,128]{1,0:T(8,128)S(1)} %fusion.3.ids_ref, s32[32,32,128]{2,1,0:T(8,128)S(1)} %copy-done.2), custom_call_target="tpu_custom_call" | custom-call | tf_op jit(solution)/shard_map/start/pallas_call | solution.py:139
  18.9 4.5 %owner_routes_kernel.1.table_ref.routes_ref = s32[16,128]{1,0:T(8,128)S(1)} custom-call(s32[1]{0:T(128)} %bitcast.me_ref, s32[16,8,128]{2,1,0:T(8,128)S(1)} %get-tuple-element.19.ids_ref), custom_call_target="tpu_custom_call" | custom-call | tf_op jit(solution)/shard_map/owner_routes_kernel/pallas_call | solution.py:367
  23.4 0.0 copy-start
  23.4 1.0 copy-done
  24.4 0.0 copy-start.3
  24.4 0.7 copy-done.3
  25.1 35.3 %source.1 = (f32[40,48,128]{2,1,0:T(8,128)S(1)}, s32[48,128]{1,0:T(8,128)S(1)}, f32[6,40,48,128]{3,2,1,0:T(8,128)S(1)}, f32[40,48,128]{2,1,0:T(8,128)S(1)}) custom-call(f32[4]{0:T(128)S(1)} %copy-done.3, s32[1]{0:T(128)} %bitcast.me_ref, s32[16,128]{1,0:T(8,128)S(1)} %owner_routes_kernel.1.table_ref.routes_ref, f32[4,16,16,128]{3,2,1,0:T(8,128)S(1)} %copy-done, ...), custom_call_target="tpu_custom_call" | custom-call | tf_op jit(solution)/shard_map/source/pallas_call | solution.py:556
  60.4 11.4 %solve.1 = (f32[32,32,128]{2,1,0:T(8,128)}, f32[4,24,16,128]{3,2,1,0:T(8,128)S(1)}) custom-call(f32[6,40,48,128]{3,2,1,0:T(8,128)S(1)} %get-tuple-element.22.coef, f32[40,48,128]{2,1,0:T(8,128)S(1)} %get-tuple-element.23.scale_ref, f32[40,48,128]{2,1,0:T(8,128)S(1)} %get-tuple-element.24.source_ref), custom_call_target="tpu_custom_call" | custom-call | tf_op jit(solution)/shard_map/solve/pallas_call | solution.py:816
  71.9 26.2 %back.1.pot_ref.rim_ref = f32[4,1,24,16,128]{4,3,2,1,0:T(8,128)S(1)} custom-call(s32[16,128]{1,0:T(8,128)S(1)} %owner_routes_kernel.1.table_ref.routes_ref, f32[4,24,16,128]{3,2,1,0:T(8,128)S(1)} %get-tuple-element.25.items_ref), custom_call_target="tpu_custom_call" | custom-call | tf_op jit(solution)/shard_map/back/pallas_call | solution.py:609
  98.1 0.0 copy-done.1
  98.1 11.8 %collide.1 = (f32[19,4,16,16,128]{4,3,2,1,0:T(8,128)S(1)}, f32[3,4,16,16,128]{4,3,2,1,0:T(8,128)S(1)}, f32[4,5,6,16,128]{4,3,2,1,0:T(8,128)S(1)}, f32[2,8,128]{2,1,0:T(8,128)S(1)}) custom-call(s32[48,128]{1,0:T(8,128)S(1)} %get-tuple-element.21.table_ref, s32[16,128]{1,0:T(8,128)S(1)} %owner_routes_kernel.1.table_ref.routes_ref, ...), custom_call_target="tpu_custom_call" | custom-call | tf_op jit(solution)/shard_map/collide/pallas_call | solution.py:952
  109.9 29.9 %faces.1 = (f32[4,5,6,16,128]{4,3,2,1,0:T(8,128)S(1)}, f32[3,16,2,8,128]{4,3,2,1,0:T(8,128)S(1)}) custom-call(s32[48,128]{1,0:T(8,128)S(1)} %get-tuple-element.21.table_ref, f32[4,5,6,16,128]{4,3,2,1,0:T(8,128)S(1)} %get-tuple-element.28.faces_ref, f32[2,8,128]{2,1,0:T(8,128)S(1)} %get-tuple-element.29.corners_ref), custom_call_target="tpu_custom_call" | custom-call | tf_op jit(solution)/shard_map/faces/pallas_call | solution.py:728
  139.8 13.5 %stream.1 = (f32[19,4,16,16,128]{4,3,2,1,0:T(8,128)}, f32[4,16,16,128]{3,2,1,0:T(8,128)}) custom-call(s32[48,128]{1,0:T(8,128)S(1)} %get-tuple-element.21.table_ref, s32[16,128]{1,0:T(8,128)S(1)} %owner_routes_kernel.1.table_ref.routes_ref, f32[19,4,16,16,128]{4,3,2,1,0:T(8,128)S(1)} %get-tuple-element.26.relaxed_ref, ...), custom_call_target="tpu_custom_call" | custom-call | tf_op jit(solution)/shard_map/stream/pallas_call | solution.py:1125
  (1 shorter events, 0.0 us)
Async XLA Ops:
  0.6 97.5 %copy-start.1 = (f32[4,16,16,128]{3,2,1,0:T(8,128)S(1)}, f32[4,16,16,128]{3,2,1,0:T(8,128)}, u32[]{:S(2)}) copy-start(f32[4,16,16,128]{3,2,1,0:T(8,128)} %charge_ref.5) | copy-start | bytes 1572868
  2.7 1.0 copy-start.2
  23.4 1.0 copy-start
  24.4 0.7 copy-start.3

commit v4 on v3

--- a/solution.py
+++ b/solution.py
@@ -11,6 +11,8 @@
 DEPTH = 128
 BLOCK = 32
 PHASES = 4
+SWEEPS = 4
+UNROLL = 2
 TILES = 4
 GROUPS = 16
 BANDS = 8
@@ -100,12 +102,10 @@
     pl.semaphore_wait(barrier, len(targets))
 
 
-def start_kernel(
-    ids_ref, phase_ref, all_ref, ext_ref, send_sem, recv_sem, ids_send, ids_recv, own_sem
-):
+def start_kernel(ids_ref, all_ref, ids_send, ids_recv, own_sem):
     me = lax.axis_index("gy")
     peers = [shifted_id(0, k) for k in range(1, GROUPS)]
-    greet(peers + [shifted_id(dx, dy) for dx, dy in AROUND if dx != 0])
+    greet(peers)
     started = []
     for k, target in enumerate(peers):
         copy = pltpu.make_async_remote_copy(
@@ -118,44 +118,27 @@
         )
         copy.start()
         started.append(copy)
-    for copy in halo_copies(phase_ref, ext_ref, 5, send_sem, recv_sem):
-        copy.start()
-        started.append(copy)
-    own = [
-        pltpu.make_async_copy(ids_ref, all_ref.at[me], own_sem.at[0]),
-        pltpu.make_async_copy(
-            phase_ref, ext_ref.at[pl.ds(5, BLOCK), pl.ds(SIDE, BLOCK)], own_sem.at[1]
-        ),
-    ]
-    for copy in own:
-        copy.start()
-    for copy in own + started:
+    own = pltpu.make_async_copy(ids_ref, all_ref.at[me], own_sem)
+    own.start()
+    own.wait()
+    for copy in started:
         copy.wait()
 
 
-def exchange_start(ids, phase):
+def exchange_start(ids):
     vmem = pl.BlockSpec(memory_space=pltpu.VMEM)
     dma = pltpu.SemaphoreType.DMA
     return pl.pallas_call(
         start_kernel,
-        out_shape=(
-            jax.ShapeDtypeStruct((GROUPS, 8, DEPTH), jnp.int32),
-            jax.ShapeDtypeStruct((BLOCK + 10, BLOCK + 2 * SIDE, DEPTH), jnp.int32),
-        ),
-        in_specs=[vmem, vmem],
-        out_specs=(vmem, vmem),
-        scratch_shapes=[
-            dma((8,)),
-            dma((8,)),
-            dma((GROUPS - 1,)),
-            dma((GROUPS - 1,)),
-            dma((2,)),
-        ],
+        out_shape=jax.ShapeDtypeStruct((GROUPS, 8, DEPTH), jnp.int32),
+        in_specs=[vmem],
+        out_specs=vmem,
+        scratch_shapes=[dma((GROUPS - 1,)), dma((GROUPS - 1,)), dma],
         compiler_params=pltpu.CompilerParams(
             collective_id=0, has_side_effects=True, vmem_limit_bytes=8 << 20
         ),
         name="start",
-    )(ids, phase)
+    )(ids)
 
 
 WIDE = BLOCK + 2 * SIDE
@@ -164,7 +147,7 @@
 INNER = pl.ds(8, WIDE)
 BEFORE = pl.ds(7, WIDE)
 AFTER = pl.ds(9, WIDE)
-PACK = 24
+PACK = 20
 
 
 def harmonic(left, right):
@@ -197,7 +180,79 @@
         scale_ref[i] = scale
         return above
 
-    lax.fori_loop(begin, end, weigh, harmonic(permit[begin], permit[begin + 1]))
+    lax.fori_loop(begin, end, weigh, harmonic(permit[begin], permit[begin + 1]), unroll=2)
+
+
+def tile_corner(t):
+    return 4 + (t // 2) * EDGE, SIDE + (t % 2) * EDGE
+
+
+def pack_rims(out, place, ref):
+    for t in range(TILES):
+        i0, j0 = tile_corner(t)
+
+        def rows(i, carry, t=t, i0=i0, j0=j0):
+            out[t, place + 2, pl.ds(i, 1)] = ref[i0 + i, pl.ds(j0 - 1, 1)]
+            out[t, place + 3, pl.ds(i, 1)] = ref[i0 + i, pl.ds(j0 + EDGE, 1)]
+            return carry
+
+        lax.fori_loop(0, EDGE, rows, 0, unroll=4)
+        out[t, place] = ref[i0 - 1, pl.ds(j0, EDGE)]
+        out[t, place + 1] = ref[i0 + EDGE, pl.ds(j0, EDGE)]
+
+
+def sweep_rows(coef, scale_ref, source_ref, pot_ref, pack, resid, upd_a, upd_b, total, between):
+    center = 0.5 * (spectrum_high + spectrum_low)
+    half = 0.5 * (spectrum_high - spectrum_low)
+    ratio = center / half
+
+    def begin(i, carry):
+        value = source_ref[i] * scale_ref[i]
+        resid[i] = value
+        value = value * (1.0 / center)
+        upd_a[i, INNER] = value
+        total[i] = value
+        return carry
+
+    lax.fori_loop(0, TALL, begin, 0, unroll=2)
+    rho = 1.0 / ratio
+    old, new = upd_a, upd_b
+    for sweep in range(SWEEPS - 1):
+        between(sweep + 1)
+        rho_new = 1.0 / (2.0 * ratio - rho)
+        keep, gain = rho_new * rho, 2.0 * rho_new / half
+
+        def relax(i, carry, old=old, new=new, keep=keep, gain=gain):
+            here = old[i, INNER]
+            near = coef[0, i] * old[i + 1, INNER] + coef[1, i] * old[i - 1, INNER]
+            near += coef[2, i] * old[i, AFTER] + coef[3, i] * old[i, BEFORE]
+            near += coef[4, i] * pltpu.roll(here, DEPTH - 1, 1)
+            near += coef[5, i] * pltpu.roll(here, 1, 1)
+            left = resid[i] - here + near
+            resid[i] = left
+            here = keep * here + gain * left
+            new[i, INNER] = here
+            total[i] = total[i] + here
+            return carry
+
+        lax.fori_loop(sweep + 1, TALL - 1 - sweep, relax, 0, unroll=UNROLL)
+        old, new = new, old
+        rho = rho_new
+
+    def emit(i, carry):
+        pot_ref[i] = total[i + 4, pl.ds(SIDE, BLOCK)]
+        return carry
+
+    lax.fori_loop(0, BLOCK, emit, 0, unroll=4)
+    for t in range(TILES):
+        i0, j0 = tile_corner(t)
+
+        def rows(i, carry, t=t, i0=i0, j0=j0):
+            pack[t, i] = total[i0 + i, pl.ds(j0, EDGE)]
+            return carry
+
+        lax.fori_loop(0, EDGE, rows, 0, unroll=4)
+    pack_rims(pack, EDGE, total)
 
 
 K_FIRST, K_X2, K_X3, K_X4, K_Y2, K_Y3, K_Y4, K_LAST = range(8)
@@ -457,38 +512,36 @@
 
 def source_kernel(
     permit_ref,
-    me_ref,
     table_ref,
     charge_ref,
     mask_ref,
     ids_ref,
     phase_ref,
+    pot_ref,
+    pack_ref,
+    others,
+    rims_ref,
+    rims,
     ext_ref,
-    face_ref,
     coef_ref,
     scale_ref,
-    others,
+    resid,
+    upd_a,
+    upd_b,
+    total,
+    phase_ext,
     permit,
     send_sem,
     recv_sem,
+    phase_send,
+    phase_recv,
     ids_send,
     ids_recv,
+    own_sem,
     *scratch,
 ):
     bands = [shifted_id(1, 0), shifted_id(-1, 0)]
     greet([ring(*peer)[2] for peer in RING_PEERS] + [shifted_id(dx, dy) for dx, dy in AROUND])
-    passed = []
-    for n, target in enumerate(bands):
-        copy = pltpu.make_async_remote_copy(
-            src_ref=ids_ref,
-            dst_ref=others.at[n],
-            send_sem=ids_send.at[n],
-            recv_sem=ids_recv.at[n],
-            device_id=target,
-            device_id_type=MESH,
-        )
-        copy.start()
-        passed.append(copy)
     part = EDGE // LANES
     lanes = []
     for n in range(LANES):
@@ -500,9 +553,11 @@
         lanes.append(
             Lane(n % 2, (TO_OWNER,), table_ref, first, scratch[16 * n : 16 * n + 16])
         )
-
-    def store(place, row):
-        face_ref[pl.ds(place, 1)] = row
+    passed = []
+    own = pltpu.make_async_copy(
+        phase_ref, phase_ext.at[pl.ds(5, BLOCK), pl.ds(SIDE, BLOCK)], own_sem
+    )
+    phases = halo_copies(phase_ref, phase_ext, 5, phase_send, phase_recv)
 
     def weights(begin, end):
         weigh_rows(begin, end, permit, coef_ref, scale_ref)
@@ -511,22 +566,30 @@
         for lane in lanes:
             lane.advance(stage)
         if stage == 0:
-            look_up_rows(permit_ref, phase_ref, permit)
+            for copy in phases:
+                copy.start()
+            own.start()
+            for n, target in enumerate(bands):
+                copy = pltpu.make_async_remote_copy(
+                    src_ref=ids_ref,
+                    dst_ref=others.at[n],
+                    send_sem=ids_send.at[n],
+                    recv_sem=ids_recv.at[n],
+                    device_id=target,
+                    device_id_type=MESH,
+                )
+                copy.start()
+                passed.append(copy)
+        elif stage == 1:
+            own.wait()
+            for copy in phases:
+                copy.wait_recv()
+            look_up_rows(permit_ref, phase_ext, permit)
             weights(0, 8)
-            for copy in passed:
-                copy.wait_recv()
-            tables = face_tables(
-                me_ref[0],
-                gathered_ids(ids_ref[...]),
-                gathered_ids(others[0]),
-                gathered_ids(others[1]),
-                store,
-            )
-            next(tables)
-        elif stage < 3:
-            next(tables, None)
+        elif stage == 2:
+            weights(8, 18)
         else:
-            weights(8, 24)
+            weights(18, 30)
     for n, lane in enumerate(lanes):
         lane.arrived()
         final = lane.stages[3][1]
@@ -539,16 +602,39 @@
     copies = halo_copies(block, ext_ref, 4, send_sem, recv_sem)
     for copy in copies:
         copy.start()
-    weights(24, TALL)
-    for copy in copies:
+    weights(30, TALL)
+    for copy in copies + passed:
         copy.wait()
-    for copy in passed:
+    for copy in phases:
         copy.wait_send()
-    for lane in lanes:
+    pack_rims(rims, 0, ext_ref)
+    returning = []
+    for n in range(2):
+
+        def first(_, slot, n=n):
+            return rims[slot, 2 * n : 2 * n + 2]
+
+        def final(here, n=n):
+            return rims_ref.at[here, :, pl.ds(2 * n, 2)]
+
+        refs = scratch[16 * (LANES + n) : 16 * (LANES + n) + 16]
+        returning.append(Lane(n, (TO_HOLDER,), table_ref, first, refs, final))
+
+    def between(stage):
+        for lane in returning:
+            lane.advance(stage)
+
+    between(0)
+    sweep_rows(
+        coef_ref, scale_ref, ext_ref, pot_ref, pack_ref, resid, upd_a, upd_b, total, between
+    )
+    for lane in returning:
+        lane.arrived()
+    for lane in lanes + returning:
         lane.close()
 
 
-def gather_source(permittivity, me, routes, charge, fluid_mask, ids, phase):
+def find_potential(permittivity, routes, charge, fluid_mask, ids, phase):
     vmem = pl.BlockSpec(memory_space=pltpu.VMEM)
     smem = pl.BlockSpec(memory_space=pltpu.SMEM)
     dma = pltpu.SemaphoreType.DMA
@@ -556,30 +642,45 @@
     return pl.pallas_call(
         source_kernel,
         out_shape=(
-            jax.ShapeDtypeStruct((TALL, WIDE, DEPTH), f32),
-            jax.ShapeDtypeStruct((48, DEPTH), jnp.int32),
-            jax.ShapeDtypeStruct((6, TALL, WIDE, DEPTH), f32),
-            jax.ShapeDtypeStruct((TALL, WIDE, DEPTH), f32),
+            jax.ShapeDtypeStruct((BLOCK, BLOCK, DEPTH), f32),
+            jax.ShapeDtypeStruct((TILES, PACK, EDGE, DEPTH), f32),
+            jax.ShapeDtypeStruct((2, GROUPS, 8, DEPTH), jnp.int32),
+            jax.ShapeDtypeStruct((TILES, 1, 4, EDGE, DEPTH), f32),
         ),
-        in_specs=[smem] * 3 + [vmem] * 4,
+        in_specs=[smem] * 2 + [vmem] * 4,
         out_specs=(vmem,) * 4,
         scratch_shapes=[
-            pltpu.VMEM((2, GROUPS, 8, DEPTH), jnp.int32),
+            pltpu.VMEM((TILES, 4, EDGE, DEPTH), f32),
+            pltpu.VMEM((TALL, WIDE, DEPTH), f32),
+            pltpu.VMEM((6, TALL, WIDE, DEPTH), f32),
+            pltpu.VMEM((TALL, WIDE, DEPTH), f32),
+            pltpu.VMEM((TALL, WIDE, DEPTH), f32),
+            pltpu.VMEM((TALL, ROOM, DEPTH), f32),
+            pltpu.VMEM((TALL, ROOM, DEPTH), f32),
+            pltpu.VMEM((TALL, WIDE, DEPTH), f32),
+            pltpu.VMEM((TALL + 2, WIDE, DEPTH), jnp.int32),
             pltpu.VMEM((TALL + 2, WIDE, DEPTH), f32),
+            dma((8,)),
+            dma((8,)),
             dma((8,)),
             dma((8,)),
             dma((2,)),
             dma((2,)),
+            dma,
         ]
-        + lane_scratch(1, (EDGE // LANES, EDGE, DEPTH)) * LANES,
+        + lane_scratch(1, (EDGE // LANES, EDGE, DEPTH)) * LANES
+        + lane_scratch(1, (2, EDGE, DEPTH)) * 2,
         compiler_params=pltpu.CompilerParams(
-            collective_id=1, has_side_effects=True, vmem_limit_bytes=24 << 20
+            collective_id=1, has_side_effects=True, vmem_limit_bytes=28 << 20
         ),
         name="source",
-    )(permittivity, me, routes, charge, fluid_mask, ids, phase)
-
-
-def back_kernel(table_ref, items_ref, out_ref, *scratch):
+    )(permittivity, routes, charge, fluid_mask, ids, phase)
+
+
+def back_kernel(me_ref, table_ref, items_ref, ids_ref, others_ref, out_ref, face_ref, *scratch):
+    def store(place, row):
+        face_ref[pl.ds(place, 1)] = row
+
     greet([ring(*peer)[2] for peer in RING_PEERS])
     part = PACK // LANES
     lanes = []
@@ -595,28 +696,42 @@
         lanes.append(
             Lane(n % 2, (TO_HOLDER,), table_ref, first, scratch[16 * n : 16 * n + 16], final)
         )
+    tables = None
     for stage in range(4):
         for lane in lanes:
             lane.advance(stage)
+        if stage == 0:
+            tables = face_tables(
+                me_ref[0],
+                gathered_ids(ids_ref[...]),
+                gathered_ids(others_ref[0]),
+                gathered_ids(others_ref[1]),
+                store,
+            )
+        next(tables, None)
     for lane in lanes:
         lane.arrived()
     for lane in lanes:
         lane.close()
 
 
-def send_back(routes, packed):
+def send_back(me, routes, packed, ids, others):
     vmem = pl.BlockSpec(memory_space=pltpu.VMEM)
+    smem = pl.BlockSpec(memory_space=pltpu.SMEM)
     return pl.pallas_call(
         back_kernel,
-        out_shape=jax.ShapeDtypeStruct((TILES, 1, PACK, EDGE, DEPTH), jnp.float32),
-        in_specs=[pl.BlockSpec(memory_space=pltpu.SMEM), vmem],
-        out_specs=vmem,
+        out_shape=(
+            jax.ShapeDtypeStruct((TILES, 1, PACK, EDGE, DEPTH), jnp.float32),
+            jax.ShapeDtypeStruct((48, DEPTH), jnp.int32),
+        ),
+        in_specs=[smem, smem, vmem, vmem, vmem],
+        out_specs=(vmem, vmem),
         scratch_shapes=lane_scratch(1, (PACK // LANES, EDGE, DEPTH)) * LANES,
         compiler_params=pltpu.CompilerParams(
             collective_id=2, has_side_effects=True, vmem_limit_bytes=24 << 20
         ),
         name="back",
-    )(routes, packed)
+    )(me, routes, packed, ids, others)
 
 
 FACES = 5
@@ -747,89 +862,6 @@
         ),
         name="faces",
     )(routes, faces, corners)
-
-
-def solve_kernel(
-    coef, scale_ref, source_ref, pot_ref, pack, resid, upd_a, upd_b, total
-):
-    center = 0.5 * (spectrum_high + spectrum_low)
-    half = 0.5 * (spectrum_high - spectrum_low)
-    ratio = center / half
-
-    def begin(i, carry):
-        value = source_ref[i] * scale_ref[i]
-        resid[i] = value
-        value = value * (1.0 / center)
-        upd_a[i, INNER] = value
-        total[i] = value
-        return carry
-
-    lax.fori_loop(0, TALL, begin, 0)
-
-    rho = 1.0 / ratio
-    old, new = upd_a, upd_b
-    for sweep in range(3):
-        rho_new = 1.0 / (2.0 * ratio - rho)
-        keep, gain = rho_new * rho, 2.0 * rho_new / half
-
-        def relax(i, carry, old=old, new=new, keep=keep, gain=gain):
-            here = old[i, INNER]
-            near = coef[0, i] * old[i + 1, INNER] + coef[1, i] * old[i - 1, INNER]
-            near += coef[2, i] * old[i, AFTER] + coef[3, i] * old[i, BEFORE]
-            near += coef[4, i] * pltpu.roll(here, DEPTH - 1, 1)
-            near += coef[5, i] * pltpu.roll(here, 1, 1)
-            left = resid[i] - here + near
-            resid[i] = left
-            here = keep * here + gain * left
-            new[i, INNER] = here
-            total[i] = total[i] + here
-            return carry
-
-        lax.fori_loop(sweep + 1, TALL - 1 - sweep, relax, 0)
-        old, new = new, old
-        rho = rho_new
-
-    def emit(i, carry):
-        pot_ref[i] = total[i + 4, pl.ds(SIDE, BLOCK)]
-        return carry
-
-    lax.fori_loop(0, BLOCK, emit, 0)
-    for t in range(TILES):
-        i0, j0 = 4 + (t // 2) * EDGE, SIDE + (t % 2) * EDGE
-
-        def rows(i, carry, t=t, i0=i0, j0=j0):
-            pack[t, i] = total[i0 + i, pl.ds(j0, EDGE)]
-            for place, ref in ((EDGE + 2, total), (EDGE + 6, source_ref)):
-                pack[t, place, pl.ds(i, 1)] = ref[i0 + i, pl.ds(j0 - 1, 1)]
-                pack[t, place + 1, pl.ds(i, 1)] = ref[i0 + i, pl.ds(j0 + EDGE, 1)]
-            return carry
-
-        lax.fori_loop(0, EDGE, rows, 0)
-        for place, ref in ((EDGE, total), (EDGE + 4, source_ref)):
-            pack[t, place] = ref[i0 - 1, pl.ds(j0, EDGE)]
-            pack[t, place + 1] = ref[i0 + EDGE, pl.ds(j0, EDGE)]
-
-
-def solve(coef, scale, source):
-    vmem = pl.BlockSpec(memory_space=pltpu.VMEM)
-    f32 = jnp.float32
-    return pl.pallas_call(
-        solve_kernel,
-        out_shape=(
-            jax.ShapeDtypeStruct((BLOCK, BLOCK, DEPTH), f32),
-            jax.ShapeDtypeStruct((TILES, PACK, EDGE, DEPTH), f32),
-        ),
-        in_specs=[vmem, vmem, vmem],
-        out_specs=(vmem, vmem),
-        scratch_shapes=[
-            pltpu.VMEM((TALL, WIDE, DEPTH), f32),
-            pltpu.VMEM((TALL, ROOM, DEPTH), f32),
-            pltpu.VMEM((TALL, ROOM, DEPTH), f32),
-            pltpu.VMEM((TALL, WIDE, DEPTH), f32),
-        ],
-        compiler_params=pltpu.CompilerParams(vmem_limit_bytes=32 << 20),
-        name="solve",
-    )(coef, scale, source)
 
 
 def collide_rows(pops, charge, field):
@@ -979,6 +1011,12 @@
     )(table, routes, populations, charge, fluid_mask, returned)
 
 
+CHARGE, SPEED = 19, 20
+SOLID = 3.0e38
+FIRST = 8 + EDGE
+STRIP = 8 + (EDGE + 2) * EDGE + 8
+
+
 def stream_kernel(
     table_ref,
     routes_ref,
@@ -989,128 +1027,131 @@
     rim_ref,
     *rest,
 ):
-    faces, (corner_ref, pops_out, charge_out, xrim, yrim, corner) = rest[:FACES], rest[FACES:]
+    faces, (corner_ref, pops_out, charge_out, grown, side, sems) = rest[:FACES], rest[FACES:]
     tile = pl.program_id(0)
+    here = lax.rem(tile, 2)
+
+    def fetch(t, slot):
+        rows = pl.ds(FIRST, EDGE * EDGE)
+        return [
+            pltpu.make_async_copy(
+                relaxed_ref.at[:, t], grown.at[slot, pl.ds(0, 19), rows], sems.at[slot, 0]
+            ),
+            pltpu.make_async_copy(
+                charge_ref.at[t], grown.at[slot, CHARGE, rows], sems.at[slot, 1]
+            ),
+            pltpu.make_async_copy(
+                vel_ref.at[:, t], grown.at[slot, pl.ds(SPEED, 3), rows], sems.at[slot, 2]
+            ),
+        ]
+
+    @pl.when(tile == 0)
+    def _():
+        for copy in fetch(0, 0):
+            copy.start()
+
+    @pl.when(tile + 1 < TILES)
+    def _():
+        for copy in fetch(tile + 1, 1 - here):
+            copy.start()
+
+    for copy in fetch(tile, here):
+        copy.wait()
+
+    cells = grown.at[here]
+    before, after = pl.ds(8, EDGE), pl.ds(FIRST + EDGE * EDGE, EDGE)
+
+    def x_rim(face, sign, rows):
+        for k, q in enumerate(crossing(0, sign) + [SPEED]):
+            cells[q, rows] = faces[face][0, 0, k]
+
     row = table_ref[R_ROW, tile]
-    plus = [crossing(0, 1), crossing(1, 1)]
-    minus = [crossing(0, -1), crossing(1, -1)]
-
-    def fill(out, face):
-        for k in range(6):
-            out[k] = faces[face][0, 0, k]
-
-    fill(yrim.at[0], 0)
-    fill(yrim.at[1], 1)
-    for n, (side, end, which) in enumerate(((0, 0, 0), (0, 1, 1), (1, 0, 2), (1, 1, 3))):
-        found = table_ref[R_CORNER + n, tile]
-        tile_in = lax.rem(found, TILES)
-        corner[side, pl.ds(end, 1)] = corner_ref[
-            found // TILES, tile_in // 2, pl.ds(lax.rem(tile_in, 2) * 4 + which, 1)
-        ]
 
     @pl.when(row == 0)
     def _():
-        fill(xrim.at[0], 3)
-        fill(xrim.at[1], 2)
+        x_rim(BELOW_X, 1, before)
+        x_rim(SAME_X, -1, after)
 
     @pl.when(row == 1)
     def _():
-        fill(xrim.at[0], 2)
-        fill(xrim.at[1], 4)
-
-    place = lax.broadcasted_iota(jnp.int32, (EDGE, DEPTH), 0)
-    first, last = place == 0, place == EDGE - 1
-
-    def rows(i, low_edge, high_edge):
-        own = mask_ref[0, i + 1, pl.ds(1, EDGE), :]
+        x_rim(SAME_X, 1, before)
+        x_rim(ABOVE_X, -1, after)
+
+    cells[CHARGE, before] = rim_ref[0, 0, 0]
+    cells[CHARGE, after] = rim_ref[0, 0, 1]
+    for face, sign, end in ((UP_Y, 1, 0), (DOWN_Y, -1, 1)):
+        for k, q in enumerate(crossing(1, sign)):
+            side[end, k, pl.ds(1, EDGE)] = faces[face][0, 0, k]
+        side[end, 5, pl.ds(1, EDGE)] = faces[face][0, 0, 5]
+        side[end, 6, pl.ds(1, EDGE)] = rim_ref[0, 0, 2 + end]
+    for n, (q, sign, layer) in enumerate(((7, 1, 0), (9, -1, 0), (10, 1, 17), (8, -1, 17))):
+        found = table_ref[R_CORNER + n, tile]
+        inside = lax.rem(found, TILES)
+        side[n % 2, crossing(1, sign).index(q), pl.ds(layer, 1)] = corner_ref[
+            found // TILES, inside // 2, pl.ds(lax.rem(inside, 2) * 4 + n, 1)
+        ]
+    spot = lax.broadcasted_iota(jnp.int32, (EDGE, DEPTH), 0)
+    ends = {-1: spot == 0, 1: spot == EDGE - 1}
+
+    def rows(i, carry):
+        def cell(q, di=0, dj=0):
+            value = cells[q, pl.ds(i * EDGE + (FIRST + di * EDGE + dj), EDGE)]
+            if dj == 0:
+                return value
+            if q < 19:
+                k = crossing(1, -dj).index(q)
+            else:
+                k = 6 if q == CHARGE else 5
+            return jnp.where(ends[dj], side[(dj + 1) // 2, k, pl.ds(i + 1 + di, 1)], value)
+
+        def flag(di=0, dj=0):
+            return mask_ref[0, i + 1 + di, pl.ds(1 + dj, EDGE), :]
+
+        own = flag()
         own_fluid = own == 1
         for q in range(19):
             step_x, step_y, step_z = LATTICE[q]
-            value_here = relaxed_ref[q, 0, i]
+            value = cell(q)
             if q == 0:
-                pops_out[q, 0, i] = value_here
+                pops_out[q, 0, i] = value
                 continue
-            side = None
-            if step_x == 1 and low_edge:
-                side, channel = 0, plus[0].index(q)
-            if step_x == -1 and high_edge:
-                side, channel = 1, minus[0].index(q)
-            if side is None:
-                moved = value_here if step_x == 0 else relaxed_ref[q, 0, i - step_x]
-            else:
-                moved = xrim[side, channel]
-            if step_y == 1:
-                if side is None:
-                    edge = yrim[0, plus[1].index(q), pl.ds(i - step_x, 1)]
-                else:
-                    edge = corner[side, pl.ds(0, 1)]
-                moved = jnp.where(first, edge, pltpu.roll(moved, 1, 0))
-            elif step_y == -1:
-                if side is None:
-                    edge = yrim[1, minus[1].index(q), pl.ds(i - step_x, 1)]
-                else:
-                    edge = corner[side, pl.ds(1, 1)]
-                moved = jnp.where(last, edge, pltpu.roll(moved, EDGE - 1, 0))
-            from_fluid = mask_ref[0, i + 1 - step_x, pl.ds(1 - step_y, EDGE), :]
+            moved = cell(q, -step_x, -step_y)
+            from_fluid = flag(-step_x, -step_y) == 1
             if step_z != 0:
-                moved = pltpu.roll(moved, step_z % DEPTH, 1)
-                from_fluid = pltpu.roll(from_fluid, step_z % DEPTH, 1)
-            bounced = relaxed_ref[opposite(q), 0, i]
-            read = jnp.where(from_fluid == 1, moved, bounced)
-            pops_out[q, 0, i] = jnp.where(own_fluid, read, value_here)
-
-        charge = charge_ref[0, i]
-        flag = own.astype(jnp.float32)
+                moved = pltpu.roll(jnp.where(from_fluid, moved, SOLID), step_z % DEPTH, 1)
+                from_fluid = moved < SOLID
+            read = jnp.where(from_fluid, moved, cell(opposite(q)))
+            pops_out[q, 0, i] = jnp.where(own_fluid, read, value)
+
+        charge = cell(CHARGE)
+        weight = own.astype(jnp.float32)
 
         def flux(speed_a, speed_b, value_a, value_b, flags):
             speed = 0.5 * (speed_a + speed_b)
             return speed * jnp.where(speed > 0, value_a, value_b) * flags
 
-        speed = vel_ref[0, 0, i]
-        if low_edge:
-            other, other_speed = rim_ref[0, 0, 0], xrim[0, 5]
-        else:
-            other, other_speed = charge_ref[0, i - 1], vel_ref[0, 0, i - 1]
-        other_flag = mask_ref[0, i, pl.ds(1, EDGE), :].astype(jnp.float32)
-        change = -flux(other_speed, speed, other, charge, other_flag * flag)
-        if high_edge:
-            other, other_speed = rim_ref[0, 0, 1], xrim[1, 5]
-        else:
-            other, other_speed = charge_ref[0, i + 1], vel_ref[0, 0, i + 1]
-        other_flag = mask_ref[0, i + 2, pl.ds(1, EDGE), :].astype(jnp.float32)
-        change += flux(speed, other_speed, charge, other, flag * other_flag)
-
-        speed = vel_ref[1, 0, i]
-        other = jnp.where(first, rim_ref[0, 0, 2, pl.ds(i, 1)], pltpu.roll(charge, 1, 0))
-        other_speed = jnp.where(first, yrim[0, 5, pl.ds(i, 1)], pltpu.roll(speed, 1, 0))
-        other_flag = mask_ref[0, i + 1, pl.ds(0, EDGE), :].astype(jnp.float32)
-        change -= flux(other_speed, speed, other, charge, other_flag * flag)
-        other = jnp.where(last, rim_ref[0, 0, 3, pl.ds(i, 1)], pltpu.roll(charge, EDGE - 1, 0))
-        other_speed = jnp.where(
-            last, yrim[1, 5, pl.ds(i, 1)], pltpu.roll(speed, EDGE - 1, 0)
-        )
-        other_flag = mask_ref[0, i + 1, pl.ds(2, EDGE), :].astype(jnp.float32)
-        change += flux(speed, other_speed, charge, other, flag * other_flag)
-
-        speed = vel_ref[2, 0, i]
-        over = flux(
-            speed,
-            pltpu.roll(speed, DEPTH - 1, 1),
-            charge,
-            pltpu.roll(charge, DEPTH - 1, 1),
-            flag * pltpu.roll(flag, DEPTH - 1, 1),
-        )
-        change += over - pltpu.roll(over, 1, 1)
+        change = None
+        for d, (di, dj) in enumerate(((1, 0), (0, 1))):
+            speed = cell(SPEED + d)
+            for sign in (1, -1):
+                other = cell(CHARGE, sign * di, sign * dj)
+                other_speed = cell(SPEED + d, sign * di, sign * dj)
+                flags = weight * flag(sign * di, sign * dj).astype(jnp.float32)
+                if sign > 0:
+                    part = flux(speed, other_speed, charge, other, flags)
+                    change = part if change is None else change + part
+                else:
+                    change = change - flux(other_speed, speed, other, charge, flags)
+        speed = cell(SPEED + 2)
+        next_charge = pltpu.roll(jnp.where(own_fluid, charge, SOLID), DEPTH - 1, 1)
+        middle = 0.5 * (speed + pltpu.roll(speed, DEPTH - 1, 1))
+        over = middle * jnp.where(middle > 0, charge, next_charge)
+        over = jnp.where(own_fluid & (next_charge < SOLID), over, 0.0)
+        change = change + over - pltpu.roll(over, 1, 1)
         charge_out[0, i] = jnp.where(own_fluid, charge - change, charge)
-
-    rows(0, True, False)
-
-    def middle(i, carry):
-        rows(i, False, False)
         return carry
 
-    lax.fori_loop(1, EDGE - 1, middle, 0)
-    rows(EDGE - 1, False, True)
+    lax.fori_loop(0, EDGE, rows, 0, unroll=2)
 
 
 def stream(table, routes, relaxed, velocity, charge, fluid_mask, returned, faces, corners):
@@ -1122,6 +1163,7 @@
         )
         for face in range(FACES)
     ]
+    anywhere = pl.BlockSpec(memory_space=pl.ANY)
     return pl.pallas_call(
         stream_kernel,
         out_shape=(
@@ -1132,12 +1174,13 @@
             num_scalar_prefetch=2,
             grid=(TILES,),
             in_specs=[
-                pl.BlockSpec((19, 1, EDGE, EDGE, DEPTH), lambda s, tab, rts: (0, s, 0, 0, 0)),
-                pl.BlockSpec((3, 1, EDGE, EDGE, DEPTH), lambda s, tab, rts: (0, s, 0, 0, 0)),
-                pl.BlockSpec((1, EDGE, EDGE, DEPTH), lambda s, tab, rts: (s, 0, 0, 0)),
+                anywhere,
+                anywhere,
+                anywhere,
                 pl.BlockSpec((1, EDGE + 2, EDGE + 2, DEPTH), lambda s, tab, rts: (s, 0, 0, 0)),
                 pl.BlockSpec(
-                    (1, 1, 4, EDGE, DEPTH), lambda s, tab, rts: (rts[TO_HOLDER * 8 + K_LAST, s], 0, 5, 0, 0)
+                    (1, 1, 4, EDGE, DEPTH),
+                    lambda s, tab, rts: (rts[TO_HOLDER * 8 + K_LAST, s], 0, 0, 0, 0),
                 ),
             ]
             + face_specs
@@ -1147,9 +1190,9 @@
                 pl.BlockSpec((1, EDGE, EDGE, DEPTH), lambda s, tab, rts: (s, 0, 0, 0)),
             ],
             scratch_shapes=[
-                pltpu.VMEM((2, 6, EDGE, DEPTH), f32),
-                pltpu.VMEM((2, 6, EDGE, DEPTH), f32),
-                pltpu.VMEM((2, 8, DEPTH), f32),
+                pltpu.VMEM((2, 23, STRIP, DEPTH), f32),
+                pltpu.VMEM((2, 7, 24, DEPTH), f32),
+                pltpu.SemaphoreType.DMA((2, 3)),
             ],
         ),
         compiler_params=pltpu.CompilerParams(vmem_limit_bytes=32 << 20),
@@ -1157,9 +1200,9 @@
     )(
         table,
         routes,
-        relaxed,
-        velocity,
-        charge,
+        relaxed.reshape(19, TILES, EDGE * EDGE, DEPTH),
+        velocity.reshape(3, TILES, EDGE * EDGE, DEPTH),
+        charge.reshape(TILES, EDGE * EDGE, DEPTH),
         fluid_mask,
         returned,
         *([faces] * FACES),
@@ -1171,19 +1214,18 @@
     me = lax.axis_index("gy").astype(jnp.int32).reshape(1)
     place = jnp.arange(8 * DEPTH, dtype=jnp.int32).reshape(8, DEPTH)
     ids_row = jnp.where(place // TILES == me, jnp.tile(tile_ids, 2 * DEPTH).reshape(8, DEPTH), 0)
-    ids, phase_ext = exchange_start(ids_row, phase_label)
+    ids = exchange_start(ids_row)
     routes = make_routes(owner_routes_kernel, 16, me, ids)
-    source_ext, table, coef, scale = gather_source(
-        permittivity, me, routes, charge, fluid_mask, ids, phase_ext
+    potential, packed, others, charge_rims = find_potential(
+        permittivity, routes, charge, fluid_mask, ids, phase_label
     )
-    potential, packed = solve(coef, scale, source_ext)
-    returned = send_back(routes, packed)
+    returned, table = send_back(me, routes, packed, ids, others)
     relaxed, velocity, faces, corners = collide(
         table, routes, populations, charge, fluid_mask, returned
     )
     rims, all_corners = send_faces(table, faces, corners)
     populations_next, charge_next = stream(
-        table, routes, relaxed, velocity, charge, fluid_mask, returned, rims, all_corners
+        table, routes, relaxed, velocity, charge, fluid_mask, charge_rims, rims, all_corners
     )
     return (populations_next, charge_next, potential)
 

time: 154 us -> 148 us (0.961)
  Pallas kernels: 148 us -> 140 us
  local copies, waits for them, and re-layouts: 4.72 us -> 6.5 us
    pallas_call x4 -> x3, Pallas kernels: 88.2 us -> 83.7 us  [the longest x1 49.4 us: find_potential(): pl.pallas_call(source_kernel, out_shape=(jax.ShapeDtypeStruct((BLOCK, BLO...]
    pallas_call x1, Pallas kernels: 13.5 us -> 9.97 us  [stream(): pl.pallas_call(stream_kernel, out_shape=(jax.ShapeDtypeStruct((19, TILES,...]
    unnamed x9 -> x10, local copies, waits for them, and re-layouts: 3.91 us -> 5.74 us
where the time goes in v4:
time: 148 us
  Pallas kernels  140 us (95%)
  local copies, waits for them, and re-layouts  6.5 us (4%)
    pallas_call x1, Pallas kernels, find_potential(): pl.pallas_call(source_kernel, out_shape=(jax.ShapeDtypeStruct((BLOCK, BLO...  49.4 us
    pallas_call x1, Pallas kernels, send_faces(): pl.pallas_call(faces_kernel, out_shape=(jax.ShapeDtypeStruct((TILES, FACE...  30.4 us
    pallas_call x1, Pallas kernels, send_back(): pl.pallas_call(back_kernel, out_shape=(jax.ShapeDtypeStruct((TILES, 1, PA...  24.5 us
    pallas_call x1, Pallas kernels, collide(): pl.pallas_call(collide_kernel, out_shape=(jax.ShapeDtypeStruct((19, TILES...  11.8 us
    pallas_call x1, Pallas kernels, stream(): pl.pallas_call(stream_kernel, out_shape=(jax.ShapeDtypeStruct((19, TILES,...  9.97 us
    pallas_call x1, Pallas kernels, exchange_start(): pl.pallas_call(start_kernel, out_shape=jax.ShapeDtypeStruct((GROUPS, 8, D...  9.88 us
    unnamed x10, local copies, waits for them, and re-layouts  5.74 us
    pallas_call x1, Pallas kernels, make_routes(): pl.pallas_call(kernel, out_shape=jax.ShapeDtypeStruct((rows, DEPTH), jnp....  4.49 us

profile of v4, /device:TPU:0, one launch (start us, length us, event | category | flops | bytes accessed | tf_op | source)
XLA Modules:
  0.0 147.5 jit_solution(16167586272352555433)
XLA Ops:
  0.6 0.7 tile.10
  1.3 0.1 tile.11
  1.4 9.9 %start.1.ids_ref = s32[16,8,128]{2,1,0:T(8,128)S(1)} custom-call(s32[8,128]{1,0:T(8,128)S(1)} %fusion.3.ids_ref), custom_call_target="tpu_custom_call" | custom-call | tf_op jit(solution)/shard_map/start/pallas_call | solution.py:131
  11.3 4.5 %owner_routes_kernel.1.table_ref.routes_ref = s32[16,128]{1,0:T(8,128)S(1)} custom-call(s32[1]{0:T(128)} %bitcast.me_ref, s32[16,8,128]{2,1,0:T(8,128)S(1)} %start.1.ids_ref), custom_call_target="tpu_custom_call" | custom-call | tf_op jit(solution)/shard_map/owner_routes_kernel/pallas_call | solution.py:422
  15.8 1.2 copy.12.mask_ref
  17.0 0.0 copy-start
  17.0 1.0 copy-done
  18.0 0.0 copy-start.2
  18.0 1.0 copy-done.2
  19.1 0.0 copy-start.3
  19.1 0.7 copy-done.3
  19.7 49.4 %source.1 = (f32[32,32,128]{2,1,0:T(8,128)S(1)}, f32[4,20,16,128]{3,2,1,0:T(8,128)S(1)}, s32[2,16,8,128]{3,2,1,0:T(8,128)S(1)}, f32[4,1,4,16,128]{4,3,2,1,0:T(8,128)S(1)}) custom-call(f32[4]{0:T(128)S(1)} %copy-done.3, s32[16,128]{1,0:T(8,128)S(1)} %owner_routes_kernel.1.table_ref.routes_ref, f32[4,16,16,128]{3,2,1,0:T(8,128)S(1)} %copy-done, ...), custom_call_target="tpu_custom_call" | custom-call | tf_op jit(solution)/shard_map/source/pallas_call | solution.py:642
  69.1 24.5 %back.1 = (f32[4,1,20,16,128]{4,3,2,1,0:T(8,128)S(1)}, s32[48,128]{1,0:T(8,128)S(1)}) custom-call(s32[1]{0:T(128)} %bitcast.me_ref, s32[16,128]{1,0:T(8,128)S(1)} %owner_routes_kernel.1.table_ref.routes_ref, f32[4,20,16,128]{3,2,1,0:T(8,128)S(1)} %get-tuple-element.17.items_ref, s32[16,8,128]{2,1,0:T(8,128)S(1)} %start.1.ids_ref, ...), custom_call_target="tpu_custom_call" | custom-call | tf_op jit(solution)/shard_map/back/pallas_call | solution.py:721
  93.6 0.0 copy-start.1
  93.6 1.0 copy-done.1
  94.6 11.8 %collide.1 = (f32[19,4,16,16,128]{4,3,2,1,0:T(8,128)S(1)}, f32[3,4,16,16,128]{4,3,2,1,0:T(8,128)S(1)}, f32[4,5,6,16,128]{4,3,2,1,0:T(8,128)S(1)}, f32[2,8,128]{2,1,0:T(8,128)S(1)}) custom-call(s32[48,128]{1,0:T(8,128)S(1)} %get-tuple-element.19.table_ref, s32[16,128]{1,0:T(8,128)S(1)} %owner_routes_kernel.1.table_ref.routes_ref, ...), custom_call_target="tpu_custom_call" | custom-call | tf_op jit(solution)/shard_map/collide/pallas_call | solution.py:984
  106.4 30.4 %faces.1 = (f32[4,5,6,16,128]{4,3,2,1,0:T(8,128)S(1)}, f32[3,16,2,8,128]{4,3,2,1,0:T(8,128)S(1)}) custom-call(s32[48,128]{1,0:T(8,128)S(1)} %get-tuple-element.19.table_ref, f32[4,5,6,16,128]{4,3,2,1,0:T(8,128)S(1)} %get-tuple-element.24.faces_ref, f32[2,8,128]{2,1,0:T(8,128)S(1)} %get-tuple-element.25.corners_ref), custom_call_target="tpu_custom_call" | custom-call | tf_op jit(solution)/shard_map/faces/pallas_call | solution.py:843
  136.8 10.0 %stream.1 = (f32[19,4,16,16,128]{4,3,2,1,0:T(8,128)}, f32[4,16,16,128]{3,2,1,0:T(8,128)}) custom-call(s32[48,128]{1,0:T(8,128)S(1)} %get-tuple-element.19.table_ref, s32[16,128]{1,0:T(8,128)S(1)} %owner_routes_kernel.1.table_ref.routes_ref, f32[19,4,256,128]{3,2,1,0:T(8,128)S(1)} %bitcast.5, f32[3,4,256,128]{3,2,1,0:T(8,128)S(1)} %bitcast.7, ...), custom_call_target="tpu_custom_call" | custom-call | tf_op jit(solution)/shard_map/stream/pallas_call | solution.py:1167
  146.7 0.8 copy.16
  (1 shorter events, 0.0 us)
Async XLA Ops:
  17.0 1.0 copy-start
  18.0 1.0 copy-start.2
  19.1 0.7 copy-start.3
  93.6 1.0 copy-start.1

commit v5 on v4

--- a/solution.py
+++ b/solution.py
@@ -148,6 +148,7 @@
 BEFORE = pl.ds(7, WIDE)
 AFTER = pl.ds(9, WIDE)
 PACK = 20
+FACES = 5
 
 
 def harmonic(left, right):
@@ -513,14 +514,17 @@
 def source_kernel(
     permit_ref,
     table_ref,
-    charge_ref,
-    mask_ref,
+    charge_hbm,
+    mask_hbm,
     ids_ref,
     phase_ref,
     pot_ref,
     pack_ref,
     others,
     rims_ref,
+    charge_ref,
+    mask_ref,
+    fetch_sem,
     rims,
     ext_ref,
     coef_ref,
@@ -541,7 +545,18 @@
     *scratch,
 ):
     bands = [shifted_id(1, 0), shifted_id(-1, 0)]
+    fetches = [
+        pltpu.make_async_copy(charge_hbm, charge_ref, fetch_sem.at[0]),
+        pltpu.make_async_copy(mask_hbm, mask_ref, fetch_sem.at[1]),
+        pltpu.make_async_copy(
+            phase_ref, phase_ext.at[pl.ds(5, BLOCK), pl.ds(SIDE, BLOCK)], own_sem
+        ),
+    ]
+    for copy in fetches:
+        copy.start()
     greet([ring(*peer)[2] for peer in RING_PEERS] + [shifted_id(dx, dy) for dx, dy in AROUND])
+    for copy in fetches:
+        copy.wait()
     part = EDGE // LANES
     lanes = []
     for n in range(LANES):
@@ -554,9 +569,6 @@
             Lane(n % 2, (TO_OWNER,), table_ref, first, scratch[16 * n : 16 * n + 16])
         )
     passed = []
-    own = pltpu.make_async_copy(
-        phase_ref, phase_ext.at[pl.ds(5, BLOCK), pl.ds(SIDE, BLOCK)], own_sem
-    )
     phases = halo_copies(phase_ref, phase_ext, 5, phase_send, phase_recv)
 
     def weights(begin, end):
@@ -568,7 +580,6 @@
         if stage == 0:
             for copy in phases:
                 copy.start()
-            own.start()
             for n, target in enumerate(bands):
                 copy = pltpu.make_async_remote_copy(
                     src_ref=ids_ref,
@@ -581,7 +592,6 @@
                 copy.start()
                 passed.append(copy)
         elif stage == 1:
-            own.wait()
             for copy in phases:
                 copy.wait_recv()
             look_up_rows(permit_ref, phase_ext, permit)
@@ -637,6 +647,7 @@
 def find_potential(permittivity, routes, charge, fluid_mask, ids, phase):
     vmem = pl.BlockSpec(memory_space=pltpu.VMEM)
     smem = pl.BlockSpec(memory_space=pltpu.SMEM)
+    anywhere = pl.BlockSpec(memory_space=pltpu.HBM)
     dma = pltpu.SemaphoreType.DMA
     f32 = jnp.float32
     return pl.pallas_call(
@@ -646,10 +657,13 @@
             jax.ShapeDtypeStruct((TILES, PACK, EDGE, DEPTH), f32),
             jax.ShapeDtypeStruct((2, GROUPS, 8, DEPTH), jnp.int32),
             jax.ShapeDtypeStruct((TILES, 1, 4, EDGE, DEPTH), f32),
+            jax.ShapeDtypeStruct((TILES, EDGE, EDGE, DEPTH), f32),
+            jax.ShapeDtypeStruct((TILES, EDGE + 2, EDGE + 2, DEPTH), jnp.int32),
         ),
-        in_specs=[smem] * 2 + [vmem] * 4,
-        out_specs=(vmem,) * 4,
+        in_specs=[smem] * 2 + [anywhere, anywhere, vmem, anywhere],
+        out_specs=(vmem,) * 6,
         scratch_shapes=[
+            dma((2,)),
             pltpu.VMEM((TILES, 4, EDGE, DEPTH), f32),
             pltpu.VMEM((TALL, WIDE, DEPTH), f32),
             pltpu.VMEM((6, TALL, WIDE, DEPTH), f32),
@@ -677,7 +691,26 @@
     )(permittivity, routes, charge, fluid_mask, ids, phase)
 
 
-def back_kernel(me_ref, table_ref, items_ref, ids_ref, others_ref, out_ref, face_ref, *scratch):
+def back_kernel(
+    me_ref,
+    table_ref,
+    items_ref,
+    ids_ref,
+    others_ref,
+    pops_hbm,
+    out_ref,
+    face_ref,
+    pops_ref,
+    pops_sem,
+    *scratch,
+):
+    fetches = [
+        pltpu.make_async_copy(pops_hbm.at[:, t], pops_ref.at[:, t], pops_sem.at[t])
+        for t in range(TILES)
+    ]
+    for copy in fetches:
+        copy.start()
+
     def store(place, row):
         face_ref[pl.ds(place, 1)] = row
 
@@ -713,9 +746,11 @@
         lane.arrived()
     for lane in lanes:
         lane.close()
-
-
-def send_back(me, routes, packed, ids, others):
+    for copy in fetches:
+        copy.wait()
+
+
+def send_back(me, routes, packed, ids, others, populations):
     vmem = pl.BlockSpec(memory_space=pltpu.VMEM)
     smem = pl.BlockSpec(memory_space=pltpu.SMEM)
     return pl.pallas_call(
@@ -723,145 +758,17 @@
         out_shape=(
             jax.ShapeDtypeStruct((TILES, 1, PACK, EDGE, DEPTH), jnp.float32),
             jax.ShapeDtypeStruct((48, DEPTH), jnp.int32),
+            jax.ShapeDtypeStruct((19, TILES, EDGE, EDGE, DEPTH), jnp.float32),
         ),
-        in_specs=[smem, smem, vmem, vmem, vmem],
-        out_specs=(vmem, vmem),
-        scratch_shapes=lane_scratch(1, (PACK // LANES, EDGE, DEPTH)) * LANES,
+        in_specs=[smem, smem, vmem, vmem, vmem, pl.BlockSpec(memory_space=pltpu.HBM)],
+        out_specs=(vmem, vmem, vmem),
+        scratch_shapes=[pltpu.SemaphoreType.DMA((TILES,))]
+        + lane_scratch(1, (PACK // LANES, EDGE, DEPTH)) * LANES,
         compiler_params=pltpu.CompilerParams(
-            collective_id=2, has_side_effects=True, vmem_limit_bytes=24 << 20
+            collective_id=2, has_side_effects=True, vmem_limit_bytes=40 << 20
         ),
         name="back",
-    )(me, routes, packed, ids, others)
-
-
-FACES = 5
-
-
-FACE_LANES = (
-    (0, (UP_Y, DOWN_Y, SAME_X)),
-    (1, (UP_Y, DOWN_Y, SAME_X)),
-    (0, (BELOW_X, ABOVE_X)),
-    (1, (BELOW_X, ABOVE_X)),
-)
-
-
-def faces_kernel(
-    table_ref,
-    faces_ref,
-    corners_ref,
-    out_ref,
-    all_ref,
-    shifted,
-    corner_send,
-    corner_recv,
-    shift_send,
-    shift_recv,
-    own_sem,
-    *scratch,
-):
-    me = lax.axis_index("gy")
-    peers = [shifted_id(0, k) for k in range(1, GROUPS)]
-    bands = [shifted_id(1, 0), shifted_id(-1, 0)]
-    greet(peers + bands)
-    shifts = []
-    for n, target in enumerate(bands):
-        copy = pltpu.make_async_remote_copy(
-            src_ref=faces_ref.at[:, 3 + n],
-            dst_ref=shifted.at[n],
-            send_sem=shift_send.at[n],
-            recv_sem=shift_recv.at[n],
-            device_id=target,
-            device_id_type=MESH,
-        )
-        copy.start()
-        shifts.append(copy)
-    lanes = []
-    for n, (order, perms) in enumerate(FACE_LANES):
-        rows = slice(order * 3, order * 3 + 3)
-
-        def first(k, slot, perms=perms, rows=rows):
-            if perms[k] < BELOW_X:
-                return faces_ref[slot, perms[k], rows]
-            return shifted[perms[k] - BELOW_X, slot, rows]
-
-        def final(here, perms=perms, order=order):
-            return out_ref.at[here, pl.ds(perms[0], len(perms)), pl.ds(order * 3, 3)]
-
-        lanes.append(Lane(order, perms, table_ref, first, scratch[16 * n : 16 * n + 16], final))
-    spread_out, forward = [], []
-    own = pltpu.make_async_copy(corners_ref, all_ref.at[0, me], own_sem)
-    for stage in range(4):
-        for n, lane in enumerate(lanes):
-            if stage == 0 and n == 2:
-                for k, target in enumerate(peers):
-                    copy = pltpu.make_async_remote_copy(
-                        src_ref=corners_ref,
-                        dst_ref=all_ref.at[0, me],
-                        send_sem=corner_send.at[k],
-                        recv_sem=corner_recv.at[k],
-                        device_id=target,
-                        device_id_type=MESH,
-                    )
-                    copy.start()
-                    spread_out.append(copy)
-                own.start()
-                for copy in shifts:
-                    copy.wait_recv()
-            lane.advance(stage)
-        if stage == 1:
-            own.wait()
-            for copy in spread_out:
-                copy.wait_recv()
-            for n, target in enumerate(bands):
-                copy = pltpu.make_async_remote_copy(
-                    src_ref=all_ref.at[0],
-                    dst_ref=all_ref.at[1 + n],
-                    send_sem=corner_send.at[GROUPS - 1 + n],
-                    recv_sem=corner_recv.at[GROUPS - 1 + n],
-                    device_id=target,
-                    device_id_type=MESH,
-                )
-                copy.start()
-                forward.append(copy)
-    for lane in lanes:
-        lane.arrived()
-    for copy in forward:
-        copy.wait_recv()
-    for copy in shifts + spread_out + forward:
-        copy.wait_send()
-    for lane in lanes:
-        lane.close()
-
-
-def send_faces(routes, faces, corners):
-    vmem = pl.BlockSpec(memory_space=pltpu.VMEM)
-    f32 = jnp.float32
-    dma = pltpu.SemaphoreType.DMA
-    scratch = []
-    for _, perms in FACE_LANES:
-        scratch += lane_scratch(len(perms), (3, EDGE, DEPTH))
-    return pl.pallas_call(
-        faces_kernel,
-        out_shape=(
-            jax.ShapeDtypeStruct((TILES, FACES, 6, EDGE, DEPTH), f32),
-            jax.ShapeDtypeStruct((3, GROUPS, 2, 8, DEPTH), f32),
-        ),
-        in_specs=[pl.BlockSpec(memory_space=pltpu.SMEM), vmem, vmem],
-        out_specs=(vmem, vmem),
-        scratch_shapes=[
-            pltpu.VMEM((2, TILES, 6, EDGE, DEPTH), f32),
-            dma((GROUPS + 1,)),
-            dma((GROUPS + 1,)),
-            dma((2,)),
-            dma((2,)),
-            dma,
-        ]
-        + scratch,
-        compiler_params=pltpu.CompilerParams(
-            collective_id=3, has_side_effects=True, vmem_limit_bytes=24 << 20
-        ),
-        name="faces",
-    )(routes, faces, corners)
+    )(me, routes, packed, ids, others, populations)
 
 
 def collide_rows(pops, charge, field):
@@ -913,102 +820,303 @@
     return result, velocity
 
 
-def collide_kernel(
-    table_ref, routes_ref, pops_ref, charge_ref, mask_ref, pot_ref, out_ref, vel_ref, face_ref, corner_ref, grown
+PITCH = 32
+
+
+def place_potential(grown, pot_ref, slot):
+    def place(i, carry):
+        start = (i + 1) * PITCH
+        grown[pl.ds(start + 8, EDGE)] = pot_ref[slot, 0, i]
+        grown[pl.ds(start + 7, 1)] = pot_ref[slot, 0, EDGE + 2, pl.ds(i, 1)]
+        grown[pl.ds(start + 8 + EDGE, 1)] = pot_ref[slot, 0, EDGE + 3, pl.ds(i, 1)]
+        return carry
+
+    lax.fori_loop(0, EDGE, place, 0, unroll=4)
+    grown[pl.ds(8, EDGE)] = pot_ref[slot, 0, EDGE]
+    grown[pl.ds((EDGE + 1) * PITCH + 8, EDGE)] = pot_ref[slot, 0, EDGE + 1]
+
+
+def field_at(here, x_low, x_high, y_low, y_high):
+    return [
+        0.5 * (x_low - x_high),
+        0.5 * (y_low - y_high),
+        0.5 * (pltpu.roll(here, 1, 1) - pltpu.roll(here, DEPTH - 1, 1)),
+    ]
+
+
+def row_field(grown, i):
+    start = i * PITCH + 8
+    return field_at(
+        *[grown[pl.ds(start + step, EDGE)] for step in (PITCH, 0, 2 * PITCH, PITCH - 1, PITCH + 1)]
+    )
+
+
+def column_field(grown, j):
+    return field_at(
+        *[
+            grown[pl.ds(8 + j + step, EDGE, stride=PITCH)]
+            for step in (PITCH, 0, 2 * PITCH, PITCH - 1, PITCH + 1)
+        ]
+    )
+
+
+def edges_kernel(
+    table_ref, routes_ref, pops_ref, charge_ref, mask_ref, pot_ref, block_ref, face_ref, corner_ref, block_out, grown
 ):
     tile = pl.program_id(0)
-
-    def place(i, carry):
-        grown[i + 1, pl.ds(8, EDGE)] = pot_ref[0, 0, i]
-        grown[i + 1, pl.ds(7, 1)] = pot_ref[0, 0, EDGE + 2, pl.ds(i, 1)]
-        grown[i + 1, pl.ds(8 + EDGE, 1)] = pot_ref[0, 0, EDGE + 3, pl.ds(i, 1)]
-        return carry
-
-    lax.fori_loop(0, EDGE, place, 0)
-    grown[0, pl.ds(8, EDGE)] = pot_ref[0, 0, EDGE]
-    grown[EDGE + 1, pl.ds(8, EDGE)] = pot_ref[0, 0, EDGE + 1]
-    y_low, y_high = crossing(1, -1), crossing(1, 1)
-
-    def rows(i, carry):
-        here = grown[i + 1, pl.ds(8, EDGE)]
-        field = [
-            0.5 * (grown[i, pl.ds(8, EDGE)] - grown[i + 2, pl.ds(8, EDGE)]),
-            0.5 * (grown[i + 1, pl.ds(7, EDGE)] - grown[i + 1, pl.ds(9, EDGE)]),
-            0.5 * (pltpu.roll(here, 1, 1) - pltpu.roll(here, DEPTH - 1, 1)),
-        ]
-        pops = [pops_ref[q, 0, i] for q in range(19)]
-        relaxed, velocity = collide_rows(pops, charge_ref[0, i], field)
-        fluid = mask_ref[0, i + 1, pl.ds(1, EDGE), :] == 1
-        for q in range(19):
-            value = jnp.where(fluid, relaxed[q], pops[q])
-            out_ref[q, 0, i] = value
-            if q in y_low:
-                face_ref[0, 1, y_low.index(q), pl.ds(i, 1)] = value[0:1]
-            if q in y_high:
-                face_ref[0, 0, y_high.index(q), pl.ds(i, 1)] = value[EDGE - 1 :]
-        for d in range(3):
-            vel_ref[d, 0, i] = velocity[d]
-        face_ref[0, 1, 5, pl.ds(i, 1)] = velocity[1][0:1]
-        face_ref[0, 0, 5, pl.ds(i, 1)] = velocity[1][EDGE - 1 :]
-        return carry
-
-    lax.fori_loop(0, EDGE, rows, 0)
-
-    def x_face(face, sign, layer):
-        for k, q in enumerate(crossing(0, sign)):
-            face_ref[0, face, k] = out_ref[q, 0, layer]
-        face_ref[0, face, 5] = vel_ref[0, 0, layer]
-
-    x_face(3, 1, EDGE - 1)
-    x_face(4, -1, 0)
-
-    @pl.when(table_ref[R_ROW, tile] == 0)
-    def _():
-        x_face(2, 1, EDGE - 1)
-
-    @pl.when(table_ref[R_ROW, tile] == 1)
-    def _():
-        x_face(2, -1, 0)
-
-    for n, (q, i, j) in enumerate(
-        ((7, EDGE - 1, EDGE - 1), (9, EDGE - 1, 0), (10, 0, EDGE - 1), (8, 0, 0))
+    block_out[...] = block_ref[...]
+    place_potential(grown, pot_ref, 0)
+
+    def finish(face, axis, sign, pops, charge, flags, field):
+        relaxed, velocity = collide_rows(pops, charge, field)
+        fluid = flags == 1
+
+        def value(q):
+            return jnp.where(fluid, relaxed[q], pops[q])
+
+        for k, q in enumerate(crossing(axis, sign)):
+            face_ref[0, face, k] = value(q)
+        face_ref[0, face, 5] = velocity[axis]
+        return value
+
+    for face, sign, j in ((UP_Y, 1, EDGE - 1), (DOWN_Y, -1, 0)):
+        finish(
+            face,
+            1,
+            sign,
+            [pops_ref[q, 0, pl.ds(j, EDGE, stride=EDGE)] for q in range(19)],
+            charge_ref[0, pl.ds(j, EDGE, stride=EDGE)],
+            mask_ref[0, pl.ds(1, EDGE), 1 + j, :],
+            column_field(grown, j),
+        )
+    for face, sign, i, corners in (
+        (BELOW_X, 1, EDGE - 1, ((0, 7, EDGE - 1), (1, 9, 0))),
+        (ABOVE_X, -1, 0, ((2, 10, EDGE - 1), (3, 8, 0))),
     ):
-        corner_ref[tile // 2, pl.ds(lax.rem(tile, 2) * 4 + n, 1)] = out_ref[q, 0, i, pl.ds(j, 1)]
-
-
-def collide(table, routes, populations, charge, fluid_mask, returned):
+        value = finish(
+            face,
+            0,
+            sign,
+            [pops_ref[q, 0, pl.ds(i * EDGE, EDGE)] for q in range(19)],
+            charge_ref[0, pl.ds(i * EDGE, EDGE)],
+            mask_ref[0, i + 1, pl.ds(1, EDGE), :],
+            row_field(grown, i),
+        )
+        for n, q, j in corners:
+            corner_ref[tile // 2, pl.ds(lax.rem(tile, 2) * 4 + n, 1)] = value(q)[j : j + 1]
+    same = lax.rem(table_ref[R_ROW, tile], 2)
+    for k in range(6):
+        face_ref[0, SAME_X, k] = jnp.where(
+            same == 0, face_ref[0, BELOW_X, k], face_ref[0, ABOVE_X, k]
+        )
+
+
+def edges(table, routes, populations, charge, fluid_mask, returned, potential):
     f32 = jnp.float32
-    pot_spec = pl.BlockSpec(
-        (1, 1, PACK, EDGE, DEPTH), lambda s, tab, rts: (rts[TO_HOLDER * 8 + K_LAST, s], 0, 0, 0, 0)
-    )
     return pl.pallas_call(
-        collide_kernel,
+        edges_kernel,
         out_shape=(
-            jax.ShapeDtypeStruct((19, TILES, EDGE, EDGE, DEPTH), f32),
-            jax.ShapeDtypeStruct((3, TILES, EDGE, EDGE, DEPTH), f32),
             jax.ShapeDtypeStruct((TILES, FACES, 6, EDGE, DEPTH), f32),
             jax.ShapeDtypeStruct((2, 8, DEPTH), f32),
+            jax.ShapeDtypeStruct((BLOCK, BLOCK, DEPTH), f32),
         ),
         grid_spec=pltpu.PrefetchScalarGridSpec(
             num_scalar_prefetch=2,
             grid=(TILES,),
             in_specs=[
-                pl.BlockSpec((19, 1, EDGE, EDGE, DEPTH), lambda s, tab, rts: (0, s, 0, 0, 0)),
-                pl.BlockSpec((1, EDGE, EDGE, DEPTH), lambda s, tab, rts: (s, 0, 0, 0)),
+                pl.BlockSpec((19, 1, EDGE * EDGE, DEPTH), lambda s, tab, rts: (0, s, 0, 0)),
+                pl.BlockSpec((1, EDGE * EDGE, DEPTH), lambda s, tab, rts: (s, 0, 0)),
                 pl.BlockSpec((1, EDGE + 2, EDGE + 2, DEPTH), lambda s, tab, rts: (s, 0, 0, 0)),
-                pot_spec,
+                pl.BlockSpec(
+                    (1, 1, PACK, EDGE, DEPTH),
+                    lambda s, tab, rts: (rts[TO_HOLDER * 8 + K_LAST, s], 0, 0, 0, 0),
+                ),
+                pl.BlockSpec((BLOCK // TILES, BLOCK, DEPTH), lambda s, tab, rts: (s, 0, 0)),
             ],
             out_specs=[
-                pl.BlockSpec((19, 1, EDGE, EDGE, DEPTH), lambda s, tab, rts: (0, s, 0, 0, 0)),
-                pl.BlockSpec((3, 1, EDGE, EDGE, DEPTH), lambda s, tab, rts: (0, s, 0, 0, 0)),
                 pl.BlockSpec((1, FACES, 6, EDGE, DEPTH), lambda s, tab, rts: (s, 0, 0, 0, 0)),
                 pl.BlockSpec((2, 8, DEPTH), lambda s, tab, rts: (0, 0, 0)),
+                pl.BlockSpec((BLOCK // TILES, BLOCK, DEPTH), lambda s, tab, rts: (s, 0, 0)),
             ],
-            scratch_shapes=[pltpu.VMEM((EDGE + 2, 32, DEPTH), f32)],
+            scratch_shapes=[pltpu.VMEM(((EDGE + 2) * PITCH, DEPTH), f32)],
         ),
-        compiler_params=pltpu.CompilerParams(vmem_limit_bytes=32 << 20),
-        name="collide",
-    )(table, routes, populations, charge, fluid_mask, returned)
+        compiler_params=pltpu.CompilerParams(vmem_limit_bytes=16 << 20),
+        name="edges",
+    )(
+        table,
+        routes,
+        populations.reshape(19, TILES, EDGE * EDGE, DEPTH),
+        charge.reshape(TILES, EDGE * EDGE, DEPTH),
+        fluid_mask,
+        returned,
+        potential,
+    )
+
+
+FACE_LANES = (
+    (0, (UP_Y, DOWN_Y, SAME_X)),
+    (1, (UP_Y, DOWN_Y, SAME_X)),
+    (0, (BELOW_X, ABOVE_X)),
+    (1, (BELOW_X, ABOVE_X)),
+)
+
+
+def faces_kernel(
+    table_ref,
+    routes_ref,
+    faces_ref,
+    corners_ref,
+    charge_ref,
+    mask_ref,
+    pot_ref,
+    pops_ref,
+    out_ref,
+    all_ref,
+    cells_ref,
+    vel_ref,
+    shifted,
+    grown,
+    pops_sem,
+    corner_send,
+    corner_recv,
+    shift_send,
+    shift_recv,
+    own_sem,
+    *scratch,
+):
+    me = lax.axis_index("gy")
+    peers = [shifted_id(0, k) for k in range(1, GROUPS)]
+    bands = [shifted_id(1, 0), shifted_id(-1, 0)]
+    fetches = [
+        pltpu.make_async_copy(pops_ref.at[:, t], cells_ref.at[:, t], pops_sem.at[t])
+        for t in range(TILES)
+    ]
+    for copy in fetches:
+        copy.start()
+
+    def collide(t, begin):
+        def rows(i, carry):
+            pops = [cells_ref[q, t, i] for q in range(19)]
+            relaxed, velocity = collide_rows(pops, charge_ref[t, i], row_field(grown, i))
+            fluid = mask_ref[t, i + 1, pl.ds(1, EDGE), :] == 1
+            for q in range(19):
+                cells_ref[q, t, i] = jnp.where(fluid, relaxed[q], pops[q])
+            for d in range(3):
+                vel_ref[d, t, i] = velocity[d]
+            return carry
+
+        lax.fori_loop(begin, begin + EDGE // len(FACE_LANES), rows, 0)
+
+    greet(peers + bands)
+    shifts = []
+    for n, target in enumerate(bands):
+        copy = pltpu.make_async_remote_copy(
+            src_ref=faces_ref.at[:, 3 + n],
+            dst_ref=shifted.at[n],
+            send_sem=shift_send.at[n],
+            recv_sem=shift_recv.at[n],
+            device_id=target,
+            device_id_type=MESH,
+        )
+        copy.start()
+        shifts.append(copy)
+    lanes = []
+    for n, (order, perms) in enumerate(FACE_LANES):
+        rows = slice(order * 3, order * 3 + 3)
+
+        def first(k, slot, perms=perms, rows=rows):
+            if perms[k] < BELOW_X:
+                return faces_ref[slot, perms[k], rows]
+            return shifted[perms[k] - BELOW_X, slot, rows]
+
+        def final(here, perms=perms, order=order):
+            return out_ref.at[here, pl.ds(perms[0], len(perms)), pl.ds(order * 3, 3)]
+
+        lanes.append(Lane(order, perms, table_ref, first, scratch[16 * n : 16 * n + 16], final))
+    spread_out, forward = [], []
+    own = pltpu.make_async_copy(corners_ref, all_ref.at[0, me], own_sem)
+    for stage in range(4):
+        for n, lane in enumerate(lanes):
+            if stage == 0 and n == 2:
+                for k, target in enumerate(peers):
+                    copy = pltpu.make_async_remote_copy(
+                        src_ref=corners_ref,
+                        dst_ref=all_ref.at[0, me],
+                        send_sem=corner_send.at[k],
+                        recv_sem=corner_recv.at[k],
+                        device_id=target,
+                        device_id_type=MESH,
+                    )
+                    copy.start()
+                    spread_out.append(copy)
+                own.start()
+                for copy in shifts:
+                    copy.wait_recv()
+            lane.advance(stage)
+            if n == 0:
+                fetches[stage].wait()
+                place_potential(grown, pot_ref, routes_ref[TO_HOLDER * 8 + K_LAST, stage])
+            collide(stage, n * (EDGE // len(FACE_LANES)))
+        if stage == 1:
+            own.wait()
+            for copy in spread_out:
+                copy.wait_recv()
+            for n, target in enumerate(bands):
+                copy = pltpu.make_async_remote_copy(
+                    src_ref=all_ref.at[0],
+                    dst_ref=all_ref.at[1 + n],
+                    send_sem=corner_send.at[GROUPS - 1 + n],
+                    recv_sem=corner_recv.at[GROUPS - 1 + n],
+                    device_id=target,
+                    device_id_type=MESH,
+                )
+                copy.start()
+                forward.append(copy)
+    for lane in lanes:
+        lane.arrived()
+    for copy in forward:
+        copy.wait_recv()
+    for copy in shifts + spread_out + forward:
+        copy.wait_send()
+    for lane in lanes:
+        lane.close()
+
+
+def collide_and_send(table, routes, faces, corners, charge, fluid_mask, returned, populations):
+    vmem = pl.BlockSpec(memory_space=pltpu.VMEM)
+    smem = pl.BlockSpec(memory_space=pltpu.SMEM)
+    anywhere = pl.BlockSpec(memory_space=pltpu.HBM)
+    f32 = jnp.float32
+    dma = pltpu.SemaphoreType.DMA
+    scratch = []
+    for _, perms in FACE_LANES:
+        scratch += lane_scratch(len(perms), (3, EDGE, DEPTH))
+    return pl.pallas_call(
+        faces_kernel,
+        out_shape=(
+            jax.ShapeDtypeStruct((TILES, FACES, 6, EDGE, DEPTH), f32),
+            jax.ShapeDtypeStruct((3, GROUPS, 2, 8, DEPTH), f32),
+            jax.ShapeDtypeStruct((19, TILES, EDGE, EDGE, DEPTH), f32),
+            jax.ShapeDtypeStruct((3, TILES, EDGE, EDGE, DEPTH), f32),
+        ),
+        in_specs=[smem, smem] + [vmem] * 5 + [pl.BlockSpec(memory_space=pl.ANY)],
+        out_specs=(vmem,) * 4,
+        scratch_shapes=[
+            pltpu.VMEM((2, TILES, 6, EDGE, DEPTH), f32),
+            pltpu.VMEM(((EDGE + 2) * PITCH, DEPTH), f32),
+            dma((TILES,)),
+            dma((GROUPS + 1,)),
+            dma((GROUPS + 1,)),
+            dma((2,)),
+            dma((2,)),
+            dma,
+        ]
+        + scratch,
+        compiler_params=pltpu.CompilerParams(
+            collective_id=3, has_side_effects=True, vmem_limit_bytes=20 << 20
+        ),
+        name="faces",
+    )(table, routes, faces, corners, charge, fluid_mask, returned, populations)
 
 
 CHARGE, SPEED = 19, 20
@@ -1195,7 +1303,7 @@
                 pltpu.SemaphoreType.DMA((2, 3)),
             ],
         ),
-        compiler_params=pltpu.CompilerParams(vmem_limit_bytes=32 << 20),
+        compiler_params=pltpu.CompilerParams(vmem_limit_bytes=24 << 20),
         name="stream",
     )(
         table,
@@ -1216,14 +1324,16 @@
     ids_row = jnp.where(place // TILES == me, jnp.tile(tile_ids, 2 * DEPTH).reshape(8, DEPTH), 0)
     ids = exchange_start(ids_row)
     routes = make_routes(owner_routes_kernel, 16, me, ids)
-    potential, packed, others, charge_rims = find_potential(
+    potential, packed, others, charge_rims, charge, fluid_mask = find_potential(
         permittivity, routes, charge, fluid_mask, ids, phase_label
     )
-    returned, table = send_back(me, routes, packed, ids, others)
-    relaxed, velocity, faces, corners = collide(
-        table, routes, populations, charge, fluid_mask, returned
+    returned, table, populations = send_back(me, routes, packed, ids, others, populations)
+    faces, corners, potential = edges(
+        table, routes, populations, charge, fluid_mask, returned, potential
     )
-    rims, all_corners = send_faces(table, faces, corners)
+    rims, all_corners, relaxed, velocity = collide_and_send(
+        table, routes, faces, corners, charge, fluid_mask, returned, populations
+    )
     populations_next, charge_next = stream(
         table, routes, relaxed, velocity, charge, fluid_mask, charge_rims, rims, all_corners
     )

time: 148 us -> 141 us (0.953)
  Pallas kernels: 140 us -> 134 us
  local copies, waits for them, and re-layouts: 6.5 us -> 4.66 us
    pallas_call x2, Pallas kernels: 42.1 us -> 35.6 us  [the longest x1 31.8 us: collide_and_send(): pl.pallas_call(faces_kernel, out_shape=(jax.ShapeDtypeStruct((TILES, FACE...]
    unnamed x10 -> x7, local copies, waits for them, and re-layouts: 5.74 us -> 3.9 us
where the time goes in v5:
time: 141 us; the launch traced here: 139 us
  Pallas kernels  134 us (95%)
  local copies, waits for them, and re-layouts  4.66 us (3%)
    pallas_call x1, Pallas kernels, find_potential(): pl.pallas_call(source_kernel, out_shape=(jax.ShapeDtypeStruct((BLOCK, BLO...  49.6 us
    pallas_call x1, Pallas kernels, collide_and_send(): pl.pallas_call(faces_kernel, out_shape=(jax.ShapeDtypeStruct((TILES, FACE...  31.8 us
    pallas_call x1, Pallas kernels, send_back(): pl.pallas_call(back_kernel, out_shape=(jax.ShapeDtypeStruct((TILES, 1, PA...  24.5 us
    pallas_call x1, Pallas kernels, stream(): pl.pallas_call(stream_kernel, out_shape=(jax.ShapeDtypeStruct((19, TILES,...  10.1 us
    pallas_call x1, Pallas kernels, exchange_start(): pl.pallas_call(start_kernel, out_shape=jax.ShapeDtypeStruct((GROUPS, 8, D...  9.88 us
    pallas_call x1, Pallas kernels, make_routes(): pl.pallas_call(kernel, out_shape=jax.ShapeDtypeStruct((rows, DEPTH), jnp....  4.49 us
    unnamed x7, local copies, waits for them, and re-layouts  3.9 us
    pallas_call x1, Pallas kernels, edges(): pl.pallas_call(edges_kernel, out_shape=(jax.ShapeDtypeStruct((TILES, FACE...  3.76 us

profile of v5, /device:TPU:0, one launch (start us, length us, event | category | flops | bytes accessed | tf_op | source)
XLA Modules:
  0.0 139.5 jit_solution(7465804065275476158)
XLA Ops:
  0.6 0.7 tile.10
  1.3 0.1 tile.11
  1.4 9.9 %start.1.ids_ref = s32[16,8,128]{2,1,0:T(8,128)S(1)} custom-call(s32[8,128]{1,0:T(8,128)S(1)} %fusion.3.ids_ref), custom_call_target="tpu_custom_call" | custom-call | tf_op jit(solution)/shard_map/start/pallas_call | solution.py:131
  11.3 4.5 %owner_routes_kernel.1.table_ref.routes_ref = s32[16,128]{1,0:T(8,128)S(1)} custom-call(s32[1]{0:T(128)} %bitcast.me_ref, s32[16,8,128]{2,1,0:T(8,128)S(1)} %start.1.ids_ref), custom_call_target="tpu_custom_call" | custom-call | tf_op jit(solution)/shard_map/owner_routes_kernel/pallas_call | solution.py:423
  15.8 1.2 copy.10.mask_hbm
  17.0 0.0 copy-start
  17.0 1.0 copy-done
  18.0 0.0 copy-start.1
  18.0 1.0 copy-done.1
  19.1 0.0 copy-start.2
  19.1 0.7 copy-done.2
  19.7 49.6 %source.1 = (f32[32,32,128]{2,1,0:T(8,128)S(1)}, f32[4,20,16,128]{3,2,1,0:T(8,128)S(1)}, s32[2,16,8,128]{3,2,1,0:T(8,128)S(1)}, f32[4,1,4,16,128]{4,3,2,1,0:T(8,...) custom-call(f32[4]{0:T(128)S(1)} %copy-done.2, ...), custom_call_target="tpu_custom_call" | custom-call | tf_op jit(solution)/shard_map/source/pallas_call | solution.py:653
  69.3 24.5 %back.1 = (f32[4,1,20,16,128]{4,3,2,1,0:T(8,128)S(1)}, s32[48,128]{1,0:T(8,128)S(1)}, f32[19,4,16,16,128]{4,3,2,1,0:T(8,128)S(1)}) custom-call(s32[1]{0:T(128)} %bitcast.me_ref, s32[16,128]{1,0:T(8,128)S(1)} %owner_routes_kernel.1.table_ref.routes_ref, f32[4,20,16,128]{3,2,1,0:T(8,128)S(1)} %get-tuple-element.21.items_ref, s32[16,8,128]{2,1,0:T(8,128)S(1)} %start.1.ids_ref, ...), custom_call_target="tpu_custom_call" | custom-call | tf_op jit(solution)/shard_map/back/pallas_call | solution.py:756
  93.8 3.8 %edges.1 = (f32[4,5,6,16,128]{4,3,2,1,0:T(8,128)S(1)}, f32[2,8,128]{2,1,0:T(8,128)S(1)}, f32[32,32,128]{2,1,0:T(8,128)}) custom-call(s32[48,128]{1,0:T(8,128)S(1)} %get-tuple-element.23.table_ref, s32[16,128]{1,0:T(8,128)S(1)} %owner_routes_kernel.1.table_ref.routes_ref, f32[19,4,256,128]{3,2,1,0:T(8,128)S(1)} %bitcast.6, f32[4,256,128]{2,1,0:T(8,128)S(1)} %bitcast.8, ...), custom_call_target="tpu_custom_call" | custom-call | tf_op jit(solution)/shard_map/edges/pallas_call | solution.py:916
  97.6 31.8 %faces.1 = (f32[4,5,6,16,128]{4,3,2,1,0:T(8,128)S(1)}, f32[3,16,2,8,128]{4,3,2,1,0:T(8,128)S(1)}, f32[19,4,16,16,128]{4,3,2,1,0:T(8,128)S(1)}, f32[3,4,16,16,128]{4,3,2,1,0:T(8,128)S(1)}) custom-call(s32[48,128]{1,0:T(8,128)S(1)} %get-tuple-element.23.table_ref, s32[16,128]{1,0:T(8,128)S(1)} %owner_routes_kernel.1.table_ref.routes_ref, ...), custom_call_target="tpu_custom_call" | custom-call | tf_op jit(solution)/shard_map/faces/pallas_call | solution.py:1094
  129.4 10.1 %stream.1 = (f32[19,4,16,16,128]{4,3,2,1,0:T(8,128)}, f32[4,16,16,128]{3,2,1,0:T(8,128)}) custom-call(s32[48,128]{1,0:T(8,128)S(1)} %get-tuple-element.23.table_ref, s32[16,128]{1,0:T(8,128)S(1)} %owner_routes_kernel.1.table_ref.routes_ref, f32[19,4,256,128]{3,2,1,0:T(8,128)S(1)} %bitcast.7, f32[3,4,256,128]{3,2,1,0:T(8,128)S(1)} %bitcast.10, ...), custom_call_target="tpu_custom_call" | custom-call | tf_op jit(solution)/shard_map/stream/pallas_call | solution.py:1275
  (1 shorter events, 0.0 us)
Async XLA Ops:
  17.0 1.0 copy-start
  18.0 1.0 copy-start.1
  19.1 0.7 copy-start.2

commit v6 on v5

--- a/solution.py
+++ b/solution.py
@@ -77,11 +77,11 @@
     return pl.ds(0, width), pl.ds(pad + BLOCK, width)
 
 
-def halo_copies(block_ref, ext_ref, width, send_sem, recv_sem):
+def halo_copies(block_ref, ext_ref, width, side, send_sem, recv_sem):
     copies = []
     for n, (dx, dy) in enumerate(AROUND):
         src_i, dst_i = span(dx, width, width)
-        src_j, dst_j = span(dy, SIDE, SIDE)
+        src_j, dst_j = span(dy, side, SIDE)
         copies.append(
             pltpu.make_async_remote_copy(
                 src_ref=block_ref.at[src_i, src_j],
@@ -569,7 +569,7 @@
             Lane(n % 2, (TO_OWNER,), table_ref, first, scratch[16 * n : 16 * n + 16])
         )
     passed = []
-    phases = halo_copies(phase_ref, phase_ext, 5, phase_send, phase_recv)
+    phases = halo_copies(phase_ref, phase_ext, 5, SIDE, phase_send, phase_recv)
 
     def weights(begin, end):
         weigh_rows(begin, end, permit, coef_ref, scale_ref)
@@ -609,7 +609,7 @@
                 table_ref[TO_OWNER * 8 + K_LAST, t], 0
             ]
     block = ext_ref.at[pl.ds(4, BLOCK), pl.ds(SIDE, BLOCK)]
-    copies = halo_copies(block, ext_ref, 4, send_sem, recv_sem)
+    copies = halo_copies(block, ext_ref, 4, 4, send_sem, recv_sem)
     for copy in copies:
         copy.start()
     weights(30, TALL)

time: 141 us -> 139 us (0.986)
  no operation moved by 1% of the time
where the time goes in v6:
time: 139 us; the launch traced here: 138 us
  Pallas kernels  133 us (96%)
  local copies, waits for them, and re-layouts  4.66 us (3%)
    pallas_call x1, Pallas kernels, find_potential(): pl.pallas_call(source_kernel, out_shape=(jax.ShapeDtypeStruct((BLOCK, BLO...  48.8 us
    pallas_call x1, Pallas kernels, collide_and_send(): pl.pallas_call(faces_kernel, out_shape=(jax.ShapeDtypeStruct((TILES, FACE...  31.7 us
    pallas_call x1, Pallas kernels, send_back(): pl.pallas_call(back_kernel, out_shape=(jax.ShapeDtypeStruct((TILES, 1, PA...  24.4 us
    pallas_call x1, Pallas kernels, stream(): pl.pallas_call(stream_kernel, out_shape=(jax.ShapeDtypeStruct((19, TILES,...  10.1 us
    pallas_call x1, Pallas kernels, exchange_start(): pl.pallas_call(start_kernel, out_shape=jax.ShapeDtypeStruct((GROUPS, 8, D...  9.88 us
    pallas_call x1, Pallas kernels, make_routes(): pl.pallas_call(kernel, out_shape=jax.ShapeDtypeStruct((rows, DEPTH), jnp....  4.49 us
    unnamed x7, local copies, waits for them, and re-layouts  3.9 us
    pallas_call x1, Pallas kernels, edges(): pl.pallas_call(edges_kernel, out_shape=(jax.ShapeDtypeStruct((TILES, FACE...  3.76 us

profile of v6, /device:TPU:0, one launch (start us, length us, event | category | flops | bytes accessed | tf_op | source)
XLA Modules:
  0.0 138.4 jit_solution(18133213132107903679)
XLA Ops:
  0.6 0.7 tile.10
  1.3 0.1 tile.11
  1.4 9.9 %start.1.ids_ref = s32[16,8,128]{2,1,0:T(8,128)S(1)} custom-call(s32[8,128]{1,0:T(8,128)S(1)} %fusion.3.ids_ref), custom_call_target="tpu_custom_call" | custom-call | tf_op jit(solution)/shard_map/start/pallas_call | solution.py:131
  11.3 4.5 %owner_routes_kernel.1.table_ref.routes_ref = s32[16,128]{1,0:T(8,128)S(1)} custom-call(s32[1]{0:T(128)} %bitcast.me_ref, s32[16,8,128]{2,1,0:T(8,128)S(1)} %start.1.ids_ref), custom_call_target="tpu_custom_call" | custom-call | tf_op jit(solution)/shard_map/owner_routes_kernel/pallas_call | solution.py:423
  15.8 1.2 copy.10.mask_hbm
  17.0 0.0 copy-start
  17.0 1.0 copy-done
  18.0 0.0 copy-start.1
  18.0 1.0 copy-done.1
  19.1 0.0 copy-start.2
  19.1 0.7 copy-done.2
  19.7 48.8 %source.1 = (f32[32,32,128]{2,1,0:T(8,128)S(1)}, f32[4,20,16,128]{3,2,1,0:T(8,128)S(1)}, s32[2,16,8,128]{3,2,1,0:T(8,128)S(1)}, f32[4,1,4,16,128]{4,3,2,1,0:T(8,...) custom-call(f32[4]{0:T(128)S(1)} %copy-done.2, ...), custom_call_target="tpu_custom_call" | custom-call | tf_op jit(solution)/shard_map/source/pallas_call | solution.py:653
  68.5 24.4 %back.1 = (f32[4,1,20,16,128]{4,3,2,1,0:T(8,128)S(1)}, s32[48,128]{1,0:T(8,128)S(1)}, f32[19,4,16,16,128]{4,3,2,1,0:T(8,128)S(1)}) custom-call(s32[1]{0:T(128)} %bitcast.me_ref, s32[16,128]{1,0:T(8,128)S(1)} %owner_routes_kernel.1.table_ref.routes_ref, f32[4,20,16,128]{3,2,1,0:T(8,128)S(1)} %get-tuple-element.21.items_ref, s32[16,8,128]{2,1,0:T(8,128)S(1)} %start.1.ids_ref, ...), custom_call_target="tpu_custom_call" | custom-call | tf_op jit(solution)/shard_map/back/pallas_call | solution.py:756
  92.9 3.8 %edges.1 = (f32[4,5,6,16,128]{4,3,2,1,0:T(8,128)S(1)}, f32[2,8,128]{2,1,0:T(8,128)S(1)}, f32[32,32,128]{2,1,0:T(8,128)}) custom-call(s32[48,128]{1,0:T(8,128)S(1)} %get-tuple-element.23.table_ref, s32[16,128]{1,0:T(8,128)S(1)} %owner_routes_kernel.1.table_ref.routes_ref, f32[19,4,256,128]{3,2,1,0:T(8,128)S(1)} %bitcast.6, f32[4,256,128]{2,1,0:T(8,128)S(1)} %bitcast.8, ...), custom_call_target="tpu_custom_call" | custom-call | tf_op jit(solution)/shard_map/edges/pallas_call | solution.py:916
  96.7 31.7 %faces.1 = (f32[4,5,6,16,128]{4,3,2,1,0:T(8,128)S(1)}, f32[3,16,2,8,128]{4,3,2,1,0:T(8,128)S(1)}, f32[19,4,16,16,128]{4,3,2,1,0:T(8,128)S(1)}, f32[3,4,16,16,128]{4,3,2,1,0:T(8,128)S(1)}) custom-call(s32[48,128]{1,0:T(8,128)S(1)} %get-tuple-element.23.table_ref, s32[16,128]{1,0:T(8,128)S(1)} %owner_routes_kernel.1.table_ref.routes_ref, ...), custom_call_target="tpu_custom_call" | custom-call | tf_op jit(solution)/shard_map/faces/pallas_call | solution.py:1094
  128.3 10.1 %stream.1 = (f32[19,4,16,16,128]{4,3,2,1,0:T(8,128)}, f32[4,16,16,128]{3,2,1,0:T(8,128)}) custom-call(s32[48,128]{1,0:T(8,128)S(1)} %get-tuple-element.23.table_ref, s32[16,128]{1,0:T(8,128)S(1)} %owner_routes_kernel.1.table_ref.routes_ref, f32[19,4,256,128]{3,2,1,0:T(8,128)S(1)} %bitcast.7, f32[3,4,256,128]{3,2,1,0:T(8,128)S(1)} %bitcast.10, ...), custom_call_target="tpu_custom_call" | custom-call | tf_op jit(solution)/shard_map/stream/pallas_call | solution.py:1275
  (1 shorter events, 0.0 us)
Async XLA Ops:
  17.0 1.0 copy-start
  18.0 1.0 copy-start.1
  19.1 0.7 copy-start.2

commit v7 on v6

--- a/solution.py
+++ b/solution.py
@@ -569,7 +569,7 @@
             Lane(n % 2, (TO_OWNER,), table_ref, first, scratch[16 * n : 16 * n + 16])
         )
     passed = []
-    phases = halo_copies(phase_ref, phase_ext, 5, SIDE, phase_send, phase_recv)
+    phases = halo_copies(phase_ref, phase_ext, 5, 5, phase_send, phase_recv)
 
     def weights(begin, end):
         weigh_rows(begin, end, permit, coef_ref, scale_ref)

time: 139 us -> 137 us (0.986)
  Pallas kernels: 133 us -> 131 us
    pallas_call x1, Pallas kernels: 48.8 us -> 47.1 us  [find_potential(): pl.pallas_call(source_kernel, out_shape=(jax.ShapeDtypeStruct((BLOCK, BLO...]
where the time goes in v7:
time: 137 us
  Pallas kernels  131 us (96%)
  local copies, waits for them, and re-layouts  4.66 us (3%)
    pallas_call x1, Pallas kernels, find_potential(): pl.pallas_call(source_kernel, out_shape=(jax.ShapeDtypeStruct((BLOCK, BLO...  47.1 us
    pallas_call x1, Pallas kernels, collide_and_send(): pl.pallas_call(faces_kernel, out_shape=(jax.ShapeDtypeStruct((TILES, FACE...  31.5 us
    pallas_call x1, Pallas kernels, send_back(): pl.pallas_call(back_kernel, out_shape=(jax.ShapeDtypeStruct((TILES, 1, PA...  24.6 us
    pallas_call x1, Pallas kernels, stream(): pl.pallas_call(stream_kernel, out_shape=(jax.ShapeDtypeStruct((19, TILES,...  10.1 us
    pallas_call x1, Pallas kernels, exchange_start(): pl.pallas_call(start_kernel, out_shape=jax.ShapeDtypeStruct((GROUPS, 8, D...  9.88 us
    pallas_call x1, Pallas kernels, make_routes(): pl.pallas_call(kernel, out_shape=jax.ShapeDtypeStruct((rows, DEPTH), jnp....  4.49 us
    unnamed x7, local copies, waits for them, and re-layouts  3.9 us
    pallas_call x1, Pallas kernels, edges(): pl.pallas_call(edges_kernel, out_shape=(jax.ShapeDtypeStruct((TILES, FACE...  3.76 us

profile of v7, /device:TPU:0, one launch (start us, length us, event | category | flops | bytes accessed | tf_op | source)
XLA Modules:
  0.0 136.8 jit_solution(2671672522550595477)
XLA Ops:
  0.6 0.7 tile.10
  1.3 0.1 tile.11
  1.4 9.9 %start.1.ids_ref = s32[16,8,128]{2,1,0:T(8,128)S(1)} custom-call(s32[8,128]{1,0:T(8,128)S(1)} %fusion.3.ids_ref), custom_call_target="tpu_custom_call" | custom-call | tf_op jit(solution)/shard_map/start/pallas_call | solution.py:131
  11.3 4.5 %owner_routes_kernel.1.table_ref.routes_ref = s32[16,128]{1,0:T(8,128)S(1)} custom-call(s32[1]{0:T(128)} %bitcast.me_ref, s32[16,8,128]{2,1,0:T(8,128)S(1)} %start.1.ids_ref), custom_call_target="tpu_custom_call" | custom-call | tf_op jit(solution)/shard_map/owner_routes_kernel/pallas_call | solution.py:423
  15.8 1.2 copy.10.mask_hbm
  17.0 0.0 copy-start
  17.0 1.0 copy-done
  18.0 0.0 copy-start.1
  18.0 1.0 copy-done.1
  19.1 0.0 copy-start.2
  19.1 0.7 copy-done.2
  19.7 47.1 %source.1 = (f32[32,32,128]{2,1,0:T(8,128)S(1)}, f32[4,20,16,128]{3,2,1,0:T(8,128)S(1)}, s32[2,16,8,128]{3,2,1,0:T(8,128)S(1)}, f32[4,1,4,16,128]{4,3,2,1,0:T(8,...) custom-call(f32[4]{0:T(128)S(1)} %copy-done.2, ...), custom_call_target="tpu_custom_call" | custom-call | tf_op jit(solution)/shard_map/source/pallas_call | solution.py:653
  66.8 24.6 %back.1 = (f32[4,1,20,16,128]{4,3,2,1,0:T(8,128)S(1)}, s32[48,128]{1,0:T(8,128)S(1)}, f32[19,4,16,16,128]{4,3,2,1,0:T(8,128)S(1)}) custom-call(s32[1]{0:T(128)} %bitcast.me_ref, s32[16,128]{1,0:T(8,128)S(1)} %owner_routes_kernel.1.table_ref.routes_ref, f32[4,20,16,128]{3,2,1,0:T(8,128)S(1)} %get-tuple-element.21.items_ref, s32[16,8,128]{2,1,0:T(8,128)S(1)} %start.1.ids_ref, ...), custom_call_target="tpu_custom_call" | custom-call | tf_op jit(solution)/shard_map/back/pallas_call | solution.py:756
  91.4 3.8 %edges.1 = (f32[4,5,6,16,128]{4,3,2,1,0:T(8,128)S(1)}, f32[2,8,128]{2,1,0:T(8,128)S(1)}, f32[32,32,128]{2,1,0:T(8,128)}) custom-call(s32[48,128]{1,0:T(8,128)S(1)} %get-tuple-element.23.table_ref, s32[16,128]{1,0:T(8,128)S(1)} %owner_routes_kernel.1.table_ref.routes_ref, f32[19,4,256,128]{3,2,1,0:T(8,128)S(1)} %bitcast.6, f32[4,256,128]{2,1,0:T(8,128)S(1)} %bitcast.8, ...), custom_call_target="tpu_custom_call" | custom-call | tf_op jit(solution)/shard_map/edges/pallas_call | solution.py:916
  95.2 31.5 %faces.1 = (f32[4,5,6,16,128]{4,3,2,1,0:T(8,128)S(1)}, f32[3,16,2,8,128]{4,3,2,1,0:T(8,128)S(1)}, f32[19,4,16,16,128]{4,3,2,1,0:T(8,128)S(1)}, f32[3,4,16,16,128]{4,3,2,1,0:T(8,128)S(1)}) custom-call(s32[48,128]{1,0:T(8,128)S(1)} %get-tuple-element.23.table_ref, s32[16,128]{1,0:T(8,128)S(1)} %owner_routes_kernel.1.table_ref.routes_ref, ...), custom_call_target="tpu_custom_call" | custom-call | tf_op jit(solution)/shard_map/faces/pallas_call | solution.py:1094
  126.7 10.1 %stream.1 = (f32[19,4,16,16,128]{4,3,2,1,0:T(8,128)}, f32[4,16,16,128]{3,2,1,0:T(8,128)}) custom-call(s32[48,128]{1,0:T(8,128)S(1)} %get-tuple-element.23.table_ref, s32[16,128]{1,0:T(8,128)S(1)} %owner_routes_kernel.1.table_ref.routes_ref, f32[19,4,256,128]{3,2,1,0:T(8,128)S(1)} %bitcast.7, f32[3,4,256,128]{3,2,1,0:T(8,128)S(1)} %bitcast.10, ...), custom_call_target="tpu_custom_call" | custom-call | tf_op jit(solution)/shard_map/stream/pallas_call | solution.py:1275
  (1 shorter events, 0.0 us)
Async XLA Ops:
  17.0 1.0 copy-start
  18.0 1.0 copy-start.1
  19.1 0.7 copy-start.2
